TPU v7x, 32 devices: a whole 2x2x4 slice. The times are simulated.
32 devices in a mesh: dp: 4 (over z), ctx: 8 (over y, x, core).
Axes of the slice: x: 2, y: 2, z: 4, core: 2. Of those that a mesh axis runs over, the one named last changes fastest.
Arguments:
- inputs: bfloat16 [4, 1024, 4096], P('dp', 'ctx'), may hold values from -6 to 6
- queries: bfloat16 [4, 1024, 4096], P('dp', 'ctx'), may hold values from -384 to 384
- keys_values: bfloat16 [4, 1024, 2, 512], P('dp', 'ctx'), may hold values from -6 to 6
- out_grad: bfloat16 [4, 1024, 4096], P('dp', 'ctx'), may hold values from -6 to 6
- tree_mask: int32 [4, 8, 8], P('dp', 'ctx'), may hold values from 0 to 1, as said below
Outputs:
- attn_out: bfloat16 [4, 1024, 4096], P('dp', 'ctx')
- query_grad: bfloat16 [4, 1024, 4096], P('dp', 'ctx')
- key_weight_grad: float32 [4096, 512], P(('dp', 'ctx'))
- value_weight_grad: float32 [4096, 512], P(('dp', 'ctx'))
Inputs may be any that keep to these rules, and one draw needn't show every extreme that they name: tree_mask[s,a,b] is 1 exactly where block b is block a or an ancestor of block a in the same tree of sequence s; a tree's blocks are consecutive, its first block is its root, every ancestor comes before its descendants, and blocks 0 and 1 belong to one tree.
All inputs are finite; a program needn't handle non-finite values.
Results may differ from a plain program's by a relative error of at most 0.029.
Values may be sent and summed in bfloat16 or wider, within the bound.
No kernel may reach another device: no remote copies, remote signals or barrier semaphores. Data moves between devices by JAX's collectives and lax.ppermute only.
A program may use at most 128 MiB of HBM per device.

v0:
```python
import math

import jax
import jax.numpy as jnp
from jax import lax
from jax.sharding import PartitionSpec as P

HEADS = 32
KV_HEADS = 4
HEAD_DIM = 128


def from_behind(block, axis, distance):
    devices = range(lax.axis_size(axis))
    route = [(i - distance, i) for i in devices if i - distance in devices]
    return lax.ppermute(block, axis, route)


def from_behind_2(value, axis, steps):
    count = lax.axis_size(axis)
    pairs = [(source, (source + steps) % count) for source in range(count)]
    return lax.ppermute(value, axis, pairs)


def body(inputs, queries, keys_values, out_grad, tree_mask):
    tokens = queries.shape[1]
    kv_width = keys_values.shape[3]
    groups = KV_HEADS
    head_dim = HEAD_DIM
    ratio = HEADS // KV_HEADS
    blocks_here = tree_mask.shape[1]
    block_len = tokens // blocks_here
    cycle_size = lax.axis_size("ctx")
    data_size = lax.axis_size("dp")
    cycle_index = lax.axis_index("ctx")
    score_scale = 1.0 / math.sqrt(head_dim)
    query_heads = queries[0].reshape(tokens, groups, ratio, head_dim)
    grad_heads = out_grad[0].reshape(tokens, groups, ratio, head_dim)
    block_rows = tree_mask[0]
    local_kv = keys_values[0]
    offsets = jnp.arange(tokens)

    def tile_blocks(source):
        return lax.dynamic_slice_in_dim(block_rows, source * blocks_here, blocks_here, 1)

    def tile_allowed(source):
        block_cols = tile_blocks(source)
        expanded = jnp.repeat(jnp.repeat(block_cols, block_len, axis=0), block_len, axis=1) == 1
        query_pos = cycle_index * tokens + offsets[:, None]
        key_pos = source * tokens + offsets[None, :]
        other_block = query_pos // block_len != key_pos // block_len
        return expanded & (other_block | (key_pos <= query_pos))

    def forward_tile(state_in, kv_tile, source, group_count):
        running_max, running_sum, weighted = state_in
        key_part = kv_tile[:, 0].reshape(tokens, group_count, head_dim)
        value_part = kv_tile[:, 1].reshape(tokens, group_count, head_dim)
        allowed = tile_allowed(source)[:, None, None, :]
        scores = (
            jnp.einsum("tgrd,sgd->tgrs", query_heads, key_part, preferred_element_type=jnp.float32)
            * score_scale
        )
        tile_max = jnp.max(jnp.where(allowed, scores, -jnp.inf), axis=3)
        new_max = jnp.maximum(running_max, tile_max)
        factor = jnp.exp(running_max - new_max)
        weights = jnp.where(allowed, jnp.exp(scores - new_max[..., None]), 0.0)
        running_sum = running_sum * factor + jnp.sum(weights, axis=3)
        weighted = weighted * factor[..., None] + jnp.einsum(
            "tgrs,sgd->tgrd",
            weights.astype(jnp.bfloat16),
            value_part,
            preferred_element_type=jnp.float32,
        )
        return (new_max, running_sum, weighted)

    def forward_step(state_in, kv_tile, source, group_count):
        return forward_tile(state_in, kv_tile, source, group_count)

    stats_one = forward_step(
        (
            jnp.full((tokens, groups, ratio), -jnp.inf, jnp.float32),
            jnp.zeros((tokens, groups, ratio), jnp.float32),
            jnp.zeros((tokens, groups, ratio, head_dim), jnp.float32),
        ),
        local_kv,
        cycle_index,
        groups,
    )

    def forward_turn(cycle_step, carried):
        stats_in, moving = carried
        moving = from_behind(moving, "ctx", 1)
        return (
            forward_step(stats_in, moving, (cycle_index - cycle_step) % cycle_size, groups),
            moving,
        )

    stats_one, moving = lax.fori_loop(1, cycle_size, forward_turn, (stats_one, local_kv))
    stat_pieces = [stats_one]
    log_total = jnp.concatenate([piece[0] + jnp.log(piece[1]) for piece in stat_pieces], axis=1)
    attn_heads = jnp.concatenate([piece[2] / piece[1][..., None] for piece in stat_pieces], axis=1)
    attn_heads = attn_heads.astype(jnp.bfloat16)
    delta = jnp.sum(grad_heads.astype(jnp.float32) * attn_heads.astype(jnp.float32), axis=3)
    attn_out = attn_heads.reshape(1, tokens, HEADS * head_dim)

    def backward_tile(query_acc, kv_tile, source, group_count):
        key_part = kv_tile[:, 0].reshape(tokens, group_count, head_dim)
        value_part = kv_tile[:, 1].reshape(tokens, group_count, head_dim)
        allowed = tile_allowed(source)[:, None, None, :]
        scores = (
            jnp.einsum("tgrd,sgd->tgrs", query_heads, key_part, preferred_element_type=jnp.float32)
            * score_scale
        )
        probs_low = jnp.where(allowed, jnp.exp(scores - log_total[..., None]), 0.0).astype(
            jnp.bfloat16
        )
        prob_grad = jnp.einsum(
            "tgrd,sgd->tgrs", grad_heads, value_part, preferred_element_type=jnp.float32
        )
        score_grad = (probs_low.astype(jnp.float32) * (prob_grad - delta[..., None])).astype(
            jnp.bfloat16
        )
        query_acc = (
            query_acc
            + jnp.einsum("tgrs,sgd->tgrd", score_grad, key_part, preferred_element_type=jnp.float32)
            * score_scale
        )
        key_grad = (
            jnp.einsum(
                "tgrs,tgrd->sgd", score_grad, query_heads, preferred_element_type=jnp.float32
            )
            * score_scale
        )
        value_grad = jnp.einsum(
            "tgrs,tgrd->sgd", probs_low, grad_heads, preferred_element_type=jnp.float32
        )
        contrib = jnp.stack(
            [
                key_grad.reshape(tokens, group_count * head_dim),
                value_grad.reshape(tokens, group_count * head_dim),
            ],
            axis=1,
        )
        return (query_acc, contrib)

    def backward_step(query_acc, kv_tile, source, group_count):
        return backward_tile(query_acc, kv_tile, source, group_count)

    def backward_turn(cycle_step, carried):
        query_acc, moving, grads_moving = carried
        query_acc, contrib = backward_step(
            query_acc, moving, (cycle_index - cycle_step) % cycle_size, groups
        )
        grads_moving = grads_moving + contrib
        moving = from_behind(moving, "ctx", 1)
        grads_moving = from_behind_2(grads_moving.astype(jnp.bfloat16), "ctx", 1).astype(
            grads_moving.dtype
        )
        return (query_acc, moving, grads_moving)

    query_acc, moving, kv_grads = lax.fori_loop(
        0,
        cycle_size,
        backward_turn,
        (
            jnp.zeros((tokens, groups, ratio, head_dim), jnp.float32),
            local_kv,
            jnp.zeros((tokens, 2, kv_width), jnp.float32),
        ),
    )
    query_grad = query_acc.astype(jnp.bfloat16).reshape(1, tokens, HEADS * head_dim)
    grad_flat = kv_grads.astype(jnp.bfloat16).reshape(tokens, 2 * kv_width)
    layer_in = inputs[0]
    grad_scale = 1.0 / math.sqrt(tokens * cycle_size * data_size)
    product = lax.dot_general(
        layer_in, grad_flat, (((0,), (0,)), ((), ())), preferred_element_type=jnp.float32
    )
    summed = lax.psum_scatter(product * grad_scale, ("dp", "ctx"), scatter_dimension=0, tiled=True)
    return (attn_out, query_grad, summed[:, :kv_width], summed[:, kv_width:])


def solution(mesh):
    in_specs = (
        P("dp", "ctx", None),
        P("dp", "ctx", None),
        P("dp", "ctx", None, None),
        P("dp", "ctx", None),
        P("dp", "ctx", None),
    )
    out_specs = (
        P("dp", "ctx", None),
        P("dp", "ctx", None),
        P(("dp", "ctx"), None),
        P(("dp", "ctx"), None),
    )
    return jax.shard_map(body, mesh=mesh, in_specs=in_specs, out_specs=out_specs, check_vma=False)
```

profile of v0, /device:TPU:0, one launch (start us, length us, event | category | flops | bytes accessed | tf_op | source)
XLA Modules:
  0.0 483.7 jit_solution(9674296410239257826)
XLA Ops:
  20.7 2.2 bitcast_add_fusion.2
  22.9 82.9 %while.46 = (s32[]{:T(128)}, f32[128,4,8]{0,2,1:T(8,128)S(1)}, f32[128,4,8]{0,2,1:T(8,128)S(1)}, f32[128,4,8,128]{3,0,2,1:T(8,128)}, bf16[128,2,512]{0,2,1:T(8,1...) while((s32[]{:T(128)}, f32[128,4,8]{0,2,1:T(8,128)S(1)}, ...), condition=%wide.region_5.6_spmd.clone.clone, body=%wide.region_2.5_spmd.clone.clone.sunk | while | flops 275329024 | bytes 31003036 | solution.py:98
  22.9 2.4 collective-permute-start
  31.8 6.0 %collective-permute-start = (bf16[128,2,512]{0,2,1:T(8,128)(2,1)}, bf16[128,2,512]{0,2,1:T(8,128)(2,1)S(1)}, u32[]{:S(2)}, u32[]{:S(2)}) collective-permute-start(bf16[128,2,512]{0,2,1:T(8,128)(2,1)} %get-tuple-element.977), channel_id=1, source_target_pairs={{0,1},{1,2},{2,3},{3,4},{4,5},{5,6},{6,7},{8,9},{9,10},{10,11},{11... | collective-permute-start | bytes 786440 | tf_op jit(solution)/shard_map/while/body/eval_jaxpr/ppermute | solution.py:16
  44.3 5.8 %collective-permute-start = (bf16[128,2,512]{0,2,1:T(8,128)(2,1)}, bf16[128,2,512]{0,2,1:T(8,128)(2,1)S(1)}, u32[]{:S(2)}, u32[]{:S(2)}) collective-permute-start(bf16[128,2,512]{0,2,1:T(8,128)(2,1)} %get-tuple-element.977), channel_id=1, source_target_pairs={{0,1},{1,2},{2,3},{3,4},{4,5},{5,6},{6,7},{8,9},{9,10},{10,11},{11... | collective-permute-start | bytes 786440 | tf_op jit(solution)/shard_map/while/body/eval_jaxpr/ppermute | solution.py:16
  56.6 5.8 %collective-permute-start = (bf16[128,2,512]{0,2,1:T(8,128)(2,1)}, bf16[128,2,512]{0,2,1:T(8,128)(2,1)S(1)}, u32[]{:S(2)}, u32[]{:S(2)}) collective-permute-start(bf16[128,2,512]{0,2,1:T(8,128)(2,1)} %get-tuple-element.977), channel_id=1, source_target_pairs={{0,1},{1,2},{2,3},{3,4},{4,5},{5,6},{6,7},{8,9},{9,10},{10,11},{11... | collective-permute-start | bytes 786440 | tf_op jit(solution)/shard_map/while/body/eval_jaxpr/ppermute | solution.py:16
  68.9 5.8 %collective-permute-start = (bf16[128,2,512]{0,2,1:T(8,128)(2,1)}, bf16[128,2,512]{0,2,1:T(8,128)(2,1)S(1)}, u32[]{:S(2)}, u32[]{:S(2)}) collective-permute-start(bf16[128,2,512]{0,2,1:T(8,128)(2,1)} %get-tuple-element.977), channel_id=1, source_target_pairs={{0,1},{1,2},{2,3},{3,4},{4,5},{5,6},{6,7},{8,9},{9,10},{10,11},{11... | collective-permute-start | bytes 786440 | tf_op jit(solution)/shard_map/while/body/eval_jaxpr/ppermute | solution.py:16
  81.2 5.8 %collective-permute-start = (bf16[128,2,512]{0,2,1:T(8,128)(2,1)}, bf16[128,2,512]{0,2,1:T(8,128)(2,1)S(1)}, u32[]{:S(2)}, u32[]{:S(2)}) collective-permute-start(bf16[128,2,512]{0,2,1:T(8,128)(2,1)} %get-tuple-element.977), channel_id=1, source_target_pairs={{0,1},{1,2},{2,3},{3,4},{4,5},{5,6},{6,7},{8,9},{9,10},{10,11},{11... | collective-permute-start | bytes 786440 | tf_op jit(solution)/shard_map/while/body/eval_jaxpr/ppermute | solution.py:16
  93.5 5.8 %collective-permute-start = (bf16[128,2,512]{0,2,1:T(8,128)(2,1)}, bf16[128,2,512]{0,2,1:T(8,128)(2,1)S(1)}, u32[]{:S(2)}, u32[]{:S(2)}) collective-permute-start(bf16[128,2,512]{0,2,1:T(8,128)(2,1)} %get-tuple-element.977), channel_id=1, source_target_pairs={{0,1},{1,2},{2,3},{3,4},{4,5},{5,6},{6,7},{8,9},{9,10},{10,11},{11... | collective-permute-start | bytes 786440 | tf_op jit(solution)/shard_map/while/body/eval_jaxpr/ppermute | solution.py:16
  105.8 2.9 copy.67
  109.3 3.1 multiply_reduce_fusion
  112.4 166.8 %while.47 = (s32[]{:T(128)}, f32[128,4,8,128]{3,0,2,1:T(8,128)}, bf16[128,2,512]{0,2,1:T(8,128)(2,1)}, f32[128,2,512]{0,2,1:T(8,128)}, s32[]{:T(128)}, /*index=5...) while((s32[]{:T(128)}, f32[128,4,8,128]{3,0,2,1:T(8,128)}, ...), condition=%wide.region_8.9_spmd.clone.clone, body=%wide.region_7.8_spmd.clone.clone.sunk | while | flops 677646336 | bytes 23532000 | solution.py:161
  113.4 6.5 %collective-permute-start.1 = (bf16[128,2,512]{0,2,1:T(8,128)(2,1)S(1)}, bf16[128,2,512]{0,2,1:T(8,128)(2,1)}, u32[]{:S(2)}, u32[]{:S(2)}) collective-permute-start(bf16[128,2,512]{0,2,1:T(8,128)(2,1)S(1)} %copy.126), channel_id=1, source_target_pairs={{0,1},{1,2},{2,3},{3,4},{4,5},{5,6},{6,7},{8,9},{9,10},{10,11},{11... | collective-permute-start | bytes 786440 | tf_op jit(solution)/shard_map/while/body/eval_jaxpr/ppermute | solution.py:16
  131.5 3.4 collective-permute-done.2
  137.7 5.6 %collective-permute-start.1 = (bf16[128,2,512]{0,2,1:T(8,128)(2,1)S(1)}, bf16[128,2,512]{0,2,1:T(8,128)(2,1)}, u32[]{:S(2)}, u32[]{:S(2)}) collective-permute-start(bf16[128,2,512]{0,2,1:T(8,128)(2,1)S(1)} %copy.126), channel_id=1, source_target_pairs={{0,1},{1,2},{2,3},{3,4},{4,5},{5,6},{6,7},{8,9},{9,10},{10,11},{11... | collective-permute-start | bytes 786440 | tf_op jit(solution)/shard_map/while/body/eval_jaxpr/ppermute | solution.py:16
  153.2 3.5 bitcast_add_fusion.6
  161.1 2.0 collective-permute-start.1
  171.2 2.4 collective-permute-start.2
  173.6 3.5 bitcast_add_fusion.6
  181.0 2.0 collective-permute-start.1
  191.1 2.3 collective-permute-start.2
  193.4 3.5 bitcast_add_fusion.6
  210.9 2.3 collective-permute-start.2
  213.2 3.5 bitcast_add_fusion.6
  230.7 2.2 collective-permute-start.2
  233.0 3.5 bitcast_add_fusion.6
  250.6 2.2 collective-permute-start.2
  252.7 3.5 bitcast_add_fusion.6
  270.4 2.1 collective-permute-start.2
  272.5 3.5 bitcast_add_fusion.6
  280.3 8.1 %multiply_bitcast_fusion = f32[4096,1024]{0,1:T(8,128)} fusion(bf16[128,1024]{0,1:T(8,128)(2,1)S(1)} %bitcast.194, bf16[1,128,4096]{2,1,0:T(8,128)(2,1)S(1)} %copy-done), kind=kOutput, calls=%fused_computation.54 | convolution fusion | flops 1077936128 | bytes 18087936 | tf_op jit(solution)/shard_map/dot_general | solution.py:175
  294.6 179.5 %reduce-scatter.2.cloned.1.call-done = f32[128,1024]{0,1:T(8,128)} async-done(((f32[4096,1024]{0,1:T(8,128)}), f32[128,1024]{0,1:T(8,128)}) %reduce-scatter.2.cloned.1.call-update) | async-done | bytes 524304 | tf_op jit(solution)/shard_map/reduce_scatter | solution.py:178
  (300 shorter events, 177.5 us)
Async XLA Ops:
  7.2 273.1 %copy-start = (bf16[1,128,4096]{2,1,0:T(8,128)(2,1)S(1)}, bf16[1,128,4096]{2,1,0:T(8,128)(2,1)}, u32[]{:S(2)}) copy-start(bf16[1,128,4096]{2,1,0:T(8,128)(2,1)} %param.9) | copy-start | bytes 3145732
  7.2 4.7 copy-start.6
  7.2 467.0 %reduce-scatter.2.cloned.1.call-start = ((), (), s32[]{:S(2)}) async-start(), calls=%async_computation.1 | async-start | bytes 17301504 | tf_op jit(solution)/shard_map/reduce_scatter | solution.py:178
  22.9 4.4 collective-permute-start
  31.8 8.1 %collective-permute-start = (bf16[128,2,512]{0,2,1:T(8,128)(2,1)}, bf16[128,2,512]{0,2,1:T(8,128)(2,1)S(1)}, u32[]{:S(2)}, u32[]{:S(2)}) collective-permute-start(bf16[128,2,512]{0,2,1:T(8,128)(2,1)} %get-tuple-element.977), channel_id=1, source_target_pairs={{0,1},{1,2},{2,3},{3,4},{4,5},{5,6},{6,7},{8,9},{9,10},{10,11},{11... | collective-permute-start | bytes 786440 | tf_op jit(solution)/shard_map/while/body/eval_jaxpr/ppermute | solution.py:16
  44.3 7.9 %collective-permute-start = (bf16[128,2,512]{0,2,1:T(8,128)(2,1)}, bf16[128,2,512]{0,2,1:T(8,128)(2,1)S(1)}, u32[]{:S(2)}, u32[]{:S(2)}) collective-permute-start(bf16[128,2,512]{0,2,1:T(8,128)(2,1)} %get-tuple-element.977), channel_id=1, source_target_pairs={{0,1},{1,2},{2,3},{3,4},{4,5},{5,6},{6,7},{8,9},{9,10},{10,11},{11... | collective-permute-start | bytes 786440 | tf_op jit(solution)/shard_map/while/body/eval_jaxpr/ppermute | solution.py:16
  56.6 7.9 %collective-permute-start = (bf16[128,2,512]{0,2,1:T(8,128)(2,1)}, bf16[128,2,512]{0,2,1:T(8,128)(2,1)S(1)}, u32[]{:S(2)}, u32[]{:S(2)}) collective-permute-start(bf16[128,2,512]{0,2,1:T(8,128)(2,1)} %get-tuple-element.977), channel_id=1, source_target_pairs={{0,1},{1,2},{2,3},{3,4},{4,5},{5,6},{6,7},{8,9},{9,10},{10,11},{11... | collective-permute-start | bytes 786440 | tf_op jit(solution)/shard_map/while/body/eval_jaxpr/ppermute | solution.py:16
  68.9 7.9 %collective-permute-start = (bf16[128,2,512]{0,2,1:T(8,128)(2,1)}, bf16[128,2,512]{0,2,1:T(8,128)(2,1)S(1)}, u32[]{:S(2)}, u32[]{:S(2)}) collective-permute-start(bf16[128,2,512]{0,2,1:T(8,128)(2,1)} %get-tuple-element.977), channel_id=1, source_target_pairs={{0,1},{1,2},{2,3},{3,4},{4,5},{5,6},{6,7},{8,9},{9,10},{10,11},{11... | collective-permute-start | bytes 786440 | tf_op jit(solution)/shard_map/while/body/eval_jaxpr/ppermute | solution.py:16
  81.2 7.9 %collective-permute-start = (bf16[128,2,512]{0,2,1:T(8,128)(2,1)}, bf16[128,2,512]{0,2,1:T(8,128)(2,1)S(1)}, u32[]{:S(2)}, u32[]{:S(2)}) collective-permute-start(bf16[128,2,512]{0,2,1:T(8,128)(2,1)} %get-tuple-element.977), channel_id=1, source_target_pairs={{0,1},{1,2},{2,3},{3,4},{4,5},{5,6},{6,7},{8,9},{9,10},{10,11},{11... | collective-permute-start | bytes 786440 | tf_op jit(solution)/shard_map/while/body/eval_jaxpr/ppermute | solution.py:16
  93.5 7.9 %collective-permute-start = (bf16[128,2,512]{0,2,1:T(8,128)(2,1)}, bf16[128,2,512]{0,2,1:T(8,128)(2,1)S(1)}, u32[]{:S(2)}, u32[]{:S(2)}) collective-permute-start(bf16[128,2,512]{0,2,1:T(8,128)(2,1)} %get-tuple-element.977), channel_id=1, source_target_pairs={{0,1},{1,2},{2,3},{3,4},{4,5},{5,6},{6,7},{8,9},{9,10},{10,11},{11... | collective-permute-start | bytes 786440 | tf_op jit(solution)/shard_map/while/body/eval_jaxpr/ppermute | solution.py:16
  113.4 23.4 %collective-permute-start.1 = (bf16[128,2,512]{0,2,1:T(8,128)(2,1)S(1)}, bf16[128,2,512]{0,2,1:T(8,128)(2,1)}, u32[]{:S(2)}, u32[]{:S(2)}) collective-permute-start(bf16[128,2,512]{0,2,1:T(8,128)(2,1)S(1)} %copy.126), channel_id=1, source_target_pairs={{0,1},{1,2},{2,3},{3,4},{4,5},{5,6},{6,7},{8,9},{9,10},{10,11},{11... | collective-permute-start | bytes 786440 | tf_op jit(solution)/shard_map/while/body/eval_jaxpr/ppermute | solution.py:16
  122.6 2.4 copy-start.4
  128.0 7.0 %collective-permute-start.2 = (bf16[128,2,512]{0,2,1:T(8,128)(2,1)}, bf16[128,2,512]{0,2,1:T(8,128)(2,1)}, u32[]{:S(2)}, u32[]{:S(2)}) collective-permute-start(bf16[128,2,512]{0,2,1:T(8,128)(2,1)} %fusion.111), channel_id=1, source_target_pairs={{0,1},{1,2},{2,3},{3,4},{4,5},{5,6},{6,7},{7,0},{8,9},{9,10},{10,1... | collective-permute-start | bytes 786440 | tf_op jit(solution)/shard_map/while/body/eval_jaxpr/ppermute | solution.py:22
  137.7 22.5 %collective-permute-start.1 = (bf16[128,2,512]{0,2,1:T(8,128)(2,1)S(1)}, bf16[128,2,512]{0,2,1:T(8,128)(2,1)}, u32[]{:S(2)}, u32[]{:S(2)}) collective-permute-start(bf16[128,2,512]{0,2,1:T(8,128)(2,1)S(1)} %copy.126), channel_id=1, source_target_pairs={{0,1},{1,2},{2,3},{3,4},{4,5},{5,6},{6,7},{8,9},{9,10},{10,11},{11... | collective-permute-start | bytes 786440 | tf_op jit(solution)/shard_map/while/body/eval_jaxpr/ppermute | solution.py:16
  146.0 2.4 copy-start.4
  151.4 7.0 %collective-permute-start.2 = (bf16[128,2,512]{0,2,1:T(8,128)(2,1)}, bf16[128,2,512]{0,2,1:T(8,128)(2,1)}, u32[]{:S(2)}, u32[]{:S(2)}) collective-permute-start(bf16[128,2,512]{0,2,1:T(8,128)(2,1)} %fusion.111), channel_id=1, source_target_pairs={{0,1},{1,2},{2,3},{3,4},{4,5},{5,6},{6,7},{7,0},{8,9},{9,10},{10,1... | collective-permute-start | bytes 786440 | tf_op jit(solution)/shard_map/while/body/eval_jaxpr/ppermute | solution.py:22
  161.1 18.9 %collective-permute-start.1 = (bf16[128,2,512]{0,2,1:T(8,128)(2,1)S(1)}, bf16[128,2,512]{0,2,1:T(8,128)(2,1)}, u32[]{:S(2)}, u32[]{:S(2)}) collective-permute-start(bf16[128,2,512]{0,2,1:T(8,128)(2,1)S(1)} %copy.126), channel_id=1, source_target_pairs={{0,1},{1,2},{2,3},{3,4},{4,5},{5,6},{6,7},{8,9},{9,10},{10,11},{11... | collective-permute-start | bytes 786440 | tf_op jit(solution)/shard_map/while/body/eval_jaxpr/ppermute | solution.py:16
  165.9 2.4 copy-start.4
  171.2 7.0 %collective-permute-start.2 = (bf16[128,2,512]{0,2,1:T(8,128)(2,1)}, bf16[128,2,512]{0,2,1:T(8,128)(2,1)}, u32[]{:S(2)}, u32[]{:S(2)}) collective-permute-start(bf16[128,2,512]{0,2,1:T(8,128)(2,1)} %fusion.111), channel_id=1, source_target_pairs={{0,1},{1,2},{2,3},{3,4},{4,5},{5,6},{6,7},{7,0},{8,9},{9,10},{10,1... | collective-permute-start | bytes 786440 | tf_op jit(solution)/shard_map/while/body/eval_jaxpr/ppermute | solution.py:22
  181.0 18.9 %collective-permute-start.1 = (bf16[128,2,512]{0,2,1:T(8,128)(2,1)S(1)}, bf16[128,2,512]{0,2,1:T(8,128)(2,1)}, u32[]{:S(2)}, u32[]{:S(2)}) collective-permute-start(bf16[128,2,512]{0,2,1:T(8,128)(2,1)S(1)} %copy.126), channel_id=1, source_target_pairs={{0,1},{1,2},{2,3},{3,4},{4,5},{5,6},{6,7},{8,9},{9,10},{10,11},{11... | collective-permute-start | bytes 786440 | tf_op jit(solution)/shard_map/while/body/eval_jaxpr/ppermute | solution.py:16
  185.7 2.4 copy-start.4
  191.1 7.0 %collective-permute-start.2 = (bf16[128,2,512]{0,2,1:T(8,128)(2,1)}, bf16[128,2,512]{0,2,1:T(8,128)(2,1)}, u32[]{:S(2)}, u32[]{:S(2)}) collective-permute-start(bf16[128,2,512]{0,2,1:T(8,128)(2,1)} %fusion.111), channel_id=1, source_target_pairs={{0,1},{1,2},{2,3},{3,4},{4,5},{5,6},{6,7},{7,0},{8,9},{9,10},{10,1... | collective-permute-start | bytes 786440 | tf_op jit(solution)/shard_map/while/body/eval_jaxpr/ppermute | solution.py:22
  200.8 18.9 %collective-permute-start.1 = (bf16[128,2,512]{0,2,1:T(8,128)(2,1)S(1)}, bf16[128,2,512]{0,2,1:T(8,128)(2,1)}, u32[]{:S(2)}, u32[]{:S(2)}) collective-permute-start(bf16[128,2,512]{0,2,1:T(8,128)(2,1)S(1)} %copy.126), channel_id=1, source_target_pairs={{0,1},{1,2},{2,3},{3,4},{4,5},{5,6},{6,7},{8,9},{9,10},{10,11},{11... | collective-permute-start | bytes 786440 | tf_op jit(solution)/shard_map/while/body/eval_jaxpr/ppermute | solution.py:16
  205.5 2.4 copy-start.4
  210.9 7.0 %collective-permute-start.2 = (bf16[128,2,512]{0,2,1:T(8,128)(2,1)}, bf16[128,2,512]{0,2,1:T(8,128)(2,1)}, u32[]{:S(2)}, u32[]{:S(2)}) collective-permute-start(bf16[128,2,512]{0,2,1:T(8,128)(2,1)} %fusion.111), channel_id=1, source_target_pairs={{0,1},{1,2},{2,3},{3,4},{4,5},{5,6},{6,7},{7,0},{8,9},{9,10},{10,1... | collective-permute-start | bytes 786440 | tf_op jit(solution)/shard_map/while/body/eval_jaxpr/ppermute | solution.py:22
  220.6 18.9 %collective-permute-start.1 = (bf16[128,2,512]{0,2,1:T(8,128)(2,1)S(1)}, bf16[128,2,512]{0,2,1:T(8,128)(2,1)}, u32[]{:S(2)}, u32[]{:S(2)}) collective-permute-start(bf16[128,2,512]{0,2,1:T(8,128)(2,1)S(1)} %copy.126), channel_id=1, source_target_pairs={{0,1},{1,2},{2,3},{3,4},{4,5},{5,6},{6,7},{8,9},{9,10},{10,11},{11... | collective-permute-start | bytes 786440 | tf_op jit(solution)/shard_map/while/body/eval_jaxpr/ppermute | solution.py:16
  225.4 2.4 copy-start.4
  230.7 7.0 %collective-permute-start.2 = (bf16[128,2,512]{0,2,1:T(8,128)(2,1)}, bf16[128,2,512]{0,2,1:T(8,128)(2,1)}, u32[]{:S(2)}, u32[]{:S(2)}) collective-permute-start(bf16[128,2,512]{0,2,1:T(8,128)(2,1)} %fusion.111), channel_id=1, source_target_pairs={{0,1},{1,2},{2,3},{3,4},{4,5},{5,6},{6,7},{7,0},{8,9},{9,10},{10,1... | collective-permute-start | bytes 786440 | tf_op jit(solution)/shard_map/while/body/eval_jaxpr/ppermute | solution.py:22
  240.5 18.9 %collective-permute-start.1 = (bf16[128,2,512]{0,2,1:T(8,128)(2,1)S(1)}, bf16[128,2,512]{0,2,1:T(8,128)(2,1)}, u32[]{:S(2)}, u32[]{:S(2)}) collective-permute-start(bf16[128,2,512]{0,2,1:T(8,128)(2,1)S(1)} %copy.126), channel_id=1, source_target_pairs={{0,1},{1,2},{2,3},{3,4},{4,5},{5,6},{6,7},{8,9},{9,10},{10,11},{11... | collective-permute-start | bytes 786440 | tf_op jit(solution)/shard_map/while/body/eval_jaxpr/ppermute | solution.py:16
  250.6 7.0 %collective-permute-start.2 = (bf16[128,2,512]{0,2,1:T(8,128)(2,1)}, bf16[128,2,512]{0,2,1:T(8,128)(2,1)}, u32[]{:S(2)}, u32[]{:S(2)}) collective-permute-start(bf16[128,2,512]{0,2,1:T(8,128)(2,1)} %fusion.111), channel_id=1, source_target_pairs={{0,1},{1,2},{2,3},{3,4},{4,5},{5,6},{6,7},{7,0},{8,9},{9,10},{10,1... | collective-permute-start | bytes 786440 | tf_op jit(solution)/shard_map/while/body/eval_jaxpr/ppermute | solution.py:22
  260.3 18.9 %collective-permute-start.1 = (bf16[128,2,512]{0,2,1:T(8,128)(2,1)S(1)}, bf16[128,2,512]{0,2,1:T(8,128)(2,1)}, u32[]{:S(2)}, u32[]{:S(2)}) collective-permute-start(bf16[128,2,512]{0,2,1:T(8,128)(2,1)S(1)} %copy.126), channel_id=1, source_target_pairs={{0,1},{1,2},{2,3},{3,4},{4,5},{5,6},{6,7},{8,9},{9,10},{10,11},{11... | collective-permute-start | bytes 786440 | tf_op jit(solution)/shard_map/while/body/eval_jaxpr/ppermute | solution.py:16
  270.4 7.0 %collective-permute-start.2 = (bf16[128,2,512]{0,2,1:T(8,128)(2,1)}, bf16[128,2,512]{0,2,1:T(8,128)(2,1)}, u32[]{:S(2)}, u32[]{:S(2)}) collective-permute-start(bf16[128,2,512]{0,2,1:T(8,128)(2,1)} %fusion.111), channel_id=1, source_target_pairs={{0,1},{1,2},{2,3},{3,4},{4,5},{5,6},{6,7},{7,0},{8,9},{9,10},{10,1... | collective-permute-start | bytes 786440 | tf_op jit(solution)/shard_map/while/body/eval_jaxpr/ppermute | solution.py:22
  (25 other events, 44.7 us)
Sparse Core Ops, SparseCore 0:
  288.5 185.5 reduce-scatter.1
where the time goes:
time: 487 us; the launch traced here: 484 us
  waiting for transfers between devices  193 us (40%)
  matrix products  87.3 us (18%)
  starting transfers between devices  78.5 us (16%)
  other arithmetic  63.3 us (13%)
  local copies, waits for them, and re-layouts  46.4 us (10%)
  between operations  14.2 us (3%)
    reduce_scatter x1, waiting for transfers between devices, body(): lax.psum_scatter(product * grad_scale, ('dp', 'ctx'), scatter_dimension=0...  180 us
    ppermute x15, starting transfers between devices, from_behind(): return lax.ppermute(block, axis, route)  61.4 us
    dot_general x8, matrix products, backward_tile(): jnp.einsum('tgrs,sgd->tgrd', score_grad, key_part, preferred_element_type...  26.1 us
    while x82, local copies, waits for them, and re-layouts  21.6 us
    eq x16, other arithmetic, tile_allowed(): jnp.repeat(jnp.repeat(block_cols, block_len, axis=0), block_len, axis=1)  20.4 us
    ppermute x8, starting transfers between devices, from_behind_2(): return lax.ppermute(value, axis, pairs)  17 us
    dot_general x8, matrix products, backward_tile(): jnp.einsum('tgrd,sgd->tgrs', query_heads, key_part, preferred_element_typ...  15.5 us
    convert_element_type x8, other arithmetic, backward_turn(): from_behind_2(grads_moving.astype(jnp.bfloat16), 'ctx', 1)  14.3 us
  transfers between devices with their start and end apart: 24, of which 9 were waited for; matrix products, arithmetic and copies ran while one was open for 26% of the time, Pallas kernels for 0%

commit v1 on v0

v1 whole, which is shorter than its diff:
```python
import functools
import math

import jax
import jax.numpy as jnp
from jax import lax
from jax.experimental import pallas as pl
from jax.experimental.pallas import tpu as pltpu
from jax.sharding import PartitionSpec as P

HEADS = 32
KV_HEADS = 4
HEAD_DIM = 128
BLOCK = 128
RATIO = HEADS // KV_HEADS
NEG = -1e30
NT = (((1,), (1,)), ((), ()))


def swap(value, axis, mask):
    pairs = [(i, i ^ mask) for i in range(lax.axis_size(axis))]
    return lax.ppermute(value, axis, pairs)


def dot(a, b, dims=(((1,), (0,)), ((), ()))):
    return lax.dot_general(a, b, dims, preferred_element_type=jnp.float32)


def attention_kernel(pieces, blocks_here, steps, per_step, where_ref, own_mask, peer_mask, *refs):
    own_q, peer_q, own_g, peer_g = refs[:4]
    kv_refs = refs[4 : 4 + pieces]
    own_o, peer_o, own_dq, peer_dq = refs[4 + pieces : 8 + pieces]
    grad_refs = refs[8 + pieces : 8 + 2 * pieces]
    bias, keys, values, keys_t, values_t, key_acc, value_acc = refs[8 + 2 * pieces :]
    group, step = pl.program_id(0), pl.program_id(1)
    rows = 2 * blocks_here * BLOCK
    score_scale = 1.0 / math.sqrt(HEAD_DIM)
    exp_scale = score_scale * math.log2(math.e)

    @pl.when((group == 0) & (step == 0))
    def _():
        me = where_ref[0]
        key_pos = lax.broadcasted_iota(jnp.int32, (BLOCK, BLOCK), 0)
        query_pos = lax.broadcasted_iota(jnp.int32, (BLOCK, BLOCK), 1)
        causal = jnp.where(key_pos <= query_pos, 0.0, NEG)
        for piece in range(pieces):
            for s in range(2 * blocks_here):
                key_device = jnp.bitwise_xor(me, 2 * piece + s // blocks_here)
                key_block = key_device * blocks_here + s % blocks_here
                for t in range(2 * blocks_here):
                    query_device = jnp.bitwise_xor(me, t // blocks_here)
                    query_block = query_device * blocks_here + t % blocks_here
                    mask_ref = own_mask if t < blocks_here else peer_mask
                    other = jnp.where(mask_ref[t % blocks_here, key_block] == 1, 0.0, NEG)
                    same = key_block == query_block
                    tile = jnp.where(same, causal, other)
                    bias[
                        piece * rows + s * BLOCK : piece * rows + (s + 1) * BLOCK,
                        t * BLOCK : (t + 1) * BLOCK,
                    ] = tile

    @pl.when(step == 0)
    def _():
        for piece in range(pieces):
            part = slice(piece * rows, (piece + 1) * rows)
            key_part = kv_refs[piece][:, :HEAD_DIM]
            value_part = kv_refs[piece][:, HEAD_DIM:]
            keys[part, :] = key_part
            values[part, :] = value_part
            keys_t[:, part] = key_part.T
            values_t[:, part] = value_part.T
        key_acc[...] = jnp.zeros_like(key_acc)
        value_acc[...] = jnp.zeros_like(value_acc)

    half = rows // 2
    for i in range(per_step):
        columns = slice(i * HEAD_DIM, (i + 1) * HEAD_DIM)
        query = jnp.concatenate([own_q[0, :, columns], peer_q[:, columns]], axis=0)
        grad = jnp.concatenate([own_g[0, :, columns], peer_g[:, columns]], axis=0)
        scores = dot(keys[...], query, NT) + bias[...]
        top = jnp.max(scores, axis=0, keepdims=True) * exp_scale
        weights = jnp.exp2(scores * exp_scale - top)
        total = jnp.sum(weights, axis=0, keepdims=True)
        probs = weights * (1.0 / total)
        probs_low = probs.astype(jnp.bfloat16)
        prob_grad = dot(values[...], grad, NT)
        delta = jnp.sum(probs * prob_grad, axis=0, keepdims=True)
        score_grad = (probs * (prob_grad - delta)).astype(jnp.bfloat16)
        value_acc[...] += dot(probs_low, grad)
        key_acc[...] += dot(score_grad, query)
        out = dot(values_t[...], probs_low).T.astype(jnp.bfloat16)
        query_grad = (dot(keys_t[...], score_grad) * score_scale).T.astype(jnp.bfloat16)
        own_o[:, columns] = out[:half]
        peer_o[:, columns] = out[half:]
        own_dq[:, columns] = query_grad[:half]
        peer_dq[:, columns] = query_grad[half:]

    @pl.when(step == steps - 1)
    def _():
        for piece in range(pieces):
            part = slice(piece * rows, (piece + 1) * rows)
            grad_refs[piece][:, :HEAD_DIM] = (key_acc[part, :] * score_scale).astype(jnp.bfloat16)
            grad_refs[piece][:, HEAD_DIM:] = value_acc[part, :].astype(jnp.bfloat16)


def attention(me, core, own_mask, peer_mask, queries, peer_q, out_grad, peer_g, kv_pieces, first):
    tokens = queries.shape[1]
    blocks_here = tokens // BLOCK
    rows = 2 * tokens
    pieces = len(kv_pieces)
    groups = kv_pieces[0].shape[1] // (2 * HEAD_DIM)
    per_step = 2
    steps = RATIO // per_step
    wide = per_step * HEAD_DIM
    half_steps = KV_HEADS // 2 * steps
    where = jnp.stack([me, core]).astype(jnp.int32)

    def own_in(g, h, where_ref, *_):
        return (0, 0, where_ref[1] * half_steps + (first + g) * steps + h)

    def peer_in(g, h, *_):
        return (0, (first + g) * steps + h)

    def out_map(g, h, *_):
        return (0, g * steps + h)

    def group_map(g, h, *_):
        return (0, g)

    keys_all = pieces * rows
    out_cols = groups * RATIO * HEAD_DIM
    result = pl.pallas_call(
        functools.partial(attention_kernel, pieces, blocks_here, steps, per_step),
        grid_spec=pltpu.PrefetchScalarGridSpec(
            num_scalar_prefetch=3,
            grid=(groups, steps),
            in_specs=[
                pl.BlockSpec((1, tokens, wide), own_in),
                pl.BlockSpec((tokens, wide), peer_in),
                pl.BlockSpec((1, tokens, wide), own_in),
                pl.BlockSpec((tokens, wide), peer_in),
            ]
            + [pl.BlockSpec((rows, 2 * HEAD_DIM), group_map)] * pieces,
            out_specs=[pl.BlockSpec((tokens, wide), out_map)] * 4
            + [pl.BlockSpec((rows, 2 * HEAD_DIM), group_map)] * pieces,
            scratch_shapes=[
                pltpu.VMEM((keys_all, rows), jnp.float32),
                pltpu.VMEM((keys_all, HEAD_DIM), jnp.bfloat16),
                pltpu.VMEM((keys_all, HEAD_DIM), jnp.bfloat16),
                pltpu.VMEM((HEAD_DIM, keys_all), jnp.bfloat16),
                pltpu.VMEM((HEAD_DIM, keys_all), jnp.bfloat16),
                pltpu.VMEM((keys_all, HEAD_DIM), jnp.float32),
                pltpu.VMEM((keys_all, HEAD_DIM), jnp.float32),
            ],
        ),
        out_shape=[jax.ShapeDtypeStruct((tokens, out_cols), jnp.bfloat16)] * 4
        + [jax.ShapeDtypeStruct((rows, 2 * HEAD_DIM * groups), jnp.bfloat16)] * pieces,
        compiler_params=pltpu.CompilerParams(vmem_limit_bytes=56 * 1024 * 1024),
        cost_estimate=pl.CostEstimate(
            flops=12 * groups * RATIO * rows * keys_all * HEAD_DIM,
            transcendentals=groups * RATIO * rows * keys_all,
            bytes_accessed=16 * tokens * out_cols,
        ),
        name="attention",
    )(where, own_mask, peer_mask, queries, peer_q, out_grad, peer_g, *kv_pieces)
    return result[:4], result[4:]


def body(inputs, queries, keys_values, out_grad, tree_mask):
    tokens = queries.shape[1]
    width = queries.shape[2]
    half = width // 2
    count = lax.axis_size("ctx")
    data_size = lax.axis_size("dp")
    me = lax.axis_index("ctx")
    data_me = lax.axis_index("dp")
    core = me % 2
    chip = me // 2
    chips = count // 2
    hops = [2 * p for p in range(1, chips)]

    own_mask = tree_mask[0]
    peer_mask = swap(own_mask, "ctx", 1)
    kv = keys_values[0].reshape(tokens, 2, KV_HEADS, HEAD_DIM)
    parts = [kv[:, :, g].reshape(tokens, 2 * HEAD_DIM) for g in range(KV_HEADS)]
    low = jnp.concatenate(parts[:2], axis=1)
    high = jnp.concatenate(parts[2:], axis=1)
    kv_keep = jnp.where(core == 0, low, high)
    kv_send = jnp.where(core == 0, high, low)
    kv_own = jnp.concatenate([kv_keep, swap(kv_send, "ctx", 1)], axis=0)
    peer_start = (1 - core) * half
    peer_q = swap(lax.dynamic_slice_in_dim(queries[0], peer_start, half, 1), "ctx", 1)
    peer_g = swap(lax.dynamic_slice_in_dim(out_grad[0], peer_start, half, 1), "ctx", 1)
    kv_pieces = [kv_own] + [swap(kv_own, "ctx", k) for k in hops]

    slices = inputs[0].reshape(tokens, data_size, chips, width // (data_size * chips))
    rows_out = width // (data_size * count)

    def slice_for(k):
        return lax.dynamic_index_in_dim(slices, (me ^ k) // 2, 2, keepdims=False)

    in_own = jnp.stack([slice_for(0)] + [swap(slice_for(k), "ctx", k) for k in hops])
    in_peer = swap(in_own, "ctx", 1)
    in_all = jnp.concatenate([in_own, in_peer], axis=1).reshape(chips * 2 * tokens, width // chips)

    (own_o, peer_o, own_dq, peer_dq), grads = attention(
        me, core, own_mask, peer_mask, queries, peer_q, out_grad, peer_g, kv_pieces, 0
    )

    def join(mine, other):
        got = swap(other, "ctx", 1)
        whole = jnp.where(
            core == 0, jnp.concatenate([mine, got], 1), jnp.concatenate([got, mine], 1)
        )
        return whole[None]

    attn_out = join(own_o, peer_o)
    query_grad = join(own_dq, peer_dq)

    total = grads[0].astype(jnp.float32)
    for p, k in enumerate(hops):
        total = total + swap(grads[p + 1], "ctx", k).astype(jnp.float32)
    total = total.astype(jnp.bfloat16)
    gathered = jnp.concatenate([total] + [swap(total, "ctx", k) for k in hops], axis=0)
    grad_scale = 1.0 / math.sqrt(tokens * count * data_size)
    product = dot(in_all, gathered, (((0,), (0,)), ((), ()))) * grad_scale
    product = product.reshape(data_size, 2 * rows_out, 4 * HEAD_DIM)

    def chunk(k):
        return lax.dynamic_index_in_dim(product, data_me ^ k, 0, keepdims=False)

    mine = chunk(0)
    for k in range(1, data_size):
        mine = mine + swap(chunk(k).astype(jnp.bfloat16), "dp", k).astype(jnp.float32)
    mine = mine.reshape(2, rows_out, 4 * HEAD_DIM)
    keep = lax.dynamic_index_in_dim(mine, core, 0, keepdims=False)
    got = swap(lax.dynamic_index_in_dim(mine, 1 - core, 0, keepdims=False), "ctx", 1)
    first = jnp.where(core == 0, keep, got).reshape(rows_out, 2, 2, HEAD_DIM)
    last = jnp.where(core == 0, got, keep).reshape(rows_out, 2, 2, HEAD_DIM)
    both = jnp.concatenate([first, last], axis=1)
    kv_width = KV_HEADS * HEAD_DIM
    return (
        attn_out,
        query_grad,
        both[:, :, 0].reshape(rows_out, kv_width),
        both[:, :, 1].reshape(rows_out, kv_width),
    )


def solution(mesh):
    in_specs = (
        P("dp", "ctx", None),
        P("dp", "ctx", None),
        P("dp", "ctx", None, None),
        P("dp", "ctx", None),
        P("dp", "ctx", None),
    )
    out_specs = (
        P("dp", "ctx", None),
        P("dp", "ctx", None),
        P(("dp", "ctx"), None),
        P(("dp", "ctx"), None),
    )
    return jax.shard_map(body, mesh=mesh, in_specs=in_specs, out_specs=out_specs, check_vma=False)
```

time: 487 us -> 120 us (0.25)
  the two profiles are of different devices: /device:TPU:0 before, /device:TPU:21 now
where the time goes in v1:
time: 120 us
  waiting for transfers between devices  45.1 us (38%)
  Pallas kernels  26.8 us (22%)
  starting transfers between devices  25.7 us (21%)
  local copies, waits for them, and re-layouts  12.6 us (10%)
  other arithmetic  6.25 us (5%)
  matrix products  2.45 us (2%)
    ppermute x23, waiting for transfers between devices, swap(): return lax.ppermute(value, axis, pairs)  45.1 us
    pallas_call x1, Pallas kernels, attention(): pl.pallas_call(functools.partial(attention_kernel, pieces, blocks_here, s...  26.8 us
    ppermute x23, starting transfers between devices, swap(): return lax.ppermute(value, axis, pairs)  25.7 us
    unnamed x21, local copies, waits for them, and re-layouts  2.69 us
    dot_general x1, matrix products, dot(): return lax.dot_general(a, b, dims, preferred_element_type=jnp.float32)  2.45 us
    select_n x2, other arithmetic, join(): jnp.where(core == 0, jnp.concatenate([mine, got], 1), jnp.concatenate([go...  2.43 us
  transfers between devices with their start and end apart: 23, of which 10 were waited for; matrix products, arithmetic and copies ran while one was open for 12% of the time, Pallas kernels for 22%

profile of v1, /device:TPU:21, one launch (start us, length us, event | category | flops | bytes accessed | tf_op | source)
XLA Modules:
  0.0 119.8 jit_solution(3746065248424464040)
XLA Ops:
  0.7 1.2 %reshape_squeeze.24 = bf16[128,2,4,128]{3,2,1,0:T(4,128)(2,1)S(1)} reshape(bf16[1,128,2,512]{3,2,1,0:T(2,128)(2,1)} %param.7) | data formatting | bytes 524288 | tf_op jit(solution)/shard_map/reshape;squeeze | solution.py:184
  1.9 1.7 %slice_reduce_fusion.4 = (bf16[128,2,128]{2,1,0:T(2,128)(2,1)S(1)}, bf16[128,2,128]{2,1,0:T(2,128)(2,1)S(1)}, bf16[128,2,128]{2,1,0:T(2,128)(2,1)S(1)}, bf16[128,2,128]{2,1,0:T(2,128)(2,1)S(1)}) fusion(bf16[128,2,4,128]{3,2,1,0:T(4,128)(2,1)S(1)} %reshape_squeeze.24), kind=kLoop, calls=%fused_computation.34 | loop fusion | bytes 524288 | tf_op jit(solution)/shard_map/slice | solution.py:185
  5.9 1.3 %collective-permute-start.9 = (bf16[128,4,256]{2,0,1:T(8,128)(2,1)S(1)}, bf16[128,4,256]{2,0,1:T(8,128)(2,1)S(1)}, u32[]{:S(2)}, u32[]{:S(2)}) collective-permute-start(bf16[128,4,256]{2,0,1:T(8,128)(2,1)S(1)} %bitcast.87), channel_id=1, source_target_pairs={{0,2},{1,3},{2,0},{3,1},{4,6},{5,7},{6,4},{7,5},{8,10},{9,11},{10,... | collective-permute-start | bytes 786440 | tf_op jit(solution)/shard_map/ppermute | solution.py:22
  7.8 1.3 %collective-permute-start.11 = (bf16[128,4,256]{2,0,1:T(8,128)(2,1)S(1)}, bf16[128,4,256]{2,0,1:T(8,128)(2,1)S(1)}, u32[]{:S(2)}, u32[]{:S(2)}) collective-permute-start(bf16[128,4,256]{2,0,1:T(8,128)(2,1)S(1)} %bitcast.85), channel_id=1, source_target_pairs={{0,6},{1,7},{2,4},{3,5},{4,2},{5,3},{6,0},{7,1},{8,14},{9,15},{10,... | collective-permute-start | bytes 786440 | tf_op jit(solution)/shard_map/ppermute | solution.py:22
  9.9 1.9 %dynamic-slice_bitcast_fusion = bf16[128,2048]{1,0:T(8,128)(2,1)} fusion(bf16[1,128,4096]{2,1,0:T(8,128)(2,1)} %refs_2_.1, s32[]{:T(128)S(6)} %select_n.107), kind=kLoop, calls=%fused_computation.19 | loop fusion | bytes 1048580 | tf_op jit(solution)/shard_map/dynamic_slice | solution.py:193
  11.8 1.3 %collective-permute-start.1 = (bf16[128,2048]{1,0:T(8,128)(2,1)}, bf16[128,2048]{1,0:T(8,128)(2,1)}, u32[]{:S(2)}, u32[]{:S(2)}) collective-permute-start(bf16[128,2048]{1,0:T(8,128)(2,1)} %dynamic-slice_bitcast_fusion.1), channel_id=1, source_target_pairs={{0,1},{1,0},{2,3},{3,2},{4,5},{5,4},{6,7},{7,6},{8,9},{9,8},{10,11... | collective-permute-start | bytes 1572872 | tf_op jit(solution)/shard_map/ppermute | solution.py:22
  14.2 1.3 %collective-permute-start.4 = (bf16[256,512]{1,0:T(8,128)(2,1)S(1)}, bf16[256,512]{1,0:T(8,128)(2,1)}, u32[]{:S(2)}, u32[]{:S(2)}) collective-permute-start(bf16[256,512]{1,0:T(8,128)(2,1)S(1)} %pad_maximum_fusion.2.refs_4_), channel_id=1, source_target_pairs={{0,2},{1,3},{2,0},{3,1},{4,6},{5,7},{6,4},{7,5},{8,10},{9,11},{10,... | collective-permute-start | bytes 786440 | tf_op jit(solution)/shard_map/ppermute | solution.py:22
  15.4 3.9 %collective-permute-done.10 = bf16[128,4,256]{2,0,1:T(8,128)(2,1)S(1)} collective-permute-done((bf16[128,4,256]{2,0,1:T(8,128)(2,1)S(1)}, bf16[128,4,256]{2,0,1:T(8,128)(2,1)S(1)}, u32[]{:S(2)}, u32[]{:S(2)}) %collective-permute-start.10) | collective-permute-done | bytes 262176 | tf_op jit(solution)/shard_map/ppermute | solution.py:22
  19.3 1.8 %collective-permute-start.6 = (bf16[256,512]{1,0:T(8,128)(2,1)S(1)}, bf16[256,512]{1,0:T(8,128)(2,1)}, u32[]{:S(2)}, u32[]{:S(2)}) collective-permute-start(bf16[256,512]{1,0:T(8,128)(2,1)S(1)} %pad_maximum_fusion.2.refs_4_), channel_id=1, source_target_pairs={{0,6},{1,7},{2,4},{3,5},{4,2},{5,3},{6,0},{7,1},{8,14},{9,15},{10,... | collective-permute-start | bytes 786440 | tf_op jit(solution)/shard_map/ppermute | solution.py:22
  22.1 2.7 %collective-permute-done.4.refs_5_ = bf16[256,512]{1,0:T(8,128)(2,1)} collective-permute-done((bf16[256,512]{1,0:T(8,128)(2,1)S(1)}, bf16[256,512]{1,0:T(8,128)(2,1)}, u32[]{:S(2)}, u32[]{:S(2)}) %collective-permute-start.4) | collective-permute-done | bytes 262176 | tf_op jit(solution)/shard_map/ppermute | solution.py:22
  24.8 2.3 %collective-permute-start.12 = (bf16[4,128,4,256]{3,1,2,0:T(8,128)(2,1)S(1)}, bf16[4,128,4,256]{3,1,2,0:T(8,128)(2,1)S(1)}, u32[]{:S(2)}, u32[]{:S(2)}) collective-permute-start(bf16[4,128,4,256]{3,1,2,0:T(8,128)(2,1)S(1)} %pad_maximum_fusion.1), channel_id=1, source_target_pairs={{0,1},{1,0},{2,3},{3,2},{4,5},{5,4},{6,7},{7,6},{8,9},{9,8},{10,11... | collective-permute-start | bytes 3145736 | tf_op jit(solution)/shard_map/ppermute | solution.py:22
  27.1 3.3 %collective-permute-done.6.refs_7_ = bf16[256,512]{1,0:T(8,128)(2,1)} collective-permute-done((bf16[256,512]{1,0:T(8,128)(2,1)S(1)}, bf16[256,512]{1,0:T(8,128)(2,1)}, u32[]{:S(2)}, u32[]{:S(2)}) %collective-permute-start.6) | collective-permute-done | bytes 262176 | tf_op jit(solution)/shard_map/ppermute | solution.py:22
  30.4 26.8 %attention.1 = (bf16[128,2048]{1,0:T(8,128)(2,1)}, bf16[128,2048]{1,0:T(8,128)(2,1)}, bf16[128,2048]{1,0:T(8,128)(2,1)}, bf16[128,2048]{1,0:T(8,128)(2,1)}, bf16...) custom-call(s32[2]{0:T(128)} %pad_add_fusion.where_ref, ...), custom_call_target="tpu_custom_call" | custom-call | flops 6442450944 | bytes 4194304 | tf_op jit(solution)/shard_map/attention/pallas_call | solution.py:132
  57.2 1.3 %collective-permute-start.13 = (bf16[256,512]{1,0:T(8,128)(2,1)}, bf16[256,512]{1,0:T(8,128)(2,1)S(1)}, u32[]{:S(2)}, u32[]{:S(2)}) collective-permute-start(bf16[256,512]{1,0:T(8,128)(2,1)} %get-tuple-element.17), channel_id=1, source_target_pairs={{0,2},{1,3},{2,0},{3,1},{4,6},{5,7},{6,4},{7,5},{8,10},{9,11},{10,... | collective-permute-start | bytes 786440 | tf_op jit(solution)/shard_map/ppermute | solution.py:22
  59.9 2.8 %collective-permute-done.13 = bf16[256,512]{1,0:T(8,128)(2,1)S(1)} collective-permute-done((bf16[256,512]{1,0:T(8,128)(2,1)}, bf16[256,512]{1,0:T(8,128)(2,1)S(1)}, u32[]{:S(2)}, u32[]{:S(2)}) %collective-permute-start.13) | collective-permute-done | bytes 262176 | tf_op jit(solution)/shard_map/ppermute | solution.py:22
  62.7 4.3 %collective-permute-done.14 = bf16[256,512]{1,0:T(8,128)(2,1)S(1)} collective-permute-done((bf16[256,512]{1,0:T(8,128)(2,1)}, bf16[256,512]{1,0:T(8,128)(2,1)S(1)}, u32[]{:S(2)}, u32[]{:S(2)}) %collective-permute-start.14) | collective-permute-done | bytes 262176 | tf_op jit(solution)/shard_map/ppermute | solution.py:22
  67.0 2.6 %collective-permute-done.15 = bf16[256,512]{1,0:T(8,128)(2,1)S(1)} collective-permute-done((bf16[256,512]{1,0:T(8,128)(2,1)}, bf16[256,512]{1,0:T(8,128)(2,1)S(1)}, u32[]{:S(2)}, u32[]{:S(2)}) %collective-permute-start.15) | collective-permute-done | bytes 262176 | tf_op jit(solution)/shard_map/ppermute | solution.py:22
  70.7 2.2 %collective-permute-start.16 = (bf16[256,512]{1,0:T(8,128)(2,1)S(1)}, bf16[256,512]{1,0:T(8,128)(2,1)}, u32[]{:S(2)}, u32[]{:S(2)}) collective-permute-start(bf16[256,512]{1,0:T(8,128)(2,1)S(1)} %add_convert_fusion), channel_id=1, source_target_pairs={{0,2},{1,3},{2,0},{3,1},{4,6},{5,7},{6,4},{7,5},{8,10},{9,11},{10,... | collective-permute-start | bytes 786440 | tf_op jit(solution)/shard_map/ppermute | solution.py:22
  72.9 1.3 %collective-permute-start.18 = (bf16[256,512]{1,0:T(8,128)(2,1)S(1)}, bf16[256,512]{1,0:T(8,128)(2,1)}, u32[]{:S(2)}, u32[]{:S(2)}) collective-permute-start(bf16[256,512]{1,0:T(8,128)(2,1)S(1)} %add_convert_fusion), channel_id=1, source_target_pairs={{0,6},{1,7},{2,4},{3,5},{4,2},{5,3},{6,0},{7,1},{8,14},{9,15},{10,... | collective-permute-start | bytes 786440 | tf_op jit(solution)/shard_map/ppermute | solution.py:22
  74.1 3.8 %collective-permute-start.8 = (bf16[128,2048]{1,0:T(8,128)(2,1)}, bf16[128,2048]{1,0:T(8,128)(2,1)S(1)}, u32[]{:S(2)}, u32[]{:S(2)}) collective-permute-start(bf16[128,2048]{1,0:T(8,128)(2,1)} %get-tuple-element.15), channel_id=1, source_target_pairs={{0,1},{1,0},{2,3},{3,2},{4,5},{5,4},{6,7},{7,6},{8,9},{9,8},{10,11... | collective-permute-start | bytes 1572872 | tf_op jit(solution)/shard_map/ppermute | solution.py:22
  78.1 1.6 %copy.26 = bf16[4,256,4,256]{3,2,1,0:T(4,128)(2,1)S(1)} copy(bf16[4,256,4,256]{3,1,2,0:T(8,128)(2,1)S(1)} %pad_maximum_fusion) | data formatting | bytes 4194304 | tf_op jit(solution)/shard_map/concatenate | solution.py:204
  80.3 5.2 %collective-permute-done.17 = bf16[256,512]{1,0:T(8,128)(2,1)} collective-permute-done((bf16[256,512]{1,0:T(8,128)(2,1)S(1)}, bf16[256,512]{1,0:T(8,128)(2,1)}, u32[]{:S(2)}, u32[]{:S(2)}) %collective-permute-start.17) | collective-permute-done | bytes 262176 | tf_op jit(solution)/shard_map/ppermute | solution.py:22
  85.4 2.5 %convolution_multiply_fusion = f32[1024,512]{1,0:T(8,128)S(1)} fusion(bf16[1024,1024]{1,0:T(8,128)(2,1)S(1)} %bitcast.66, bf16[256,512]{1,0:T(8,128)(2,1)} %collective-permute-done.18, bf16[256,512]{1,0:T(8,128)(2,1)} %collective-permute-done.17, bf16[256,512]{1,0:T(8,128)(2,1)} %collective-permute-done.16, bf16[256,512]{1,0:T(8,128)(2,1)S(1)} %add_convert_fusion), kind=kOutput, calls=%fused_computation.1 | convolution fusion | flops 1078460416 | bytes 5242880 | tf_op jit(solution)/shard_map/dot_general | solution.py:26
  88.0 1.4 %collective-permute-start.19 = (bf16[256,512]{1,0:T(8,128)(2,1)S(1)}, bf16[256,512]{1,0:T(8,128)(2,1)S(1)}, u32[]{:S(2)}, u32[]{:S(2)}) collective-permute-start(bf16[256,512]{1,0:T(8,128)(2,1)S(1)} %get-tuple-element.26), channel_id=1, source_target_pairs={{0,8},{8,0},{16,24},{24,16},{1,9},{9,1},{17,25},{25,17},{2,10},{10... | collective-permute-start | bytes 786440 | tf_op jit(solution)/shard_map/ppermute | solution.py:22
  89.4 1.3 %collective-permute-start.21 = (bf16[256,512]{1,0:T(8,128)(2,1)S(1)}, bf16[256,512]{1,0:T(8,128)(2,1)S(1)}, u32[]{:S(2)}, u32[]{:S(2)}) collective-permute-start(bf16[256,512]{1,0:T(8,128)(2,1)S(1)} %get-tuple-element.27), channel_id=1, source_target_pairs={{0,24},{8,16},{16,8},{24,0},{1,25},{9,17},{17,9},{25,1},{2,26},{10... | collective-permute-start | bytes 786440 | tf_op jit(solution)/shard_map/ppermute | solution.py:22
  90.7 1.2 %maximum_select_fusion.1 = bf16[1,128,4096]{2,1,0:T(8,128)(2,1)} fusion(bf16[1,128,2048]{2,1,0:T(8,128)(2,1)S(1)} %bitcast.82, bf16[1,128,2048]{2,1,0:T(8,128)(2,1)S(1)} %bitcast.80, pred[]{:T(512)S(6)} %eq.4), kind=kLoop, calls=%fused_computation.3 | loop fusion | flops 4718592 | bytes 2097153 | tf_op jit(solution)/shard_map/jit(_where)/select_n | solution.py:212
  92.0 6.0 %collective-permute-done.19 = bf16[256,512]{1,0:T(8,128)(2,1)S(1)} collective-permute-done((bf16[256,512]{1,0:T(8,128)(2,1)S(1)}, bf16[256,512]{1,0:T(8,128)(2,1)S(1)}, u32[]{:S(2)}, u32[]{:S(2)}) %collective-permute-start.19) | collective-permute-done | bytes 262176 | tf_op jit(solution)/shard_map/ppermute | solution.py:22
  98.0 1.5 %collective-permute-done.20 = bf16[256,512]{1,0:T(8,128)(2,1)S(1)} collective-permute-done((bf16[256,512]{1,0:T(8,128)(2,1)S(1)}, bf16[256,512]{1,0:T(8,128)(2,1)S(1)}, u32[]{:S(2)}, u32[]{:S(2)}) %collective-permute-start.20) | collective-permute-done | bytes 262176 | tf_op jit(solution)/shard_map/ppermute | solution.py:22
  99.5 12.7 %collective-permute-done.21 = bf16[256,512]{1,0:T(8,128)(2,1)S(1)} collective-permute-done((bf16[256,512]{1,0:T(8,128)(2,1)S(1)}, bf16[256,512]{1,0:T(8,128)(2,1)S(1)}, u32[]{:S(2)}, u32[]{:S(2)}) %collective-permute-start.21) | collective-permute-done | bytes 262176 | tf_op jit(solution)/shard_map/ppermute | solution.py:22
  112.4 2.7 %collective-permute-start.22 = (f32[128,512]{1,0:T(8,128)S(1)}, f32[128,512]{1,0:T(8,128)S(1)}, u32[]{:S(2)}, u32[]{:S(2)}) collective-permute-start(f32[128,512]{1,0:T(8,128)S(1)} %dynamic-slice_bitcast_fusion.2), channel_id=1, source_target_pairs={{0,1},{1,0},{2,3},{3,2},{4,5},{5,4},{6,7},{7,6},{8,9},{9,8},{10,11... | collective-permute-start | bytes 786440 | tf_op jit(solution)/shard_map/ppermute | solution.py:22
  115.1 1.2 %maximum_select_fusion = bf16[1,128,4096]{2,1,0:T(8,128)(2,1)} fusion(bf16[1,128,2048]{2,1,0:T(8,128)(2,1)S(1)} %bitcast.81, bf16[1,128,2048]{2,1,0:T(8,128)(2,1)S(1)} %bitcast.79, pred[]{:T(512)S(6)} %eq.4), kind=kLoop, calls=%fused_computation.2 | loop fusion | flops 4718592 | bytes 2097153 | tf_op jit(solution)/shard_map/jit(_where)/select_n | solution.py:212
  116.9 1.5 %slice_reduce_fusion = (f32[128,4,128]{2,1,0:T(4,128)S(1)}, f32[128,4,128]{2,1,0:T(4,128)S(1)}) fusion(f32[128,4,2,128]{3,2,1,0:T(2,128)S(1)} %constant_dynamic-update-slice_fusion), kind=kLoop, calls=%fused_computation.26 | loop fusion | bytes 1048576 | tf_op jit(solution)/shard_map/slice | solution.py:246
  (64 shorter events, 11.1 us)
Async XLA Ops:
  0.6 4.3 %copy-start.5 = (s32[1,1,8]{2,1,0:T(1,128)S(1)}, s32[1,1,8]{2,1,0:T(1,128)}, u32[]{:S(2)}) copy-start(s32[1,1,8]{2,1,0:T(1,128)} %param.9) | copy-start | bytes 100
  0.6 4.3 %copy-start = (bf16[1,128,4096]{2,1,0:T(8,128)(2,1)S(1)}, bf16[1,128,4096]{2,1,0:T(8,128)(2,1)}, u32[]{:S(2)}) copy-start(bf16[1,128,4096]{2,1,0:T(8,128)(2,1)} %param.5) | copy-start | bytes 3145732
  4.3 8.8 %collective-permute-start.3 = (bf16[128,512]{1,0:T(8,128)(2,1)}, bf16[128,512]{1,0:T(8,128)(2,1)}, u32[]{:S(2)}, u32[]{:S(2)}) collective-permute-start(bf16[128,512]{1,0:T(8,128)(2,1)} %get-tuple-element.36), channel_id=1, source_target_pairs={{0,1},{1,0},{2,3},{3,2},{4,5},{5,4},{6,7},{7,6},{8,9},{9,8},{10,11... | collective-permute-start | bytes 393224 | tf_op jit(solution)/shard_map/ppermute | solution.py:22
  5.0 6.8 %collective-permute-start = (s32[1,8]{1,0:T(1,128)S(1)}, s32[1,8]{1,0:T(1,128)S(1)}, u32[]{:S(2)}, u32[]{:S(2)}) collective-permute-start(s32[1,8]{1,0:T(1,128)S(1)} %bitcast.93), channel_id=1, source_target_pairs={{0,1},{1,0},{2,3},{3,2},{4,5},{5,4},{6,7},{7,6},{8,9},{9,8},{10,11... | collective-permute-start | bytes 104 | tf_op jit(solution)/shard_map/ppermute | solution.py:22
  5.6 3.4 %copy-start.4 = (bf16[1,128,4096]{2,1,0:T(8,128)(2,1)S(1)}, bf16[1,128,4096]{2,1,0:T(8,128)(2,1)}, u32[]{:S(2)}) copy-start(bf16[1,128,4096]{2,1,0:T(8,128)(2,1)} %refs_0_.1) | copy-start | bytes 3145732
  5.9 8.2 %collective-permute-start.9 = (bf16[128,4,256]{2,0,1:T(8,128)(2,1)S(1)}, bf16[128,4,256]{2,0,1:T(8,128)(2,1)S(1)}, u32[]{:S(2)}, u32[]{:S(2)}) collective-permute-start(bf16[128,4,256]{2,0,1:T(8,128)(2,1)S(1)} %bitcast.87), channel_id=1, source_target_pairs={{0,2},{1,3},{2,0},{3,1},{4,6},{5,7},{6,4},{7,5},{8,10},{9,11},{10,... | collective-permute-start | bytes 786440 | tf_op jit(solution)/shard_map/ppermute | solution.py:22
  7.4 12.0 %collective-permute-start.10 = (bf16[128,4,256]{2,0,1:T(8,128)(2,1)S(1)}, bf16[128,4,256]{2,0,1:T(8,128)(2,1)S(1)}, u32[]{:S(2)}, u32[]{:S(2)}) collective-permute-start(bf16[128,4,256]{2,0,1:T(8,128)(2,1)S(1)} %bitcast.86), channel_id=1, source_target_pairs={{0,4},{1,5},{2,6},{3,7},{4,0},{5,1},{6,2},{7,3},{8,12},{9,13},{10,... | collective-permute-start | bytes 786440 | tf_op jit(solution)/shard_map/ppermute | solution.py:22
  7.8 11.5 %collective-permute-start.11 = (bf16[128,4,256]{2,0,1:T(8,128)(2,1)S(1)}, bf16[128,4,256]{2,0,1:T(8,128)(2,1)S(1)}, u32[]{:S(2)}, u32[]{:S(2)}) collective-permute-start(bf16[128,4,256]{2,0,1:T(8,128)(2,1)S(1)} %bitcast.85), channel_id=1, source_target_pairs={{0,6},{1,7},{2,4},{3,5},{4,2},{5,3},{6,0},{7,1},{8,14},{9,15},{10,... | collective-permute-start | bytes 786440 | tf_op jit(solution)/shard_map/ppermute | solution.py:22
  11.8 18.6 %copy-start.6 = (s32[1,8]{1,0:T(1,128)}, s32[1,8]{1,0:T(1,128)S(1)}, u32[]{:S(2)}) copy-start(s32[1,8]{1,0:T(1,128)S(1)} %collective-permute-done.peer_mask) | copy-start | bytes 100
  11.8 18.6 %collective-permute-start.1 = (bf16[128,2048]{1,0:T(8,128)(2,1)}, bf16[128,2048]{1,0:T(8,128)(2,1)}, u32[]{:S(2)}, u32[]{:S(2)}) collective-permute-start(bf16[128,2048]{1,0:T(8,128)(2,1)} %dynamic-slice_bitcast_fusion.1), channel_id=1, source_target_pairs={{0,1},{1,0},{2,3},{3,2},{4,5},{5,4},{6,7},{7,6},{8,9},{9,8},{10,11... | collective-permute-start | bytes 1572872 | tf_op jit(solution)/shard_map/ppermute | solution.py:22
  13.1 17.2 %collective-permute-start.2 = (bf16[128,2048]{1,0:T(8,128)(2,1)}, bf16[128,2048]{1,0:T(8,128)(2,1)}, u32[]{:S(2)}, u32[]{:S(2)}) collective-permute-start(bf16[128,2048]{1,0:T(8,128)(2,1)} %dynamic-slice_bitcast_fusion), channel_id=1, source_target_pairs={{0,1},{1,0},{2,3},{3,2},{4,5},{5,4},{6,7},{7,6},{8,9},{9,8},{10,11... | collective-permute-start | bytes 1572872 | tf_op jit(solution)/shard_map/ppermute | solution.py:22
  14.1 16.2 %copy-start.3 = (bf16[256,512]{1,0:T(8,128)(2,1)}, bf16[256,512]{1,0:T(8,128)(2,1)S(1)}, u32[]{:S(2)}) copy-start(bf16[256,512]{1,0:T(8,128)(2,1)S(1)} %pad_maximum_fusion.2.refs_4_) | copy-start | bytes 786436
  14.2 10.6 %collective-permute-start.4 = (bf16[256,512]{1,0:T(8,128)(2,1)S(1)}, bf16[256,512]{1,0:T(8,128)(2,1)}, u32[]{:S(2)}, u32[]{:S(2)}) collective-permute-start(bf16[256,512]{1,0:T(8,128)(2,1)S(1)} %pad_maximum_fusion.2.refs_4_), channel_id=1, source_target_pairs={{0,2},{1,3},{2,0},{3,1},{4,6},{5,7},{6,4},{7,5},{8,10},{9,11},{10,... | collective-permute-start | bytes 786440 | tf_op jit(solution)/shard_map/ppermute | solution.py:22
  19.3 7.7 %collective-permute-start.5 = (bf16[256,512]{1,0:T(8,128)(2,1)S(1)}, bf16[256,512]{1,0:T(8,128)(2,1)}, u32[]{:S(2)}, u32[]{:S(2)}) collective-permute-start(bf16[256,512]{1,0:T(8,128)(2,1)S(1)} %pad_maximum_fusion.2.refs_4_), channel_id=1, source_target_pairs={{0,4},{1,5},{2,6},{3,7},{4,0},{5,1},{6,2},{7,3},{8,12},{9,13},{10,... | collective-permute-start | bytes 786440 | tf_op jit(solution)/shard_map/ppermute | solution.py:22
  19.3 11.1 %collective-permute-start.6 = (bf16[256,512]{1,0:T(8,128)(2,1)S(1)}, bf16[256,512]{1,0:T(8,128)(2,1)}, u32[]{:S(2)}, u32[]{:S(2)}) collective-permute-start(bf16[256,512]{1,0:T(8,128)(2,1)S(1)} %pad_maximum_fusion.2.refs_4_), channel_id=1, source_target_pairs={{0,6},{1,7},{2,4},{3,5},{4,2},{5,3},{6,0},{7,1},{8,14},{9,15},{10,... | collective-permute-start | bytes 786440 | tf_op jit(solution)/shard_map/ppermute | solution.py:22
  24.8 53.2 %collective-permute-start.12 = (bf16[4,128,4,256]{3,1,2,0:T(8,128)(2,1)S(1)}, bf16[4,128,4,256]{3,1,2,0:T(8,128)(2,1)S(1)}, u32[]{:S(2)}, u32[]{:S(2)}) collective-permute-start(bf16[4,128,4,256]{3,1,2,0:T(8,128)(2,1)S(1)} %pad_maximum_fusion.1), channel_id=1, source_target_pairs={{0,1},{1,0},{2,3},{3,2},{4,5},{5,4},{6,7},{7,6},{8,9},{9,8},{10,11... | collective-permute-start | bytes 3145736 | tf_op jit(solution)/shard_map/ppermute | solution.py:22
  57.2 5.5 %collective-permute-start.13 = (bf16[256,512]{1,0:T(8,128)(2,1)}, bf16[256,512]{1,0:T(8,128)(2,1)S(1)}, u32[]{:S(2)}, u32[]{:S(2)}) collective-permute-start(bf16[256,512]{1,0:T(8,128)(2,1)} %get-tuple-element.17), channel_id=1, source_target_pairs={{0,2},{1,3},{2,0},{3,1},{4,6},{5,7},{6,4},{7,5},{8,10},{9,11},{10,... | collective-permute-start | bytes 786440 | tf_op jit(solution)/shard_map/ppermute | solution.py:22
  58.4 8.5 %collective-permute-start.14 = (bf16[256,512]{1,0:T(8,128)(2,1)}, bf16[256,512]{1,0:T(8,128)(2,1)S(1)}, u32[]{:S(2)}, u32[]{:S(2)}) collective-permute-start(bf16[256,512]{1,0:T(8,128)(2,1)} %get-tuple-element.18), channel_id=1, source_target_pairs={{0,4},{1,5},{2,6},{3,7},{4,0},{5,1},{6,2},{7,3},{8,12},{9,13},{10,... | collective-permute-start | bytes 786440 | tf_op jit(solution)/shard_map/ppermute | solution.py:22
  59.6 10.0 %collective-permute-start.15 = (bf16[256,512]{1,0:T(8,128)(2,1)}, bf16[256,512]{1,0:T(8,128)(2,1)S(1)}, u32[]{:S(2)}, u32[]{:S(2)}) collective-permute-start(bf16[256,512]{1,0:T(8,128)(2,1)} %get-tuple-element.19), channel_id=1, source_target_pairs={{0,6},{1,7},{2,4},{3,5},{4,2},{5,3},{6,0},{7,1},{8,14},{9,15},{10,... | collective-permute-start | bytes 786440 | tf_op jit(solution)/shard_map/ppermute | solution.py:22
  70.7 9.6 %collective-permute-start.16 = (bf16[256,512]{1,0:T(8,128)(2,1)S(1)}, bf16[256,512]{1,0:T(8,128)(2,1)}, u32[]{:S(2)}, u32[]{:S(2)}) collective-permute-start(bf16[256,512]{1,0:T(8,128)(2,1)S(1)} %add_convert_fusion), channel_id=1, source_target_pairs={{0,2},{1,3},{2,0},{3,1},{4,6},{5,7},{6,4},{7,5},{8,10},{9,11},{10,... | collective-permute-start | bytes 786440 | tf_op jit(solution)/shard_map/ppermute | solution.py:22
  72.9 12.6 %collective-permute-start.17 = (bf16[256,512]{1,0:T(8,128)(2,1)S(1)}, bf16[256,512]{1,0:T(8,128)(2,1)}, u32[]{:S(2)}, u32[]{:S(2)}) collective-permute-start(bf16[256,512]{1,0:T(8,128)(2,1)S(1)} %add_convert_fusion), channel_id=1, source_target_pairs={{0,4},{1,5},{2,6},{3,7},{4,0},{5,1},{6,2},{7,3},{8,12},{9,13},{10,... | collective-permute-start | bytes 786440 | tf_op jit(solution)/shard_map/ppermute | solution.py:22
  72.9 12.6 %collective-permute-start.18 = (bf16[256,512]{1,0:T(8,128)(2,1)S(1)}, bf16[256,512]{1,0:T(8,128)(2,1)}, u32[]{:S(2)}, u32[]{:S(2)}) collective-permute-start(bf16[256,512]{1,0:T(8,128)(2,1)S(1)} %add_convert_fusion), channel_id=1, source_target_pairs={{0,6},{1,7},{2,4},{3,5},{4,2},{5,3},{6,0},{7,1},{8,14},{9,15},{10,... | collective-permute-start | bytes 786440 | tf_op jit(solution)/shard_map/ppermute | solution.py:22
  74.1 16.6 %collective-permute-start.8 = (bf16[128,2048]{1,0:T(8,128)(2,1)}, bf16[128,2048]{1,0:T(8,128)(2,1)S(1)}, u32[]{:S(2)}, u32[]{:S(2)}) collective-permute-start(bf16[128,2048]{1,0:T(8,128)(2,1)} %get-tuple-element.15), channel_id=1, source_target_pairs={{0,1},{1,0},{2,3},{3,2},{4,5},{5,4},{6,7},{7,6},{8,9},{9,8},{10,11... | collective-permute-start | bytes 1572872 | tf_op jit(solution)/shard_map/ppermute | solution.py:22
  77.9 37.2 %collective-permute-start.7 = (bf16[128,2048]{1,0:T(8,128)(2,1)}, bf16[128,2048]{1,0:T(8,128)(2,1)S(1)}, u32[]{:S(2)}, u32[]{:S(2)}) collective-permute-start(bf16[128,2048]{1,0:T(8,128)(2,1)} %get-tuple-element.13), channel_id=1, source_target_pairs={{0,1},{1,0},{2,3},{3,2},{4,5},{5,4},{6,7},{7,6},{8,9},{9,8},{10,11... | collective-permute-start | bytes 1572872 | tf_op jit(solution)/shard_map/ppermute | solution.py:22
  85.4 5.3 %copy-start.2 = (bf16[128,2048]{1,0:T(8,128)(2,1)S(1)}, bf16[128,2048]{1,0:T(8,128)(2,1)}, u32[]{:S(2)}) copy-start(bf16[128,2048]{1,0:T(8,128)(2,1)} %get-tuple-element.14) | copy-start | bytes 1572868
  88.0 10.0 %collective-permute-start.19 = (bf16[256,512]{1,0:T(8,128)(2,1)S(1)}, bf16[256,512]{1,0:T(8,128)(2,1)S(1)}, u32[]{:S(2)}, u32[]{:S(2)}) collective-permute-start(bf16[256,512]{1,0:T(8,128)(2,1)S(1)} %get-tuple-element.26), channel_id=1, source_target_pairs={{0,8},{8,0},{16,24},{24,16},{1,9},{9,1},{17,25},{25,17},{2,10},{10... | collective-permute-start | bytes 786440 | tf_op jit(solution)/shard_map/ppermute | solution.py:22
  89.4 10.1 %collective-permute-start.20 = (bf16[256,512]{1,0:T(8,128)(2,1)S(1)}, bf16[256,512]{1,0:T(8,128)(2,1)S(1)}, u32[]{:S(2)}, u32[]{:S(2)}) collective-permute-start(bf16[256,512]{1,0:T(8,128)(2,1)S(1)} %get-tuple-element.28), channel_id=1, source_target_pairs={{0,16},{8,24},{16,0},{24,8},{1,17},{9,25},{17,1},{25,9},{2,18},{10... | collective-permute-start | bytes 786440 | tf_op jit(solution)/shard_map/ppermute | solution.py:22
  89.4 22.8 %collective-permute-start.21 = (bf16[256,512]{1,0:T(8,128)(2,1)S(1)}, bf16[256,512]{1,0:T(8,128)(2,1)S(1)}, u32[]{:S(2)}, u32[]{:S(2)}) collective-permute-start(bf16[256,512]{1,0:T(8,128)(2,1)S(1)} %get-tuple-element.27), channel_id=1, source_target_pairs={{0,24},{8,16},{16,8},{24,0},{1,25},{9,17},{17,9},{25,1},{2,26},{10... | collective-permute-start | bytes 786440 | tf_op jit(solution)/shard_map/ppermute | solution.py:22
  90.7 24.4 %copy-start.1 = (bf16[128,2048]{1,0:T(8,128)(2,1)S(1)}, bf16[128,2048]{1,0:T(8,128)(2,1)}, u32[]{:S(2)}) copy-start(bf16[128,2048]{1,0:T(8,128)(2,1)} %get-tuple-element.12) | copy-start | bytes 1572868
  112.4 4.0 %collective-permute-start.22 = (f32[128,512]{1,0:T(8,128)S(1)}, f32[128,512]{1,0:T(8,128)S(1)}, u32[]{:S(2)}, u32[]{:S(2)}) collective-permute-start(f32[128,512]{1,0:T(8,128)S(1)} %dynamic-slice_bitcast_fusion.2), channel_id=1, source_target_pairs={{0,1},{1,0},{2,3},{3,2},{4,5},{5,4},{6,7},{7,6},{8,9},{9,8},{10,11... | collective-permute-start | bytes 786440 | tf_op jit(solution)/shard_map/ppermute | solution.py:22

commit v2 on v1

v2 whole, which is shorter than its diff:
```python
import functools
import math

import jax
import jax.numpy as jnp
from jax import lax
from jax.experimental import pallas as pl
from jax.experimental.pallas import tpu as pltpu
from jax.sharding import PartitionSpec as P

HEADS = 32
KV_HEADS = 4
HEAD_DIM = 128
BLOCK = 128
RATIO = HEADS // KV_HEADS
NEG = -1e30
NT = (((1,), (1,)), ((), ()))


def swap(value, axis, mask):
    pairs = [(i, i ^ mask) for i in range(lax.axis_size(axis))]
    return lax.ppermute(value, axis, pairs)


def dot(a, b, dims=(((1,), (0,)), ((), ()))):
    return lax.dot_general(a, b, dims, preferred_element_type=jnp.float32)


def copy_columns(chips, span, wide, chip, inputs_ref, outs, start):
    for k, out in enumerate(outs):
        for i, d in enumerate(span):
            source = pl.ds(pl.multiple_of((d * chips + jnp.bitwise_xor(chip, k)) * wide, wide), wide)
            out[:, start + i * wide : start + (i + 1) * wide] = inputs_ref[0, :, source]


def attention_kernel(pieces, blocks_here, steps, per_step, span, wide, where_ref, own_mask, peer_mask, *refs):
    if span:
        inputs_ref, *refs = refs
    own_q, peer_q, own_g, peer_g = refs[:4]
    kv_refs = refs[4 : 4 + pieces]
    own_o, own_dq, peer_out = refs[4 + pieces : 7 + pieces]
    grad_refs = refs[7 + pieces : 7 + 2 * pieces]
    (mask_cols, causal, keys, values, keys_t, values_t, key_acc, value_acc, scores, weights, flows) = refs[
        7 + 2 * pieces :
    ]
    group, step = pl.program_id(0), pl.program_id(1)
    rows = 2 * blocks_here * BLOCK
    half = rows // 2
    blocks = 2 * blocks_here
    tiles = pieces * blocks
    score_scale = 1.0 / math.sqrt(HEAD_DIM)
    exp_scale = score_scale * math.log2(math.e)
    low = jnp.bfloat16

    @pl.when((group == 0) & (step == 0))
    def _():
        me = where_ref[0]
        lane = lax.broadcasted_iota(jnp.int32, (BLOCK, HEAD_DIM), 1)
        for t in range(blocks):
            mask_ref = own_mask if t < blocks_here else peer_mask
            tile = jnp.zeros((BLOCK, HEAD_DIM), jnp.float32)
            for block in range(tiles):
                key_device = jnp.bitwise_xor(me, block // blocks_here)
                seen = mask_ref[t % blocks_here, key_device * blocks_here + block % blocks_here]
                tile = jnp.where(lane == block, jnp.where(seen == 1, 0.0, NEG), tile)
            mask_cols[t * BLOCK : (t + 1) * BLOCK, :] = tile.astype(low)
        for block in range(tiles):
            part = slice(block * BLOCK, (block + 1) * BLOCK)
            keys[part, HEAD_DIM:] = jnp.where(lane == block, 1.0, 0.0).astype(low)
            values[part, HEAD_DIM:] = jnp.where(lane < 3, 1.0, 0.0).astype(low)
        key_pos = lax.broadcasted_iota(jnp.int32, (BLOCK, BLOCK), 0)
        query_pos = lax.broadcasted_iota(jnp.int32, (BLOCK, BLOCK), 1)
        causal[...] = jnp.where(key_pos <= query_pos, 0.0, NEG)

    @pl.when(step == 0)
    def _():
        for piece in range(2 * pieces):
            part = slice(piece * half, (piece + 1) * half)
            column = piece % 2 * 2 * HEAD_DIM
            key_part = kv_refs[piece // 2][:, column : column + HEAD_DIM]
            value_part = kv_refs[piece // 2][:, column + HEAD_DIM : column + 2 * HEAD_DIM]
            keys[part, :HEAD_DIM] = key_part
            values[part, :HEAD_DIM] = value_part
            keys_t[:, part] = key_part.T
            values_t[:, part] = value_part.T
        key_acc[...] = jnp.zeros_like(key_acc)
        value_acc[...] = jnp.zeros_like(value_acc)

    state = [dict() for _ in range(per_step)]

    def take(own, peer, i):
        columns = slice(i * HEAD_DIM, (i + 1) * HEAD_DIM)
        return jnp.concatenate([own[0, :, columns], peer[0, :, columns]], axis=0)

    def fold(x, op):
        return op(x.reshape(x.shape[0] // 8, 8, x.shape[1]), axis=0)

    def score(i):
        query = jnp.concatenate([take(own_q, peer_q, i), mask_cols[...]], axis=1)
        top = None
        for tile in range(tiles):
            part = slice(tile * BLOCK, (tile + 1) * BLOCK)
            got = dot(keys[part, :], query, NT)
            if tile < blocks:
                here = slice(tile * BLOCK, (tile + 1) * BLOCK)
                cut = got[:, here] + causal[...]
                got = jnp.concatenate(
                    [x for x in (got[:, : here.start], cut, got[:, here.stop :]) if x.shape[1]], axis=1
                )
            scores[i, part, :] = got
            best = fold(got, jnp.max)
            top = best if top is None else jnp.maximum(top, best)
        state[i]["top"] = jnp.max(top, axis=0, keepdims=True) * exp_scale

    def soften(i):
        top = state[i]["top"]
        total = None
        for tile in range(tiles):
            part = slice(tile * BLOCK, (tile + 1) * BLOCK)
            weight = jnp.exp2(scores[i, part, :] * exp_scale - top)
            weights[part, i * rows : (i + 1) * rows] = weight.astype(low)
            add = fold(weight, jnp.sum)
            total = add if total is None else total + add
        state[i]["inverse"] = 1.0 / jnp.sum(total, axis=0, keepdims=True)

    def attend(i):
        columns = slice(i * HEAD_DIM, (i + 1) * HEAD_DIM)
        inverse = state[i]["inverse"]
        grad_t = (take(own_g, peer_g, i).T.astype(jnp.float32) * inverse).astype(low)
        out_t = dot(values_t[...], weights[:, i * rows : (i + 1) * rows]) * inverse
        delta = -jnp.sum(out_t * grad_t.astype(jnp.float32), axis=0, keepdims=True)
        out = out_t.astype(low).T
        own_o[:, columns] = out[:half]
        peer_out[:, columns] = out[half:]
        first = delta.astype(low).astype(jnp.float32)
        second = (delta - first).astype(low).astype(jnp.float32)
        third = delta - first - second
        line = lax.broadcasted_iota(jnp.int32, (HEAD_DIM, rows), 0)
        extra = jnp.where(
            line == 0, first, jnp.where(line == 1, second, jnp.where(line == 2, third, 0.0))
        ).astype(low)
        state[i]["grad_t"] = grad_t
        state[i]["both_t"] = jnp.concatenate([grad_t, extra], axis=0)

    def flow(i):
        both_t = state[i]["both_t"]
        span = slice(i * rows, (i + 1) * rows)
        for tile in range(tiles):
            part = slice(tile * BLOCK, (tile + 1) * BLOCK)
            got = dot(values[part, :], both_t)
            flows[part, span] = (weights[part, span].astype(jnp.float32) * got).astype(low)

    def finish(i):
        columns = slice(i * HEAD_DIM, (i + 1) * HEAD_DIM)
        span = slice(i * rows, (i + 1) * rows)
        query_grad = (dot(keys_t[...], flows[:, span]) * score_scale).astype(low).T
        own_dq[:, columns] = query_grad[:half]
        start = (RATIO + i) * HEAD_DIM
        peer_out[:, start : start + HEAD_DIM] = query_grad[half:]

    stages = [score, soften, attend, flow, finish]
    for slot in range(per_step + len(stages) - 1):
        for lag, stage in reversed(list(enumerate(stages))):
            if 0 <= slot - lag < per_step:
                stage(slot - lag)
    queries = jnp.concatenate([take(own_q, peer_q, i) for i in range(per_step)], axis=0)
    grads_t = jnp.concatenate([state[i]["grad_t"] for i in range(per_step)], axis=1)
    value_acc[...] += dot(weights[...], grads_t, NT)
    key_acc[...] += dot(flows[...], queries)

    @pl.when(step == steps - 1)
    def _():
        for piece in range(2 * pieces):
            part = slice(piece * half, (piece + 1) * half)
            column = piece % 2 * 2 * HEAD_DIM
            out = grad_refs[piece // 2]
            out[:, column : column + HEAD_DIM] = (key_acc[part, :] * score_scale).astype(low)
            out[:, column + HEAD_DIM : column + 2 * HEAD_DIM] = value_acc[part, :].astype(low)
        if span:
            copy_columns(pieces, span, wide, where_ref[0] // 2, inputs_ref, grad_refs, 4 * HEAD_DIM)


def attention(me, core, own_mask, peer_mask, queries, peer_q, out_grad, peer_g, kv_pieces, group, inputs=None, span=()):
    tokens = queries.shape[1]
    blocks_here = tokens // BLOCK
    rows = 2 * tokens
    pieces = len(kv_pieces)
    per_step = RATIO
    steps = RATIO // per_step
    wide = per_step * HEAD_DIM
    where = jnp.stack([me, core]).astype(jnp.int32)

    def heads_in(g, h, where_ref, *_):
        return (0, 0, (where_ref[1] * (KV_HEADS // 2) + group) * steps + h)

    def fixed(g, h, *_):
        return (0, 0)

    wide_in = inputs.shape[2] // (lax.axis_size("dp") * pieces) if span else 0
    extra = [inputs] if span else []
    grad_cols = 4 * HEAD_DIM + wide_in * len(span)
    keys_all = pieces * rows
    out_cols = RATIO * HEAD_DIM
    result = pl.pallas_call(
        functools.partial(attention_kernel, pieces, blocks_here, steps, per_step, span, wide_in),
        grid_spec=pltpu.PrefetchScalarGridSpec(
            num_scalar_prefetch=3,
            grid=(1, steps),
            in_specs=[pl.BlockSpec(x.shape, lambda *_: (0, 0, 0)) for x in extra]
            + [pl.BlockSpec((1, tokens, wide), heads_in)] * 4
            + [pl.BlockSpec((tokens, 4 * HEAD_DIM), fixed)] * pieces,
            out_specs=[pl.BlockSpec((tokens, wide), fixed)] * 2
            + [pl.BlockSpec((tokens, 2 * wide), fixed)]
            + [pl.BlockSpec((tokens, grad_cols), fixed)] * pieces,
            scratch_shapes=[
                pltpu.VMEM((rows, HEAD_DIM), jnp.bfloat16),
                pltpu.VMEM((BLOCK, BLOCK), jnp.float32),
                pltpu.VMEM((keys_all, 2 * HEAD_DIM), jnp.bfloat16),
                pltpu.VMEM((keys_all, 2 * HEAD_DIM), jnp.bfloat16),
                pltpu.VMEM((HEAD_DIM, keys_all), jnp.bfloat16),
                pltpu.VMEM((HEAD_DIM, keys_all), jnp.bfloat16),
                pltpu.VMEM((keys_all, HEAD_DIM), jnp.float32),
                pltpu.VMEM((keys_all, HEAD_DIM), jnp.float32),
                pltpu.VMEM((per_step, keys_all, rows), jnp.float32),
                pltpu.VMEM((keys_all, per_step * rows), jnp.bfloat16),
                pltpu.VMEM((keys_all, per_step * rows), jnp.bfloat16),
            ],
        ),
        out_shape=[jax.ShapeDtypeStruct((tokens, out_cols), jnp.bfloat16)] * 2
        + [jax.ShapeDtypeStruct((tokens, 2 * out_cols), jnp.bfloat16)]
        + [jax.ShapeDtypeStruct((tokens, grad_cols), jnp.bfloat16)] * pieces,
        compiler_params=pltpu.CompilerParams(vmem_limit_bytes=56 * 1024 * 1024),
        cost_estimate=pl.CostEstimate(
            flops=(24 if span else 1) * RATIO * rows * keys_all * HEAD_DIM,
            transcendentals=RATIO * rows * keys_all,
            bytes_accessed=16 * tokens * out_cols,
        ),
        name="attention",
    )(where, own_mask, peer_mask, *extra, queries, peer_q, out_grad, peer_g, *kv_pieces)
    return list(result[:3]), list(result[3:])


def small_call(kernel, name, scalars, operands, out_shape, cost=2_000_000, scratch=(), streamed=False):
    whole = pl.BlockSpec(memory_space=pltpu.VMEM)
    return pl.pallas_call(
        kernel,
        grid=(1,) if streamed else (),
        in_specs=[pl.BlockSpec(memory_space=pltpu.SMEM)]
        + [pl.BlockSpec(x.shape, lambda i, n=x.ndim: (0,) * n) if streamed else whole for x in operands],
        out_specs=jax.tree.map(lambda _: whole, out_shape),
        out_shape=out_shape,
        scratch_shapes=scratch,
        compiler_params=pltpu.CompilerParams(vmem_limit_bytes=32 * 1024 * 1024),
        cost_estimate=pl.CostEstimate(flops=0, transcendentals=0, bytes_accessed=cost),
        name=name,
    )(scalars, *operands)


def turn_kernel(offset, scalar_ref, *refs):
    *parts, out = refs
    tokens = parts[0].shape[0]
    for i, part in enumerate(parts):
        out[:, i * tokens : (i + 1) * tokens] = part[:, offset:].T


def product_kernel(plan, scale, scalar_ref, own_low, own_high, peer_low, peer_high, *refs):
    *refs, whole = refs
    pieces = len(refs) - len(plan)
    grads, outs = refs[:pieces], refs[pieces:]
    own_grad = jnp.concatenate([g[:, : 2 * HEAD_DIM] for g in grads], axis=0)
    peer_grad = jnp.concatenate([g[:, 2 * HEAD_DIM :] for g in grads], axis=0)
    half = own_low.shape[0]
    for i, (own, peer) in enumerate(((own_low, peer_low), (own_high, peer_high))):
        got = dot(own[...], own_grad) + dot(peer[...], peer_grad)
        whole[i * half : i * half + own.shape[0], :] = got * scale
    for chunks, out in zip(plan, outs):
        size = out.shape[0] // len(chunks)
        for i, k in enumerate(chunks):
            start = pl.multiple_of(jnp.bitwise_xor(scalar_ref[0], k) * size, size)
            out[i * size : (i + 1) * size, :] = whole[pl.ds(start, size), :].astype(out.dtype)


def pack_kernel(span, scalar_ref, inputs_ref, front, *outs):
    wide = (outs[0].shape[1] - front.shape[1]) // len(span)
    copy_columns(len(outs), span, wide, scalar_ref[0], inputs_ref, outs, front.shape[1])
    for out in outs[1:]:
        out[:, : front.shape[1]] = front[...]


def columns_for(inputs, me, k, chips, span):
    tokens, width = inputs.shape[1:]
    wide = width // (lax.axis_size("dp") * chips)
    shaped = inputs[0].reshape(tokens, -1, chips, wide)[:, span[0] : span[-1] + 1]
    part = lax.dynamic_index_in_dim(shaped, (me // 2) ^ k, 2, keepdims=False)
    return part.reshape(tokens, wide * len(span))


def pack(inputs, front, me, chips, span):
    tokens = inputs.shape[1]
    wide = inputs.shape[2] // (lax.axis_size("dp") * chips)
    if wide % HEAD_DIM:
        return [
            jnp.concatenate([front, columns_for(inputs, me, k, chips, span)], axis=1)
            for k in range(chips)
        ]
    return small_call(
        functools.partial(pack_kernel, span),
        "pack",
        (me // 2).reshape(1).astype(jnp.int32),
        [inputs, front],
        [jax.ShapeDtypeStruct((tokens, front.shape[1] + wide * len(span)), jnp.bfloat16)] * chips,
        cost=1,
    )


def settle_kernel(starts, scalar_ref, *refs):
    *parts, keep, send = refs
    size = keep.shape[0]
    core = scalar_ref[0]
    count = len(parts) // 2
    for first, out in ((core * size, keep), ((1 - core) * size, send)):
        for j in range(2):
            total = None
            for ref, start in zip(parts[j * count : (j + 1) * count], starts):
                part = ref[pl.ds(pl.multiple_of(first + start, size), size), :].astype(jnp.float32)
                total = part if total is None else total + part
            out[:, j * 2 * HEAD_DIM : (j + 1) * 2 * HEAD_DIM] = total


def close_kernel(scalar_ref, keep, got, key_out, value_out):
    core = scalar_ref[0]
    for side, ref in ((core, keep), (1 - core, got)):
        for i in range(2):
            span = pl.ds(pl.multiple_of((2 * side + i) * HEAD_DIM, HEAD_DIM), HEAD_DIM)
            key_out[:, span] = ref[:, 2 * i * HEAD_DIM : (2 * i + 1) * HEAD_DIM]
            value_out[:, span] = ref[:, (2 * i + 1) * HEAD_DIM : (2 * i + 2) * HEAD_DIM]


def join_kernel(scalar_ref, own_o_a, own_o_b, own_dq_a, own_dq_b, got_a, got_b, out, query_grad, sem):
    core = scalar_ref[0]
    wide = own_o_a.shape[1]
    copies = []
    for j, (whole, own) in enumerate(((out, (own_o_a, own_o_b)), (query_grad, (own_dq_a, own_dq_b)))):
        for i in range(2):
            other = (got_a, got_b)[i].at[:, j * wide : (j + 1) * wide]
            for side, ref in ((core, own[i]), (1 - core, other)):
                span = pl.ds(pl.multiple_of((2 * side + i) * wide, wide), wide)
                copies.append(pltpu.make_async_copy(ref, whole.at[0, :, span], sem.at[len(copies)]))
    for copy in copies:
        copy.start()
    for copy in copies:
        copy.wait()


def join(core_scalar, parts, shape):
    return pl.pallas_call(
        join_kernel,
        in_specs=[pl.BlockSpec(memory_space=pltpu.SMEM)]
        + [pl.BlockSpec(memory_space=pl.ANY)] * len(parts),
        out_specs=[pl.BlockSpec(memory_space=pltpu.VMEM)] * 2,
        out_shape=[jax.ShapeDtypeStruct(shape, jnp.bfloat16)] * 2,
        scratch_shapes=[pltpu.SemaphoreType.DMA((8,))],
        cost_estimate=pl.CostEstimate(flops=0, transcendentals=0, bytes_accessed=4_000_000),
        name="join",
    )(core_scalar, *parts)


def hold(values, *others):
    return lax.optimization_barrier((values, others))[0]


def body(inputs, queries, keys_values, out_grad, tree_mask):
    tokens = queries.shape[1]
    width = queries.shape[2]
    count = lax.axis_size("ctx")
    data_size = lax.axis_size("dp")
    me = lax.axis_index("ctx")
    data_me = lax.axis_index("dp")
    core = me % 2
    chips = count // 2
    hops = [2 * p for p in range(1, chips)]
    low, high = jnp.bfloat16, jnp.float32
    core_scalar = core.reshape(1).astype(jnp.int32)
    data_scalar = data_me.reshape(1).astype(jnp.int32)

    halves = [[], []]
    for source in (keys_values, swap(keys_values, "ctx", 1)):
        for j in range(2):
            both = source[0, :, j].reshape(tokens, 2, 2 * HEAD_DIM)
            both = lax.dynamic_index_in_dim(both, core, 1, keepdims=False)
            halves[0].append(both[:, :HEAD_DIM])
            halves[1].append(both[:, HEAD_DIM:])
    own_a, own_b = (jnp.concatenate(half, axis=1) for half in halves)
    pieces_a = [own_a] + [swap(own_a, "ctx", k) for k in hops]
    own_mask, queries_later, out_grad_later = hold((tree_mask[0], queries, out_grad), own_a)
    peer_mask = swap(own_mask, "ctx", 1)
    peer_q = swap(queries_later, "ctx", 1)
    peer_g = swap(out_grad_later, "ctx", 1)
    middle = data_size // 2
    whole_lanes = width // (data_size * chips) % HEAD_DIM == 0
    low_span, high_span = range(middle), range(middle, data_size)
    packed_b = pack(inputs, hold(own_b, peer_mask), me, chips, low_span)
    sends = hold(packed_b[1:], peer_q, peer_g)
    pieces_b = [own_b] + [swap(x, "ctx", k) for x, k in zip(sends, hops)]

    heads = (me, core, own_mask, peer_mask, queries, peer_q, out_grad, peer_g)
    if whole_lanes:
        outs_a, packed_a = attention(*heads, pieces_a, 0, inputs, high_span)
    else:
        outs_a, packed_a = attention(*heads, pieces_a, 0)
        packed_a = [
            jnp.concatenate([x, columns_for(inputs, me, k, chips, high_span)], axis=1)
            for k, x in enumerate(packed_a)
        ]
    back_a = [swap(x, "ctx", k) for x, k in zip(packed_a[1:], hops)]
    got_a = swap(outs_a[2], "ctx", 1)
    pieces_b = hold(pieces_b, outs_a[2])

    def turn(parts, streamed):
        return small_call(
            functools.partial(turn_kernel, 4 * HEAD_DIM),
            "turn",
            core_scalar,
            parts,
            jax.ShapeDtypeStruct((parts[0].shape[1] - 4 * HEAD_DIM, chips * tokens), low),
            cost=1,
            streamed=streamed,
        )

    own_low = turn(list(packed_b[:1]) + list(pieces_b[1:]), True)
    peer_low = swap(own_low, "ctx", 1)
    outs_b, grads_b = attention(*heads, pieces_b, 1)
    grads_b, back_a, got_a, peer_low = lax.optimization_barrier((grads_b, back_a, got_a, peer_low))
    back_b = [swap(x, "ctx", k) for x, k in zip(grads_b[1:], hops)]
    own_high = turn(list(packed_a[:1]) + list(back_a), False)
    peer_high = swap(own_high, "ctx", 1)

    def owned(mine, back):
        total = mine.astype(high)
        for x in back:
            total = total + x.astype(high)
        return total.astype(low)

    def gathered(total):
        return [total] + [swap(total, "ctx", k) for k in hops]

    scale = 1.0 / math.sqrt(tokens * count * data_size)
    rows_out = width // (data_size * count)
    size = 2 * rows_out
    pairwise = data_size == 4
    plan = [[0], [2], [3, 1]] if pairwise else [[k] for k in range(data_size)]
    kinds = [high, high, low] if pairwise else [high] + [low] * (data_size - 1)

    def product(grads):
        return small_call(
            functools.partial(product_kernel, plan, scale),
            "product",
            data_scalar,
            [own_low, own_high, peer_low, peer_high] + grads,
            [
                jax.ShapeDtypeStruct((size * len(chunks), 2 * HEAD_DIM), kind)
                for chunks, kind in zip(plan, kinds)
            ],
            scratch=[pltpu.VMEM((size * data_size, 2 * HEAD_DIM), high)],
        )

    folded = 4 * HEAD_DIM
    all_a = gathered(owned(packed_a[0][:, :folded], [x[:, :folded] for x in back_a]))
    all_b = gathered(owned(grads_b[0], back_b))
    chunks_a = product(all_a)
    all_b = hold(all_b, chunks_a)
    chunks_b = product(all_b)
    if pairwise:
        near_a = swap(chunks_a[2], "dp", 1)
        cross_a = (chunks_a[1] + near_a[:size].astype(high)).astype(low)
        near_b = swap(hold(chunks_b[2], cross_a), "dp", 1)
        cross_b = (chunks_b[1] + near_b[:size].astype(high)).astype(low)
        arrived = [[near_a, swap(cross_a, "dp", 2)], [near_b, swap(cross_b, "dp", 2)]]
        starts = [0, size, 0]
    else:
        arrived = [[swap(x[k], "dp", k) for k in range(1, data_size)] for x in (chunks_a, chunks_b)]
        cross_b = chunks_b[0]
        starts = [0] * data_size
    got_b = swap(hold(outs_b[2], chunks_b), "ctx", 1)
    parts = [outs_a[0], outs_b[0], outs_a[1], outs_b[1], got_a, got_b]
    attn_out, query_grad = join(core_scalar, hold(parts, cross_b), queries.shape)
    arrived, attn_out, query_grad = lax.optimization_barrier((arrived, attn_out, query_grad))
    kept, sent = small_call(
        functools.partial(settle_kernel, starts),
        "settle",
        core_scalar,
        [chunks_a[0]] + arrived[0] + [chunks_b[0]] + arrived[1],
        [jax.ShapeDtypeStruct((rows_out, 4 * HEAD_DIM), high)] * 2,
    )
    key_out, value_out = small_call(
        close_kernel,
        "close",
        core_scalar,
        [kept, swap(sent, "ctx", 1)],
        [jax.ShapeDtypeStruct((rows_out, KV_HEADS * HEAD_DIM), high)] * 2,
    )
    return attn_out, query_grad, key_out, value_out


def solution(mesh):
    in_specs = (
        P("dp", "ctx", None),
        P("dp", "ctx", None),
        P("dp", "ctx", None, None),
        P("dp", "ctx", None),
        P("dp", "ctx", None),
    )
    out_specs = (
        P("dp", "ctx", None),
        P("dp", "ctx", None),
        P(("dp", "ctx"), None),
        P(("dp", "ctx"), None),
    )
    return jax.shard_map(body, mesh=mesh, in_specs=in_specs, out_specs=out_specs, check_vma=False)
```

time: 120 us -> 94.6 us (0.79)
  the two profiles are of different devices: /device:TPU:21 before, /device:TPU:0 now
where the time goes in v2:
time: 94.6 us; the launch traced here: 94.1 us
  starting transfers between devices  31.6 us (33%)
  Pallas kernels  30.2 us (32%)
  waiting for transfers between devices  23 us (24%)
  local copies, waits for them, and re-layouts  5.87 us (6%)
  other arithmetic  2.37 us (3%)
  between operations  1.02 us (1%)
    ppermute x31, starting transfers between devices, swap(): return lax.ppermute(value, axis, pairs)  31.6 us
    pallas_call x2, Pallas kernels, attention(): pl.pallas_call(functools.partial(attention_kernel, pieces, blocks_here, s...  24.4 us
    ppermute x31, waiting for transfers between devices, swap(): return lax.ppermute(value, axis, pairs)  23 us
    unnamed x41, local copies, waits for them, and re-layouts  3.75 us
    pallas_call x7, Pallas kernels, small_call(): pl.pallas_call(kernel, grid=(1,) if streamed else (), in_specs=[pl.BlockS...  2.93 us
    pallas_call x1, Pallas kernels, join(): pl.pallas_call(join_kernel, in_specs=[pl.BlockSpec(memory_space=pltpu.SME...  2.88 us
  transfers between devices with their start and end apart: 31, of which 10 were waited for; matrix products, arithmetic and copies ran while one was open for 3% of the time, Pallas kernels for 31%

profile of v2, /device:TPU:0, one launch (start us, length us, event | category | flops | bytes accessed | tf_op | source)
XLA Modules:
  0.0 94.1 jit_solution(15018460441432655670)
XLA Ops:
  0.6 1.2 %copy.13 = bf16[1,128,2,512]{1,3,2,0:T(8,128)(2,1)S(1)} copy(bf16[1,128,2,512]{3,2,1,0:T(2,128)(2,1)} %param.7) | data formatting | bytes 524288 | tf_op args[2]
  3.6 1.0 %fusion.1 = (bf16[1,128,1,512]{1,3,2,0:T(8,128)(2,1)S(1)}, bf16[1,128,1,512]{1,3,2,0:T(8,128)(2,1)S(1)}) fusion(bf16[1,128,2,512]{1,3,2,0:T(8,128)(2,1)} %collective-permute-done), kind=kLoop, calls=%fused_computation.12 | loop fusion | bytes 524288 | tf_op jit(solution)/shard_map/slice | solution.py:389
  6.2 3.8 %collective-permute-start.9 = (bf16[128,512]{1,0:T(8,128)(2,1)S(1)}, bf16[128,512]{1,0:T(8,128)(2,1)}, u32[]{:S(2)}, u32[]{:S(2)}) collective-permute-start(bf16[128,512]{1,0:T(8,128)(2,1)S(1)} %pad_maximum_fusion.1.refs_5_), channel_id=1, source_target_pairs={{0,6},{1,7},{2,4},{3,5},{4,2},{5,3},{6,0},{7,1},{8,14},{9,15},{10,... | collective-permute-start | bytes 393224 | tf_op jit(solution)/shard_map/ppermute | solution.py:22
  10.6 1.1 %collective-permute-done.1.peer_mask = s32[1,8]{1,0:T(1,128)S(1)} collective-permute-done((s32[1,8]{1,0:T(1,128)S(1)}, s32[1,8]{1,0:T(1,128)S(1)}, u32[]{:S(2)}, u32[]{:S(2)}) %collective-permute-start.1) | collective-permute-done | bytes 64 | tf_op jit(solution)/shard_map/ppermute | solution.py:22
  11.7 1.0 %collective-permute-start.7 = (bf16[128,512]{1,0:T(8,128)(2,1)S(1)}, bf16[128,512]{1,0:T(8,128)(2,1)}, u32[]{:S(2)}, u32[]{:S(2)}) collective-permute-start(bf16[128,512]{1,0:T(8,128)(2,1)S(1)} %pad_maximum_fusion.1.refs_5_), channel_id=1, source_target_pairs={{0,2},{1,3},{2,0},{3,1},{4,6},{5,7},{6,4},{7,5},{8,10},{9,11},{10,... | collective-permute-start | bytes 393224 | tf_op jit(solution)/shard_map/ppermute | solution.py:22
  14.8 1.0 %collective-permute-start.4 = (bf16[128,1024]{1,0:T(8,128)(2,1)S(1)}, bf16[128,1024]{1,0:T(8,128)(2,1)S(1)}, u32[]{:S(2)}, u32[]{:S(2)}) collective-permute-start(bf16[128,1024]{1,0:T(8,128)(2,1)S(1)} %get-tuple-element.80), channel_id=1, source_target_pairs={{0,2},{1,3},{2,0},{3,1},{4,6},{5,7},{6,4},{7,5},{8,10},{9,11},{10,... | collective-permute-start | bytes 786440 | tf_op jit(solution)/shard_map/ppermute | solution.py:22
  15.8 1.5 %collective-permute-start.5 = (bf16[128,1024]{1,0:T(8,128)(2,1)S(1)}, bf16[128,1024]{1,0:T(8,128)(2,1)S(1)}, u32[]{:S(2)}, u32[]{:S(2)}) collective-permute-start(bf16[128,1024]{1,0:T(8,128)(2,1)S(1)} %get-tuple-element.81), channel_id=1, source_target_pairs={{0,4},{1,5},{2,6},{3,7},{4,0},{5,1},{6,2},{7,3},{8,12},{9,13},{10,... | collective-permute-start | bytes 786440 | tf_op jit(solution)/shard_map/ppermute | solution.py:22
  17.3 1.0 %collective-permute-start.6 = (bf16[128,1024]{1,0:T(8,128)(2,1)S(1)}, bf16[128,1024]{1,0:T(8,128)(2,1)S(1)}, u32[]{:S(2)}, u32[]{:S(2)}) collective-permute-start(bf16[128,1024]{1,0:T(8,128)(2,1)S(1)} %get-tuple-element.82), channel_id=1, source_target_pairs={{0,6},{1,7},{2,4},{3,5},{4,2},{5,3},{6,0},{7,1},{8,14},{9,15},{10,... | collective-permute-start | bytes 786440 | tf_op jit(solution)/shard_map/ppermute | solution.py:22
  18.3 12.4 %attention.2 = (bf16[128,1024]{1,0:T(8,128)(2,1)}, bf16[128,1024]{1,0:T(8,128)(2,1)}, bf16[128,2048]{1,0:T(8,128)(2,1)}, bf16[128,1024]{1,0:T(8,128)(2,1)}, bf16...) custom-call(s32[2]{0:T(128)} %pad_add_fusion.where_ref, s32[1,8]{1,0:T(1,128)} %bitcast.21, ...), custom_call_target="tpu_custom_call" | custom-call | flops 6442450944 | bytes 2097152 | tf_op jit(solution)/shard_map/attention/pallas_call | solution.py:204
  32.1 1.0 %collective-permute-start.10 = (bf16[128,1024]{1,0:T(8,128)(2,1)S(1)}, bf16[128,1024]{1,0:T(8,128)(2,1)S(1)}, u32[]{:S(2)}, u32[]{:S(2)}) collective-permute-start(bf16[128,1024]{1,0:T(8,128)(2,1)S(1)} %copy-done.17), channel_id=1, source_target_pairs={{0,2},{1,3},{2,0},{3,1},{4,6},{5,7},{6,4},{7,5},{8,10},{9,11},{10,... | collective-permute-start | bytes 786440 | tf_op jit(solution)/shard_map/ppermute | solution.py:22
  33.1 1.5 %collective-permute-start.11 = (bf16[128,1024]{1,0:T(8,128)(2,1)S(1)}, bf16[128,1024]{1,0:T(8,128)(2,1)S(1)}, u32[]{:S(2)}, u32[]{:S(2)}) collective-permute-start(bf16[128,1024]{1,0:T(8,128)(2,1)S(1)} %copy-done.16), channel_id=1, source_target_pairs={{0,4},{1,5},{2,6},{3,7},{4,0},{5,1},{6,2},{7,3},{8,12},{9,13},{10,... | collective-permute-start | bytes 786440 | tf_op jit(solution)/shard_map/ppermute | solution.py:22
  34.6 1.0 %collective-permute-start.12 = (bf16[128,1024]{1,0:T(8,128)(2,1)S(1)}, bf16[128,1024]{1,0:T(8,128)(2,1)S(1)}, u32[]{:S(2)}, u32[]{:S(2)}) collective-permute-start(bf16[128,1024]{1,0:T(8,128)(2,1)S(1)} %copy-done.15), channel_id=1, source_target_pairs={{0,6},{1,7},{2,4},{3,5},{4,2},{5,3},{6,0},{7,1},{8,14},{9,15},{10,... | collective-permute-start | bytes 786440 | tf_op jit(solution)/shard_map/ppermute | solution.py:22
  35.5 12.0 %attention.3 = (bf16[128,1024]{1,0:T(8,128)(2,1)}, bf16[128,1024]{1,0:T(8,128)(2,1)}, bf16[128,2048]{1,0:T(8,128)(2,1)}, bf16[128,512]{1,0:T(8,128)(2,1)}, bf16[...) custom-call(s32[2]{0:T(128)} %pad_add_fusion.where_ref, s32[1,8]{1,0:T(1,128)} %bitcast.22, ...), custom_call_target="tpu_custom_call" | custom-call | flops 268435456 | bytes 2097152 | tf_op jit(solution)/shard_map/attention/pallas_call | solution.py:204
  48.5 2.0 %collective-permute-start.18 = (bf16[128,512]{1,0:T(8,128)(2,1)S(1)}, bf16[128,512]{1,0:T(8,128)(2,1)S(1)}, u32[]{:S(2)}, u32[]{:S(2)}) collective-permute-start(bf16[128,512]{1,0:T(8,128)(2,1)S(1)} %add_convert_fusion.3.refs_0_), channel_id=1, source_target_pairs={{0,6},{1,7},{2,4},{3,5},{4,2},{5,3},{6,0},{7,1},{8,14},{9,15},{10,... | collective-permute-start | bytes 393224 | tf_op jit(solution)/shard_map/ppermute | solution.py:22
  51.0 1.0 %collective-permute-start.16 = (bf16[128,512]{1,0:T(8,128)(2,1)S(1)}, bf16[128,512]{1,0:T(8,128)(2,1)S(1)}, u32[]{:S(2)}, u32[]{:S(2)}) collective-permute-start(bf16[128,512]{1,0:T(8,128)(2,1)S(1)} %add_convert_fusion.3.refs_0_), channel_id=1, source_target_pairs={{0,2},{1,3},{2,0},{3,1},{4,6},{5,7},{6,4},{7,5},{8,10},{9,11},{10,... | collective-permute-start | bytes 393224 | tf_op jit(solution)/shard_map/ppermute | solution.py:22
  52.0 1.0 %collective-permute-start.21 = (bf16[128,512]{1,0:T(8,128)(2,1)}, bf16[128,512]{1,0:T(8,128)(2,1)S(1)}, u32[]{:S(2)}, u32[]{:S(2)}) collective-permute-start(bf16[128,512]{1,0:T(8,128)(2,1)} %get-tuple-element.103), channel_id=1, source_target_pairs={{0,2},{1,3},{2,0},{3,1},{4,6},{5,7},{6,4},{7,5},{8,10},{9,11},{10,... | collective-permute-start | bytes 393224 | tf_op jit(solution)/shard_map/ppermute | solution.py:22
  53.0 2.7 %collective-permute-done.18.refs_3_ = bf16[128,512]{1,0:T(8,128)(2,1)S(1)} collective-permute-done((bf16[128,512]{1,0:T(8,128)(2,1)S(1)}, bf16[128,512]{1,0:T(8,128)(2,1)S(1)}, u32[]{:S(2)}, u32[]{:S(2)}) %collective-permute-start.18) | collective-permute-done | bytes 131104 | tf_op jit(solution)/shard_map/ppermute | solution.py:22
  55.8 1.6 %collective-permute-start.22 = (bf16[128,512]{1,0:T(8,128)(2,1)S(1)}, bf16[128,512]{1,0:T(8,128)(2,1)S(1)}, u32[]{:S(2)}, u32[]{:S(2)}) collective-permute-start(bf16[128,512]{1,0:T(8,128)(2,1)S(1)} %copy-done.19), channel_id=1, source_target_pairs={{0,4},{1,5},{2,6},{3,7},{4,0},{5,1},{6,2},{7,3},{8,12},{9,13},{10,... | collective-permute-start | bytes 393224 | tf_op jit(solution)/shard_map/ppermute | solution.py:22
  58.2 1.8 %collective-permute-start.23 = (bf16[128,512]{1,0:T(8,128)(2,1)S(1)}, bf16[128,512]{1,0:T(8,128)(2,1)S(1)}, u32[]{:S(2)}, u32[]{:S(2)}) collective-permute-start(bf16[128,512]{1,0:T(8,128)(2,1)S(1)} %copy-done.18), channel_id=1, source_target_pairs={{0,6},{1,7},{2,4},{3,5},{4,2},{5,3},{6,0},{7,1},{8,14},{9,15},{10,... | collective-permute-start | bytes 393224 | tf_op jit(solution)/shard_map/ppermute | solution.py:22
  60.9 1.6 %collective-permute-start.19 = (bf16[512,256]{1,0:T(8,128)(2,1)S(1)}, bf16[512,256]{1,0:T(8,128)(2,1)S(1)}, u32[]{:S(2)}, u32[]{:S(2)}) collective-permute-start(bf16[512,256]{1,0:T(8,128)(2,1)S(1)} %get-tuple-element.100), channel_id=1, source_target_pairs={{0,8},{8,0},{16,24},{24,16},{1,9},{9,1},{17,25},{25,17},{2,10},{10... | collective-permute-start | bytes 786440 | tf_op jit(solution)/shard_map/ppermute | solution.py:22
  62.5 2.0 %collective-permute-done.23 = bf16[128,512]{1,0:T(8,128)(2,1)S(1)} collective-permute-done((bf16[128,512]{1,0:T(8,128)(2,1)S(1)}, bf16[128,512]{1,0:T(8,128)(2,1)S(1)}, u32[]{:S(2)}, u32[]{:S(2)}) %collective-permute-start.23) | collective-permute-done | bytes 131104 | tf_op jit(solution)/shard_map/ppermute | solution.py:22
  64.6 1.6 %collective-permute-start.26 = (bf16[128,512]{1,0:T(8,128)(2,1)S(1)}, bf16[128,512]{1,0:T(8,128)(2,1)S(1)}, u32[]{:S(2)}, u32[]{:S(2)}) collective-permute-start(bf16[128,512]{1,0:T(8,128)(2,1)S(1)} %add_convert_fusion.1.refs_0_), channel_id=1, source_target_pairs={{0,6},{1,7},{2,4},{3,5},{4,2},{5,3},{6,0},{7,1},{8,14},{9,15},{10,... | collective-permute-start | bytes 393224 | tf_op jit(solution)/shard_map/ppermute | solution.py:22
  66.1 1.0 %collective-permute-start.25 = (bf16[128,512]{1,0:T(8,128)(2,1)S(1)}, bf16[128,512]{1,0:T(8,128)(2,1)S(1)}, u32[]{:S(2)}, u32[]{:S(2)}) collective-permute-start(bf16[128,512]{1,0:T(8,128)(2,1)S(1)} %add_convert_fusion.1.refs_0_), channel_id=1, source_target_pairs={{0,4},{1,5},{2,6},{3,7},{4,0},{5,1},{6,2},{7,3},{8,12},{9,13},{10,... | collective-permute-start | bytes 393224 | tf_op jit(solution)/shard_map/ppermute | solution.py:22
  67.1 1.0 %collective-permute-start.24 = (bf16[128,512]{1,0:T(8,128)(2,1)S(1)}, bf16[128,512]{1,0:T(8,128)(2,1)S(1)}, u32[]{:S(2)}, u32[]{:S(2)}) collective-permute-start(bf16[128,512]{1,0:T(8,128)(2,1)S(1)} %add_convert_fusion.1.refs_0_), channel_id=1, source_target_pairs={{0,2},{1,3},{2,0},{3,1},{4,6},{5,7},{6,4},{7,5},{8,10},{9,11},{10,... | collective-permute-start | bytes 393224 | tf_op jit(solution)/shard_map/ppermute | solution.py:22
  68.1 3.4 %collective-permute-done.26.refs_3_ = bf16[128,512]{1,0:T(8,128)(2,1)S(1)} collective-permute-done((bf16[128,512]{1,0:T(8,128)(2,1)S(1)}, bf16[128,512]{1,0:T(8,128)(2,1)S(1)}, u32[]{:S(2)}, u32[]{:S(2)}) %collective-permute-start.26) | collective-permute-done | bytes 131104 | tf_op jit(solution)/shard_map/ppermute | solution.py:22
  71.6 1.2 %collective-permute-done.25.refs_2_ = bf16[128,512]{1,0:T(8,128)(2,1)S(1)} collective-permute-done((bf16[128,512]{1,0:T(8,128)(2,1)S(1)}, bf16[128,512]{1,0:T(8,128)(2,1)S(1)}, u32[]{:S(2)}, u32[]{:S(2)}) %collective-permute-start.25) | collective-permute-done | bytes 131104 | tf_op jit(solution)/shard_map/ppermute | solution.py:22
  73.7 1.6 %collective-permute-start.27 = (bf16[512,256]{1,0:T(8,128)(2,1)S(1)}, bf16[512,256]{1,0:T(8,128)(2,1)S(1)}, u32[]{:S(2)}, u32[]{:S(2)}) collective-permute-start(bf16[512,256]{1,0:T(8,128)(2,1)S(1)} %get-tuple-element.112), channel_id=1, source_target_pairs={{0,8},{8,0},{16,24},{24,16},{1,9},{9,1},{17,25},{25,17},{2,10},{10... | collective-permute-start | bytes 786440 | tf_op jit(solution)/shard_map/ppermute | solution.py:22
  75.3 2.6 %collective-permute-start.20 = (bf16[256,256]{1,0:T(8,128)(2,1)S(1)}, bf16[256,256]{1,0:T(8,128)(2,1)S(1)}, u32[]{:S(2)}, u32[]{:S(2)}) collective-permute-start(bf16[256,256]{1,0:T(8,128)(2,1)S(1)} %add_convert_fusion.2), channel_id=1, source_target_pairs={{0,16},{8,24},{16,0},{24,8},{1,17},{9,25},{17,1},{25,9},{2,18},{10... | collective-permute-start | bytes 393224 | tf_op jit(solution)/shard_map/ppermute | solution.py:22
  77.9 7.1 %collective-permute-done.27.refs_4_ = bf16[512,256]{1,0:T(8,128)(2,1)S(1)} collective-permute-done((bf16[512,256]{1,0:T(8,128)(2,1)S(1)}, bf16[512,256]{1,0:T(8,128)(2,1)S(1)}, u32[]{:S(2)}, u32[]{:S(2)}) %collective-permute-start.27) | collective-permute-done | bytes 262176 | tf_op jit(solution)/shard_map/ppermute | solution.py:22
  86.1 2.9 %join.1 = (bf16[1,128,4096]{2,1,0:T(8,128)(2,1)}, bf16[1,128,4096]{2,1,0:T(8,128)(2,1)}) custom-call(s32[1]{0:T(128)} %bitcast.1.scalar_ref, bf16[128,1024]{1,0:T(8,128)(2,1)} %get-tuple-element.122.own_o_a, bf16[128,1024]{1,0:T(8,128)(2,1)} %get-tuple-element.123.own_o_b, bf16[128,1024]{1,0:T(8,128)(2,1)} %get-tuple-element.124.own_dq_a, ...), custom_call_target="tpu_custom_call" | custom-call | bytes 4000000 | tf_op jit(solution)/shard_map/join/pallas_call | solution.py:356
  89.0 2.6 %collective-permute-done.28.refs_5_ = bf16[256,256]{1,0:T(8,128)(2,1)S(1)} collective-permute-done((bf16[256,256]{1,0:T(8,128)(2,1)S(1)}, bf16[256,256]{1,0:T(8,128)(2,1)S(1)}, u32[]{:S(2)}, u32[]{:S(2)}) %collective-permute-start.28) | collective-permute-done | bytes 131104 | tf_op jit(solution)/shard_map/ppermute | solution.py:22
  91.7 1.5 %collective-permute-done.30.got = f32[128,512]{1,0:T(8,128)S(1)} collective-permute-done((f32[128,512]{1,0:T(8,128)S(1)}, f32[128,512]{1,0:T(8,128)S(1)}, u32[]{:S(2)}, u32[]{:S(2)}) %collective-permute-start.30) | collective-permute-done | bytes 262176 | tf_op jit(solution)/shard_map/ppermute | solution.py:22
  (100 shorter events, 13.3 us)
Async XLA Ops:
  1.8 1.8 %collective-permute-start = (bf16[1,128,2,512]{1,3,2,0:T(8,128)(2,1)S(1)}, bf16[1,128,2,512]{1,3,2,0:T(8,128)(2,1)}, u32[]{:S(2)}, u32[]{:S(2)}) collective-permute-start(bf16[1,128,2,512]{1,3,2,0:T(8,128)(2,1)S(1)} %copy.13), channel_id=1, source_target_pairs={{0,1},{1,0},{2,3},{3,2},{4,5},{5,4},{6,7},{7,6},{8,9},{9,8},{10,11... | collective-permute-start | bytes 786440 | tf_op jit(solution)/shard_map/ppermute | solution.py:22
  5.7 9.1 %collective-permute-start.2 = (bf16[1,128,4096]{2,1,0:T(8,128)(2,1)S(1)}, bf16[1,128,4096]{2,1,0:T(8,128)(2,1)}, u32[]{:S(2)}, u32[]{:S(2)}) collective-permute-start(bf16[1,128,4096]{2,1,0:T(8,128)(2,1)S(1)} %copy-done.6), channel_id=1, source_target_pairs={{0,1},{1,0},{2,3},{3,2},{4,5},{5,4},{6,7},{7,6},{8,9},{9,8},{10,11... | collective-permute-start | bytes 3145736 | tf_op jit(solution)/shard_map/ppermute | solution.py:22
  6.1 8.7 %collective-permute-start.3 = (bf16[1,128,4096]{2,1,0:T(8,128)(2,1)S(1)}, bf16[1,128,4096]{2,1,0:T(8,128)(2,1)}, u32[]{:S(2)}, u32[]{:S(2)}) collective-permute-start(bf16[1,128,4096]{2,1,0:T(8,128)(2,1)S(1)} %copy-done.7), channel_id=1, source_target_pairs={{0,1},{1,0},{2,3},{3,2},{4,5},{5,4},{6,7},{7,6},{8,9},{9,8},{10,11... | collective-permute-start | bytes 3145736 | tf_op jit(solution)/shard_map/ppermute | solution.py:22
  6.2 11.1 %collective-permute-start.9 = (bf16[128,512]{1,0:T(8,128)(2,1)S(1)}, bf16[128,512]{1,0:T(8,128)(2,1)}, u32[]{:S(2)}, u32[]{:S(2)}) collective-permute-start(bf16[128,512]{1,0:T(8,128)(2,1)S(1)} %pad_maximum_fusion.1.refs_5_), channel_id=1, source_target_pairs={{0,6},{1,7},{2,4},{3,5},{4,2},{5,3},{6,0},{7,1},{8,14},{9,15},{10,... | collective-permute-start | bytes 393224 | tf_op jit(solution)/shard_map/ppermute | solution.py:22
  10.1 8.2 %collective-permute-start.8 = (bf16[128,512]{1,0:T(8,128)(2,1)S(1)}, bf16[128,512]{1,0:T(8,128)(2,1)}, u32[]{:S(2)}, u32[]{:S(2)}) collective-permute-start(bf16[128,512]{1,0:T(8,128)(2,1)S(1)} %pad_maximum_fusion.1.refs_5_), channel_id=1, source_target_pairs={{0,4},{1,5},{2,6},{3,7},{4,0},{5,1},{6,2},{7,3},{8,12},{9,13},{10,... | collective-permute-start | bytes 393224 | tf_op jit(solution)/shard_map/ppermute | solution.py:22
  10.6 1.1 %collective-permute-start.1 = (s32[1,8]{1,0:T(1,128)S(1)}, s32[1,8]{1,0:T(1,128)S(1)}, u32[]{:S(2)}, u32[]{:S(2)}) collective-permute-start(s32[1,8]{1,0:T(1,128)S(1)} %bitcast.23), channel_id=1, source_target_pairs={{0,1},{1,0},{2,3},{3,2},{4,5},{5,4},{6,7},{7,6},{8,9},{9,8},{10,11... | collective-permute-start | bytes 104 | tf_op jit(solution)/shard_map/ppermute | solution.py:22
  11.7 6.6 %collective-permute-start.7 = (bf16[128,512]{1,0:T(8,128)(2,1)S(1)}, bf16[128,512]{1,0:T(8,128)(2,1)}, u32[]{:S(2)}, u32[]{:S(2)}) collective-permute-start(bf16[128,512]{1,0:T(8,128)(2,1)S(1)} %pad_maximum_fusion.1.refs_5_), channel_id=1, source_target_pairs={{0,2},{1,3},{2,0},{3,1},{4,6},{5,7},{6,4},{7,5},{8,10},{9,11},{10,... | collective-permute-start | bytes 393224 | tf_op jit(solution)/shard_map/ppermute | solution.py:22
  14.8 15.9 %collective-permute-start.4 = (bf16[128,1024]{1,0:T(8,128)(2,1)S(1)}, bf16[128,1024]{1,0:T(8,128)(2,1)S(1)}, u32[]{:S(2)}, u32[]{:S(2)}) collective-permute-start(bf16[128,1024]{1,0:T(8,128)(2,1)S(1)} %get-tuple-element.80), channel_id=1, source_target_pairs={{0,2},{1,3},{2,0},{3,1},{4,6},{5,7},{6,4},{7,5},{8,10},{9,11},{10,... | collective-permute-start | bytes 786440 | tf_op jit(solution)/shard_map/ppermute | solution.py:22
  15.8 14.9 %collective-permute-start.5 = (bf16[128,1024]{1,0:T(8,128)(2,1)S(1)}, bf16[128,1024]{1,0:T(8,128)(2,1)S(1)}, u32[]{:S(2)}, u32[]{:S(2)}) collective-permute-start(bf16[128,1024]{1,0:T(8,128)(2,1)S(1)} %get-tuple-element.81), channel_id=1, source_target_pairs={{0,4},{1,5},{2,6},{3,7},{4,0},{5,1},{6,2},{7,3},{8,12},{9,13},{10,... | collective-permute-start | bytes 786440 | tf_op jit(solution)/shard_map/ppermute | solution.py:22
  17.3 13.4 %collective-permute-start.6 = (bf16[128,1024]{1,0:T(8,128)(2,1)S(1)}, bf16[128,1024]{1,0:T(8,128)(2,1)S(1)}, u32[]{:S(2)}, u32[]{:S(2)}) collective-permute-start(bf16[128,1024]{1,0:T(8,128)(2,1)S(1)} %get-tuple-element.82), channel_id=1, source_target_pairs={{0,6},{1,7},{2,4},{3,5},{4,2},{5,3},{6,0},{7,1},{8,14},{9,15},{10,... | collective-permute-start | bytes 786440 | tf_op jit(solution)/shard_map/ppermute | solution.py:22
  30.6 16.9 %collective-permute-start.13 = (bf16[128,2048]{1,0:T(8,128)(2,1)}, bf16[128,2048]{1,0:T(8,128)(2,1)S(1)}, u32[]{:S(2)}, u32[]{:S(2)}) collective-permute-start(bf16[128,2048]{1,0:T(8,128)(2,1)} %get-tuple-element.83), channel_id=1, source_target_pairs={{0,1},{1,0},{2,3},{3,2},{4,5},{5,4},{6,7},{7,6},{8,9},{9,8},{10,11... | collective-permute-start | bytes 1572872 | tf_op jit(solution)/shard_map/ppermute | solution.py:22
  31.5 16.0 %collective-permute-start.14 = (bf16[512,512]{1,0:T(8,128)(2,1)S(1)}, bf16[512,512]{1,0:T(8,128)(2,1)S(1)}, u32[]{:S(2)}, u32[]{:S(2)}) collective-permute-start(bf16[512,512]{1,0:T(8,128)(2,1)S(1)} %turn.2.own_low), channel_id=1, source_target_pairs={{0,1},{1,0},{2,3},{3,2},{4,5},{5,4},{6,7},{7,6},{8,9},{9,8},{10,11... | collective-permute-start | bytes 1572872 | tf_op jit(solution)/shard_map/ppermute | solution.py:22
  32.1 15.5 %collective-permute-start.10 = (bf16[128,1024]{1,0:T(8,128)(2,1)S(1)}, bf16[128,1024]{1,0:T(8,128)(2,1)S(1)}, u32[]{:S(2)}, u32[]{:S(2)}) collective-permute-start(bf16[128,1024]{1,0:T(8,128)(2,1)S(1)} %copy-done.17), channel_id=1, source_target_pairs={{0,2},{1,3},{2,0},{3,1},{4,6},{5,7},{6,4},{7,5},{8,10},{9,11},{10,... | collective-permute-start | bytes 786440 | tf_op jit(solution)/shard_map/ppermute | solution.py:22
  33.1 14.5 %collective-permute-start.11 = (bf16[128,1024]{1,0:T(8,128)(2,1)S(1)}, bf16[128,1024]{1,0:T(8,128)(2,1)S(1)}, u32[]{:S(2)}, u32[]{:S(2)}) collective-permute-start(bf16[128,1024]{1,0:T(8,128)(2,1)S(1)} %copy-done.16), channel_id=1, source_target_pairs={{0,4},{1,5},{2,6},{3,7},{4,0},{5,1},{6,2},{7,3},{8,12},{9,13},{10,... | collective-permute-start | bytes 786440 | tf_op jit(solution)/shard_map/ppermute | solution.py:22
  34.6 13.0 %copy-start.5 = (bf16[128,1024]{1,0:T(8,128)(2,1)S(1)}, bf16[128,1024]{1,0:T(8,128)(2,1)}, u32[]{:S(2)}) copy-start(bf16[128,1024]{1,0:T(8,128)(2,1)} %get-tuple-element.87.refs_0_) | copy-start | bytes 786436
  34.6 13.0 %collective-permute-start.12 = (bf16[128,1024]{1,0:T(8,128)(2,1)S(1)}, bf16[128,1024]{1,0:T(8,128)(2,1)S(1)}, u32[]{:S(2)}, u32[]{:S(2)}) collective-permute-start(bf16[128,1024]{1,0:T(8,128)(2,1)S(1)} %copy-done.15), channel_id=1, source_target_pairs={{0,6},{1,7},{2,4},{3,5},{4,2},{5,3},{6,0},{7,1},{8,14},{9,15},{10,... | collective-permute-start | bytes 786440 | tf_op jit(solution)/shard_map/ppermute | solution.py:22
  48.4 11.7 %collective-permute-start.15 = (bf16[512,512]{1,0:T(8,128)(2,1)S(1)}, bf16[512,512]{1,0:T(8,128)(2,1)S(1)}, u32[]{:S(2)}, u32[]{:S(2)}) collective-permute-start(bf16[512,512]{1,0:T(8,128)(2,1)S(1)} %turn.3.own_high), channel_id=1, source_target_pairs={{0,1},{1,0},{2,3},{3,2},{4,5},{5,4},{6,7},{7,6},{8,9},{9,8},{10,11... | collective-permute-start | bytes 1572872 | tf_op jit(solution)/shard_map/ppermute | solution.py:22
  48.5 7.3 %collective-permute-start.18 = (bf16[128,512]{1,0:T(8,128)(2,1)S(1)}, bf16[128,512]{1,0:T(8,128)(2,1)S(1)}, u32[]{:S(2)}, u32[]{:S(2)}) collective-permute-start(bf16[128,512]{1,0:T(8,128)(2,1)S(1)} %add_convert_fusion.3.refs_0_), channel_id=1, source_target_pairs={{0,6},{1,7},{2,4},{3,5},{4,2},{5,3},{6,0},{7,1},{8,14},{9,15},{10,... | collective-permute-start | bytes 393224 | tf_op jit(solution)/shard_map/ppermute | solution.py:22
  50.5 7.7 %collective-permute-start.17 = (bf16[128,512]{1,0:T(8,128)(2,1)S(1)}, bf16[128,512]{1,0:T(8,128)(2,1)S(1)}, u32[]{:S(2)}, u32[]{:S(2)}) collective-permute-start(bf16[128,512]{1,0:T(8,128)(2,1)S(1)} %add_convert_fusion.3.refs_0_), channel_id=1, source_target_pairs={{0,4},{1,5},{2,6},{3,7},{4,0},{5,1},{6,2},{7,3},{8,12},{9,13},{10,... | collective-permute-start | bytes 393224 | tf_op jit(solution)/shard_map/ppermute | solution.py:22
  51.0 9.1 %collective-permute-start.16 = (bf16[128,512]{1,0:T(8,128)(2,1)S(1)}, bf16[128,512]{1,0:T(8,128)(2,1)S(1)}, u32[]{:S(2)}, u32[]{:S(2)}) collective-permute-start(bf16[128,512]{1,0:T(8,128)(2,1)S(1)} %add_convert_fusion.3.refs_0_), channel_id=1, source_target_pairs={{0,2},{1,3},{2,0},{3,1},{4,6},{5,7},{6,4},{7,5},{8,10},{9,11},{10,... | collective-permute-start | bytes 393224 | tf_op jit(solution)/shard_map/ppermute | solution.py:22
  52.0 10.5 %collective-permute-start.21 = (bf16[128,512]{1,0:T(8,128)(2,1)}, bf16[128,512]{1,0:T(8,128)(2,1)S(1)}, u32[]{:S(2)}, u32[]{:S(2)}) collective-permute-start(bf16[128,512]{1,0:T(8,128)(2,1)} %get-tuple-element.103), channel_id=1, source_target_pairs={{0,2},{1,3},{2,0},{3,1},{4,6},{5,7},{6,4},{7,5},{8,10},{9,11},{10,... | collective-permute-start | bytes 393224 | tf_op jit(solution)/shard_map/ppermute | solution.py:22
  55.8 6.7 %collective-permute-start.22 = (bf16[128,512]{1,0:T(8,128)(2,1)S(1)}, bf16[128,512]{1,0:T(8,128)(2,1)S(1)}, u32[]{:S(2)}, u32[]{:S(2)}) collective-permute-start(bf16[128,512]{1,0:T(8,128)(2,1)S(1)} %copy-done.19), channel_id=1, source_target_pairs={{0,4},{1,5},{2,6},{3,7},{4,0},{5,1},{6,2},{7,3},{8,12},{9,13},{10,... | collective-permute-start | bytes 393224 | tf_op jit(solution)/shard_map/ppermute | solution.py:22
  58.2 6.3 %collective-permute-start.23 = (bf16[128,512]{1,0:T(8,128)(2,1)S(1)}, bf16[128,512]{1,0:T(8,128)(2,1)S(1)}, u32[]{:S(2)}, u32[]{:S(2)}) collective-permute-start(bf16[128,512]{1,0:T(8,128)(2,1)S(1)} %copy-done.18), channel_id=1, source_target_pairs={{0,6},{1,7},{2,4},{3,5},{4,2},{5,3},{6,0},{7,1},{8,14},{9,15},{10,... | collective-permute-start | bytes 393224 | tf_op jit(solution)/shard_map/ppermute | solution.py:22
  60.9 12.8 %collective-permute-start.19 = (bf16[512,256]{1,0:T(8,128)(2,1)S(1)}, bf16[512,256]{1,0:T(8,128)(2,1)S(1)}, u32[]{:S(2)}, u32[]{:S(2)}) collective-permute-start(bf16[512,256]{1,0:T(8,128)(2,1)S(1)} %get-tuple-element.100), channel_id=1, source_target_pairs={{0,8},{8,0},{16,24},{24,16},{1,9},{9,1},{17,25},{25,17},{2,10},{10... | collective-permute-start | bytes 786440 | tf_op jit(solution)/shard_map/ppermute | solution.py:22
  64.6 7.0 %collective-permute-start.26 = (bf16[128,512]{1,0:T(8,128)(2,1)S(1)}, bf16[128,512]{1,0:T(8,128)(2,1)S(1)}, u32[]{:S(2)}, u32[]{:S(2)}) collective-permute-start(bf16[128,512]{1,0:T(8,128)(2,1)S(1)} %add_convert_fusion.1.refs_0_), channel_id=1, source_target_pairs={{0,6},{1,7},{2,4},{3,5},{4,2},{5,3},{6,0},{7,1},{8,14},{9,15},{10,... | collective-permute-start | bytes 393224 | tf_op jit(solution)/shard_map/ppermute | solution.py:22
  66.1 6.7 %collective-permute-start.25 = (bf16[128,512]{1,0:T(8,128)(2,1)S(1)}, bf16[128,512]{1,0:T(8,128)(2,1)S(1)}, u32[]{:S(2)}, u32[]{:S(2)}) collective-permute-start(bf16[128,512]{1,0:T(8,128)(2,1)S(1)} %add_convert_fusion.1.refs_0_), channel_id=1, source_target_pairs={{0,4},{1,5},{2,6},{3,7},{4,0},{5,1},{6,2},{7,3},{8,12},{9,13},{10,... | collective-permute-start | bytes 393224 | tf_op jit(solution)/shard_map/ppermute | solution.py:22
  67.1 5.7 %collective-permute-start.24 = (bf16[128,512]{1,0:T(8,128)(2,1)S(1)}, bf16[128,512]{1,0:T(8,128)(2,1)S(1)}, u32[]{:S(2)}, u32[]{:S(2)}) collective-permute-start(bf16[128,512]{1,0:T(8,128)(2,1)S(1)} %add_convert_fusion.1.refs_0_), channel_id=1, source_target_pairs={{0,2},{1,3},{2,0},{3,1},{4,6},{5,7},{6,4},{7,5},{8,10},{9,11},{10,... | collective-permute-start | bytes 393224 | tf_op jit(solution)/shard_map/ppermute | solution.py:22
  73.7 11.4 %collective-permute-start.27 = (bf16[512,256]{1,0:T(8,128)(2,1)S(1)}, bf16[512,256]{1,0:T(8,128)(2,1)S(1)}, u32[]{:S(2)}, u32[]{:S(2)}) collective-permute-start(bf16[512,256]{1,0:T(8,128)(2,1)S(1)} %get-tuple-element.112), channel_id=1, source_target_pairs={{0,8},{8,0},{16,24},{24,16},{1,9},{9,1},{17,25},{25,17},{2,10},{10... | collective-permute-start | bytes 786440 | tf_op jit(solution)/shard_map/ppermute | solution.py:22
  75.3 10.0 %collective-permute-start.29 = (bf16[128,2048]{1,0:T(8,128)(2,1)S(1)}, bf16[128,2048]{1,0:T(8,128)(2,1)S(1)}, u32[]{:S(2)}, u32[]{:S(2)}) collective-permute-start(bf16[128,2048]{1,0:T(8,128)(2,1)S(1)} %copy-done.14), channel_id=1, source_target_pairs={{0,1},{1,0},{2,3},{3,2},{4,5},{5,4},{6,7},{7,6},{8,9},{9,8},{10,11... | collective-permute-start | bytes 1572872 | tf_op jit(solution)/shard_map/ppermute | solution.py:22
  75.3 13.7 %collective-permute-start.20 = (bf16[256,256]{1,0:T(8,128)(2,1)S(1)}, bf16[256,256]{1,0:T(8,128)(2,1)S(1)}, u32[]{:S(2)}, u32[]{:S(2)}) collective-permute-start(bf16[256,256]{1,0:T(8,128)(2,1)S(1)} %add_convert_fusion.2), channel_id=1, source_target_pairs={{0,16},{8,24},{16,0},{24,8},{1,17},{9,25},{17,1},{25,9},{2,18},{10... | collective-permute-start | bytes 393224 | tf_op jit(solution)/shard_map/ppermute | solution.py:22
  85.1 6.5 %collective-permute-start.28 = (bf16[256,256]{1,0:T(8,128)(2,1)S(1)}, bf16[256,256]{1,0:T(8,128)(2,1)S(1)}, u32[]{:S(2)}, u32[]{:S(2)}) collective-permute-start(bf16[256,256]{1,0:T(8,128)(2,1)S(1)} %add_convert_fusion), channel_id=1, source_target_pairs={{0,16},{8,24},{16,0},{24,8},{1,17},{9,25},{17,1},{25,9},{2,18},{10... | collective-permute-start | bytes 393224 | tf_op jit(solution)/shard_map/ppermute | solution.py:22
  91.7 1.6 %collective-permute-start.30 = (f32[128,512]{1,0:T(8,128)S(1)}, f32[128,512]{1,0:T(8,128)S(1)}, u32[]{:S(2)}, u32[]{:S(2)}) collective-permute-start(f32[128,512]{1,0:T(8,128)S(1)} %get-tuple-element.137), channel_id=1, source_target_pairs={{0,1},{1,0},{2,3},{3,2},{4,5},{5,4},{6,7},{7,6},{8,9},{9,8},{10,11... | collective-permute-start | bytes 786440 | tf_op jit(solution)/shard_map/ppermute | solution.py:22
  (19 other events, 71.2 us)

commit v3 on v2

--- a/solution.py
+++ b/solution.py
@@ -110,6 +110,7 @@
             scores[i, part, :] = got
             best = fold(got, jnp.max)
             top = best if top is None else jnp.maximum(top, best)
+            yield
         state[i]["top"] = jnp.max(top, axis=0, keepdims=True) * exp_scale
 
     def soften(i):
@@ -121,13 +122,21 @@
             weights[part, i * rows : (i + 1) * rows] = weight.astype(low)
             add = fold(weight, jnp.sum)
             total = add if total is None else total + add
+            yield
         state[i]["inverse"] = 1.0 / jnp.sum(total, axis=0, keepdims=True)
 
     def attend(i):
         columns = slice(i * HEAD_DIM, (i + 1) * HEAD_DIM)
         inverse = state[i]["inverse"]
         grad_t = (take(own_g, peer_g, i).T.astype(jnp.float32) * inverse).astype(low)
-        out_t = dot(values_t[...], weights[:, i * rows : (i + 1) * rows]) * inverse
+        out_t = None
+        wide_tile = 2 * BLOCK
+        for start in range(0, tiles * BLOCK, wide_tile):
+            part = slice(start, start + wide_tile)
+            got = dot(values_t[:, part], weights[part, i * rows : (i + 1) * rows])
+            out_t = got if out_t is None else out_t + got
+            yield
+        out_t = out_t * inverse
         delta = -jnp.sum(out_t * grad_t.astype(jnp.float32), axis=0, keepdims=True)
         out = out_t.astype(low).T
         own_o[:, columns] = out[:half]
@@ -141,6 +150,7 @@
         ).astype(low)
         state[i]["grad_t"] = grad_t
         state[i]["both_t"] = jnp.concatenate([grad_t, extra], axis=0)
+        yield
 
     def flow(i):
         both_t = state[i]["both_t"]
@@ -149,6 +159,7 @@
             part = slice(tile * BLOCK, (tile + 1) * BLOCK)
             got = dot(values[part, :], both_t)
             flows[part, span] = (weights[part, span].astype(jnp.float32) * got).astype(low)
+            yield
 
     def finish(i):
         columns = slice(i * HEAD_DIM, (i + 1) * HEAD_DIM)
@@ -157,16 +168,29 @@
         own_dq[:, columns] = query_grad[:half]
         start = (RATIO + i) * HEAD_DIM
         peer_out[:, start : start + HEAD_DIM] = query_grad[half:]
-
-    stages = [score, soften, attend, flow, finish]
+        yield
+
+    def gather(i):
+        if i % 2:
+            span = slice((i - 1) * rows, (i + 1) * rows)
+            grads_t = jnp.concatenate([state[j]["grad_t"] for j in (i - 1, i)], axis=1)
+            queries = jnp.concatenate([take(own_q, peer_q, j) for j in (i - 1, i)], axis=0)
+            for tile in range(tiles):
+                part = slice(tile * BLOCK, (tile + 1) * BLOCK)
+                value_acc[part, :] += dot(weights[part, span], grads_t, NT)
+                key_acc[part, :] += dot(flows[part, span], queries)
+                yield
+
+    stages = [score, soften, attend, flow, finish, gather]
     for slot in range(per_step + len(stages) - 1):
-        for lag, stage in reversed(list(enumerate(stages))):
-            if 0 <= slot - lag < per_step:
-                stage(slot - lag)
-    queries = jnp.concatenate([take(own_q, peer_q, i) for i in range(per_step)], axis=0)
-    grads_t = jnp.concatenate([state[i]["grad_t"] for i in range(per_step)], axis=1)
-    value_acc[...] += dot(weights[...], grads_t, NT)
-    key_acc[...] += dot(flows[...], queries)
+        active = [
+            stage(slot - lag)
+            for lag, stage in reversed(list(enumerate(stages)))
+            if 0 <= slot - lag < per_step
+        ]
+        done = object()
+        while active:
+            active = [work for work in active if next(work, done) is not done]
 
     @pl.when(step == steps - 1)
     def _():
@@ -229,7 +253,7 @@
         out_shape=[jax.ShapeDtypeStruct((tokens, out_cols), jnp.bfloat16)] * 2
         + [jax.ShapeDtypeStruct((tokens, 2 * out_cols), jnp.bfloat16)]
         + [jax.ShapeDtypeStruct((tokens, grad_cols), jnp.bfloat16)] * pieces,
-        compiler_params=pltpu.CompilerParams(vmem_limit_bytes=56 * 1024 * 1024),
+        compiler_params=pltpu.CompilerParams(vmem_limit_bytes=(16 << 20) + 8 * per_step * rows * keys_all + 2 * per_step * rows * keys_all),
         cost_estimate=pl.CostEstimate(
             flops=(24 if span else 1) * RATIO * rows * keys_all * HEAD_DIM,
             transcendentals=RATIO * rows * keys_all,
@@ -254,6 +278,15 @@
         cost_estimate=pl.CostEstimate(flops=0, transcendentals=0, bytes_accessed=cost),
         name=name,
     )(scalars, *operands)
+
+
+def pick_kernel(scalar_ref, own, peer, *outs):
+    for i, out in enumerate(outs):
+        for j in range(4):
+            source = (own, peer)[j // 2]
+            start = (j % 2 * KV_HEADS + 2 * scalar_ref[0] + i) * HEAD_DIM
+            lanes = pl.ds(pl.multiple_of(start, HEAD_DIM), HEAD_DIM)
+            out[:, j * HEAD_DIM : (j + 1) * HEAD_DIM] = source[:, lanes]
 
 
 def turn_kernel(offset, scalar_ref, *refs):
@@ -383,14 +416,15 @@
     core_scalar = core.reshape(1).astype(jnp.int32)
     data_scalar = data_me.reshape(1).astype(jnp.int32)
 
-    halves = [[], []]
-    for source in (keys_values, swap(keys_values, "ctx", 1)):
-        for j in range(2):
-            both = source[0, :, j].reshape(tokens, 2, 2 * HEAD_DIM)
-            both = lax.dynamic_index_in_dim(both, core, 1, keepdims=False)
-            halves[0].append(both[:, :HEAD_DIM])
-            halves[1].append(both[:, HEAD_DIM:])
-    own_a, own_b = (jnp.concatenate(half, axis=1) for half in halves)
+    flat = lax.optimization_barrier(keys_values.reshape(tokens, 2 * KV_HEADS * HEAD_DIM))
+    own_a, own_b = small_call(
+        pick_kernel,
+        "pick",
+        core_scalar,
+        [flat, swap(flat, "ctx", 1)],
+        [jax.ShapeDtypeStruct((tokens, 4 * HEAD_DIM), low)] * 2,
+        cost=1,
+    )
     pieces_a = [own_a] + [swap(own_a, "ctx", k) for k in hops]
     own_mask, queries_later, out_grad_later = hold((tree_mask[0], queries, out_grad), own_a)
     peer_mask = swap(own_mask, "ctx", 1)

time: 94.6 us -> 91 us (0.962)
  waiting for transfers between devices: 23 us -> 28 us
  Pallas kernels: 30.2 us -> 25.7 us
  local copies, waits for them, and re-layouts: 5.87 us -> 3.84 us
  other arithmetic: 2.37 us -> 1.25 us
    ppermute x31, waiting for transfers between devices: 23 us -> 28 us  [swap(): return lax.ppermute(value, axis, pairs)]
    pallas_call x2, Pallas kernels: 24.4 us -> 19.8 us  [attention(): pl.pallas_call(functools.partial(attention_kernel, pieces, blocks_here, s...]
    slice x6 -> x0, local copies, waits for them, and re-layouts: 1.66 us -> none  [the longest x2 1 us: body(): both = source[0, :, j].reshape(tokens, 2, 2 * HEAD_DIM)]
    concatenate x2 -> x0, other arithmetic: 1.55 us -> none  [body(): own_a, own_b = (jnp.concatenate(half, axis=1) for half in halves)]
    convert_element_type x2, other arithmetic: 0.16 us -> 1.12 us  [owned(): return total.astype(low)]
    unnamed x41 -> x25, local copies, waits for them, and re-layouts: 3.75 us -> 3.84 us
    pallas_call x7 -> x8, Pallas kernels: 2.93 us -> 2.99 us  [small_call(): pl.pallas_call(kernel, grid=(1,) if streamed else (), in_specs=[pl.BlockS...]
  transfers between devices with their start and end apart: 31 -> 31, of which waited for: 10 -> 15; matrix products, arithmetic and copies ran while one was open for 3% -> 1% of each run, Pallas kernels for 31% -> 27%
where the time goes in v3:
time: 91 us; the launch traced here: 90.7 us
  starting transfers between devices  31 us (34%)
  waiting for transfers between devices  28 us (31%)
  Pallas kernels  25.7 us (28%)
  local copies, waits for them, and re-layouts  3.84 us (4%)
  other arithmetic  1.25 us (1%)
    ppermute x31, starting transfers between devices, swap(): return lax.ppermute(value, axis, pairs)  31 us
    ppermute x31, waiting for transfers between devices, swap(): return lax.ppermute(value, axis, pairs)  28 us
    pallas_call x2, Pallas kernels, attention(): pl.pallas_call(functools.partial(attention_kernel, pieces, blocks_here, s...  19.8 us
    unnamed x25, local copies, waits for them, and re-layouts  3.84 us
    pallas_call x8, Pallas kernels, small_call(): pl.pallas_call(kernel, grid=(1,) if streamed else (), in_specs=[pl.BlockS...  2.99 us
    pallas_call x1, Pallas kernels, join(): pl.pallas_call(join_kernel, in_specs=[pl.BlockSpec(memory_space=pltpu.SME...  2.88 us
  transfers between devices with their start and end apart: 31, of which 15 were waited for; matrix products, arithmetic and copies ran while one was open for 1% of the time, Pallas kernels for 27%

profile of v3, /device:TPU:0, one launch (start us, length us, event | category | flops | bytes accessed | tf_op | source)
XLA Modules:
  0.0 90.7 jit_solution(15141346208471017637)
XLA Ops:
  0.7 1.1 %copy.9 = bf16[16,8,2,512]{3,1,2,0:T(8,128)(2,1)S(1)} copy(bf16[16,8,2,512]{3,2,1,0:T(2,128)(2,1)} %bitcast.13) | data formatting | bytes 524288
  2.3 1.2 %collective-permute-done.peer = bf16[128,1024]{1,0:T(8,128)(2,1)S(1)} collective-permute-done((bf16[128,1024]{1,0:T(8,128)(2,1)S(1)}, bf16[128,1024]{1,0:T(8,128)(2,1)S(1)}, u32[]{:S(2)}, u32[]{:S(2)}) %collective-permute-start) | collective-permute-done | bytes 262176 | tf_op jit(solution)/shard_map/ppermute | solution.py:22
  4.1 3.8 %collective-permute-start.9 = (bf16[128,512]{1,0:T(8,128)(2,1)S(1)}, bf16[128,512]{1,0:T(8,128)(2,1)S(1)}, u32[]{:S(2)}, u32[]{:S(2)}) collective-permute-start(bf16[128,512]{1,0:T(8,128)(2,1)S(1)} %get-tuple-element.75.refs_5_), channel_id=1, source_target_pairs={{0,6},{1,7},{2,4},{3,5},{4,2},{5,3},{6,0},{7,1},{8,14},{9,15},{10,... | collective-permute-start | bytes 393224 | tf_op jit(solution)/shard_map/ppermute | solution.py:22
  8.4 1.3 %collective-permute-done.1.peer_mask = s32[1,8]{1,0:T(1,128)S(1)} collective-permute-done((s32[1,8]{1,0:T(1,128)}, s32[1,8]{1,0:T(1,128)S(1)}, u32[]{:S(2)}, u32[]{:S(2)}) %collective-permute-start.1) | collective-permute-done | bytes 64 | tf_op jit(solution)/shard_map/ppermute | solution.py:22
  9.7 1.0 %collective-permute-start.7 = (bf16[128,512]{1,0:T(8,128)(2,1)S(1)}, bf16[128,512]{1,0:T(8,128)(2,1)}, u32[]{:S(2)}, u32[]{:S(2)}) collective-permute-start(bf16[128,512]{1,0:T(8,128)(2,1)S(1)} %get-tuple-element.75.refs_5_), channel_id=1, source_target_pairs={{0,2},{1,3},{2,0},{3,1},{4,6},{5,7},{6,4},{7,5},{8,10},{9,11},{10,... | collective-permute-start | bytes 393224 | tf_op jit(solution)/shard_map/ppermute | solution.py:22
  10.9 1.1 %collective-permute-start.4 = (bf16[128,1024]{1,0:T(8,128)(2,1)S(1)}, bf16[128,1024]{1,0:T(8,128)(2,1)S(1)}, u32[]{:S(2)}, u32[]{:S(2)}) collective-permute-start(bf16[128,1024]{1,0:T(8,128)(2,1)S(1)} %get-tuple-element.84), channel_id=1, source_target_pairs={{0,2},{1,3},{2,0},{3,1},{4,6},{5,7},{6,4},{7,5},{8,10},{9,11},{10,... | collective-permute-start | bytes 786440 | tf_op jit(solution)/shard_map/ppermute | solution.py:22
  12.0 1.5 %collective-permute-start.5 = (bf16[128,1024]{1,0:T(8,128)(2,1)S(1)}, bf16[128,1024]{1,0:T(8,128)(2,1)S(1)}, u32[]{:S(2)}, u32[]{:S(2)}) collective-permute-start(bf16[128,1024]{1,0:T(8,128)(2,1)S(1)} %get-tuple-element.85), channel_id=1, source_target_pairs={{0,4},{1,5},{2,6},{3,7},{4,0},{5,1},{6,2},{7,3},{8,12},{9,13},{10,... | collective-permute-start | bytes 786440 | tf_op jit(solution)/shard_map/ppermute | solution.py:22
  14.7 1.4 %collective-permute-done.7.refs_6_ = bf16[128,512]{1,0:T(8,128)(2,1)} collective-permute-done((bf16[128,512]{1,0:T(8,128)(2,1)S(1)}, bf16[128,512]{1,0:T(8,128)(2,1)}, u32[]{:S(2)}, u32[]{:S(2)}) %collective-permute-start.7) | collective-permute-done | bytes 131104 | tf_op jit(solution)/shard_map/ppermute | solution.py:22
  16.1 1.2 %copy-done.2 = bf16[1,128,4096]{2,1,0:T(8,128)(2,1)S(1)} copy-done((bf16[1,128,4096]{2,1,0:T(8,128)(2,1)S(1)}, bf16[1,128,4096]{2,1,0:T(8,128)(2,1)}, u32[]{:S(2)}) %copy-start.2) | copy-done | bytes 1048600
  17.4 9.6 %attention.2 = (bf16[128,1024]{1,0:T(8,128)(2,1)S(1)}, bf16[128,1024]{1,0:T(8,128)(2,1)S(1)}, bf16[128,2048]{1,0:T(8,128)(2,1)S(1)}, bf16[128,1024]{1,0:T(8,128)...) custom-call(s32[2]{0:T(128)S(1)} %pad_add_fusion.where_ref, ...), custom_call_target="tpu_custom_call" | custom-call | flops 6442450944 | bytes 2097152 | tf_op jit(solution)/shard_map/attention/pallas_call | solution.py:228
  27.8 1.0 %collective-permute-start.10 = (bf16[128,1024]{1,0:T(8,128)(2,1)S(1)}, bf16[128,1024]{1,0:T(8,128)(2,1)S(1)}, u32[]{:S(2)}, u32[]{:S(2)}) collective-permute-start(bf16[128,1024]{1,0:T(8,128)(2,1)S(1)} %get-tuple-element.97), channel_id=1, source_target_pairs={{0,2},{1,3},{2,0},{3,1},{4,6},{5,7},{6,4},{7,5},{8,10},{9,11},{10,... | collective-permute-start | bytes 786440 | tf_op jit(solution)/shard_map/ppermute | solution.py:22
  28.9 1.5 %collective-permute-start.11 = (bf16[128,1024]{1,0:T(8,128)(2,1)S(1)}, bf16[128,1024]{1,0:T(8,128)(2,1)S(1)}, u32[]{:S(2)}, u32[]{:S(2)}) collective-permute-start(bf16[128,1024]{1,0:T(8,128)(2,1)S(1)} %get-tuple-element.98), channel_id=1, source_target_pairs={{0,4},{1,5},{2,6},{3,7},{4,0},{5,1},{6,2},{7,3},{8,12},{9,13},{10,... | collective-permute-start | bytes 786440 | tf_op jit(solution)/shard_map/ppermute | solution.py:22
  31.3 10.2 %attention.3 = (bf16[128,1024]{1,0:T(8,128)(2,1)S(1)}, bf16[128,1024]{1,0:T(8,128)(2,1)S(1)}, bf16[128,2048]{1,0:T(8,128)(2,1)S(1)}, bf16[128,512]{1,0:T(8,128)(...) custom-call(s32[2]{0:T(128)S(1)} %pad_add_fusion.where_ref, ...), custom_call_target="tpu_custom_call" | custom-call | flops 268435456 | bytes 2097152 | tf_op jit(solution)/shard_map/attention/pallas_call | solution.py:228
  41.9 1.2 %collective-permute-done.12.refs_3_ = bf16[128,1024]{1,0:T(8,128)(2,1)S(1)} collective-permute-done((bf16[128,1024]{1,0:T(8,128)(2,1)S(1)}, bf16[128,1024]{1,0:T(8,128)(2,1)S(1)}, u32[]{:S(2)}, u32[]{:S(2)}) %collective-permute-start.12) | collective-permute-done | bytes 262176 | tf_op jit(solution)/shard_map/ppermute | solution.py:22
  44.0 1.8 %collective-permute-start.18 = (bf16[128,512]{1,0:T(8,128)(2,1)S(1)}, bf16[128,512]{1,0:T(8,128)(2,1)S(1)}, u32[]{:S(2)}, u32[]{:S(2)}) collective-permute-start(bf16[128,512]{1,0:T(8,128)(2,1)S(1)} %add_convert_fusion.3.refs_0_), channel_id=1, source_target_pairs={{0,6},{1,7},{2,4},{3,5},{4,2},{5,3},{6,0},{7,1},{8,14},{9,15},{10,... | collective-permute-start | bytes 393224 | tf_op jit(solution)/shard_map/ppermute | solution.py:22
  47.5 1.0 %collective-permute-start.21 = (bf16[128,512]{1,0:T(8,128)(2,1)}, bf16[128,512]{1,0:T(8,128)(2,1)S(1)}, u32[]{:S(2)}, u32[]{:S(2)}) collective-permute-start(bf16[128,512]{1,0:T(8,128)(2,1)} %get-tuple-element.107), channel_id=1, source_target_pairs={{0,2},{1,3},{2,0},{3,1},{4,6},{5,7},{6,4},{7,5},{8,10},{9,11},{10,... | collective-permute-start | bytes 393224 | tf_op jit(solution)/shard_map/ppermute | solution.py:22
  48.5 2.7 %collective-permute-done.18.refs_3_ = bf16[128,512]{1,0:T(8,128)(2,1)S(1)} collective-permute-done((bf16[128,512]{1,0:T(8,128)(2,1)S(1)}, bf16[128,512]{1,0:T(8,128)(2,1)S(1)}, u32[]{:S(2)}, u32[]{:S(2)}) %collective-permute-start.18) | collective-permute-done | bytes 131104 | tf_op jit(solution)/shard_map/ppermute | solution.py:22
  51.3 1.3 %collective-permute-start.22 = (bf16[128,512]{1,0:T(8,128)(2,1)}, bf16[128,512]{1,0:T(8,128)(2,1)}, u32[]{:S(2)}, u32[]{:S(2)}) collective-permute-start(bf16[128,512]{1,0:T(8,128)(2,1)} %get-tuple-element.108), channel_id=1, source_target_pairs={{0,4},{1,5},{2,6},{3,7},{4,0},{5,1},{6,2},{7,3},{8,12},{9,13},{10,... | collective-permute-start | bytes 393224 | tf_op jit(solution)/shard_map/ppermute | solution.py:22
  52.6 1.1 %collective-permute-done.17.refs_2_ = bf16[128,512]{1,0:T(8,128)(2,1)S(1)} collective-permute-done((bf16[128,512]{1,0:T(8,128)(2,1)S(1)}, bf16[128,512]{1,0:T(8,128)(2,1)S(1)}, u32[]{:S(2)}, u32[]{:S(2)}) %collective-permute-start.17) | collective-permute-done | bytes 131104 | tf_op jit(solution)/shard_map/ppermute | solution.py:22
  53.7 1.8 %collective-permute-start.23 = (bf16[128,512]{1,0:T(8,128)(2,1)S(1)}, bf16[128,512]{1,0:T(8,128)(2,1)}, u32[]{:S(2)}, u32[]{:S(2)}) collective-permute-start(bf16[128,512]{1,0:T(8,128)(2,1)S(1)} %get-tuple-element.109), channel_id=1, source_target_pairs={{0,6},{1,7},{2,4},{3,5},{4,2},{5,3},{6,0},{7,1},{8,14},{9,15},{10,... | collective-permute-start | bytes 393224 | tf_op jit(solution)/shard_map/ppermute | solution.py:22
  56.3 1.6 %collective-permute-start.19 = (bf16[512,256]{1,0:T(8,128)(2,1)S(1)}, bf16[512,256]{1,0:T(8,128)(2,1)S(1)}, u32[]{:S(2)}, u32[]{:S(2)}) collective-permute-start(bf16[512,256]{1,0:T(8,128)(2,1)S(1)} %get-tuple-element.104), channel_id=1, source_target_pairs={{0,8},{8,0},{16,24},{24,16},{1,9},{9,1},{17,25},{25,17},{2,10},{10... | collective-permute-start | bytes 786440 | tf_op jit(solution)/shard_map/ppermute | solution.py:22
  57.9 2.2 %collective-permute-done.23 = bf16[128,512]{1,0:T(8,128)(2,1)} collective-permute-done((bf16[128,512]{1,0:T(8,128)(2,1)S(1)}, bf16[128,512]{1,0:T(8,128)(2,1)}, u32[]{:S(2)}, u32[]{:S(2)}) %collective-permute-start.23) | collective-permute-done | bytes 131104 | tf_op jit(solution)/shard_map/ppermute | solution.py:22
  60.1 1.0 %add_convert_fusion.1.refs_0_ = bf16[128,512]{1,0:T(8,128)(2,1)S(1)} fusion(bf16[128,512]{1,0:T(8,128)(2,1)} %collective-permute-done.23, bf16[128,512]{1,0:T(8,128)(2,1)} %collective-permute-done.22, bf16[128,512]{1,0:T(8,128)(2,1)S(1)} %collective-permute-done.21, bf16[128,512]{1,0:T(8,128)(2,1)S(1)} %get-tuple-element.106), kind=kLoop, calls=%fused_computation.1 | loop fusion | flops 524288 | bytes 655360 | tf_op jit(solution)/shard_map/convert_element_type | solution.py:476
  61.1 1.8 %collective-permute-start.26 = (bf16[128,512]{1,0:T(8,128)(2,1)S(1)}, bf16[128,512]{1,0:T(8,128)(2,1)S(1)}, u32[]{:S(2)}, u32[]{:S(2)}) collective-permute-start(bf16[128,512]{1,0:T(8,128)(2,1)S(1)} %add_convert_fusion.1.refs_0_), channel_id=1, source_target_pairs={{0,6},{1,7},{2,4},{3,5},{4,2},{5,3},{6,0},{7,1},{8,14},{9,15},{10,... | collective-permute-start | bytes 393224 | tf_op jit(solution)/shard_map/ppermute | solution.py:22
  64.7 3.6 %collective-permute-done.26.refs_3_ = bf16[128,512]{1,0:T(8,128)(2,1)S(1)} collective-permute-done((bf16[128,512]{1,0:T(8,128)(2,1)S(1)}, bf16[128,512]{1,0:T(8,128)(2,1)S(1)}, u32[]{:S(2)}, u32[]{:S(2)}) %collective-permute-start.26) | collective-permute-done | bytes 131104 | tf_op jit(solution)/shard_map/ppermute | solution.py:22
  68.3 1.1 %collective-permute-done.25.refs_2_ = bf16[128,512]{1,0:T(8,128)(2,1)S(1)} collective-permute-done((bf16[128,512]{1,0:T(8,128)(2,1)S(1)}, bf16[128,512]{1,0:T(8,128)(2,1)S(1)}, u32[]{:S(2)}, u32[]{:S(2)}) %collective-permute-start.25) | collective-permute-done | bytes 131104 | tf_op jit(solution)/shard_map/ppermute | solution.py:22
  70.3 1.6 %collective-permute-start.27 = (bf16[512,256]{1,0:T(8,128)(2,1)S(1)}, bf16[512,256]{1,0:T(8,128)(2,1)S(1)}, u32[]{:S(2)}, u32[]{:S(2)}) collective-permute-start(bf16[512,256]{1,0:T(8,128)(2,1)S(1)} %get-tuple-element.116), channel_id=1, source_target_pairs={{0,8},{8,0},{16,24},{24,16},{1,9},{9,1},{17,25},{25,17},{2,10},{10... | collective-permute-start | bytes 786440 | tf_op jit(solution)/shard_map/ppermute | solution.py:22
  71.9 2.6 %collective-permute-start.20 = (bf16[256,256]{1,0:T(8,128)(2,1)S(1)}, bf16[256,256]{1,0:T(8,128)(2,1)S(1)}, u32[]{:S(2)}, u32[]{:S(2)}) collective-permute-start(bf16[256,256]{1,0:T(8,128)(2,1)S(1)} %add_convert_fusion.2), channel_id=1, source_target_pairs={{0,16},{8,24},{16,0},{24,8},{1,17},{9,25},{17,1},{25,9},{2,18},{10... | collective-permute-start | bytes 393224 | tf_op jit(solution)/shard_map/ppermute | solution.py:22
  74.5 7.1 %collective-permute-done.27.refs_4_ = bf16[512,256]{1,0:T(8,128)(2,1)S(1)} collective-permute-done((bf16[512,256]{1,0:T(8,128)(2,1)S(1)}, bf16[512,256]{1,0:T(8,128)(2,1)S(1)}, u32[]{:S(2)}, u32[]{:S(2)}) %collective-permute-start.27) | collective-permute-done | bytes 262176 | tf_op jit(solution)/shard_map/ppermute | solution.py:22
  82.7 2.9 %join.1 = (bf16[1,128,4096]{2,1,0:T(8,128)(2,1)}, bf16[1,128,4096]{2,1,0:T(8,128)(2,1)}) custom-call(s32[1]{0:T(128)} %bitcast.1.scalar_ref, bf16[128,1024]{1,0:T(8,128)(2,1)} %copy-done.3, bf16[128,1024]{1,0:T(8,128)(2,1)} %copy-done.5, bf16[128,1024]{1,0:T(8,128)(2,1)} %copy-done.4, bf16[128,1024]{1,0:T(8,128)(2,1)} %copy-done.6, ...), custom_call_target="tpu_custom_call" | custom-call | bytes 4000000 | tf_op jit(solution)/shard_map/join/pallas_call | solution.py:389
  85.6 2.5 %collective-permute-done.28.refs_5_ = bf16[256,256]{1,0:T(8,128)(2,1)S(1)} collective-permute-done((bf16[256,256]{1,0:T(8,128)(2,1)S(1)}, bf16[256,256]{1,0:T(8,128)(2,1)S(1)}, u32[]{:S(2)}, u32[]{:S(2)}) %collective-permute-start.28) | collective-permute-done | bytes 131104 | tf_op jit(solution)/shard_map/ppermute | solution.py:22
  88.3 1.5 %collective-permute-done.30.got = f32[128,512]{1,0:T(8,128)S(1)} collective-permute-done((f32[128,512]{1,0:T(8,128)S(1)}, f32[128,512]{1,0:T(8,128)S(1)}, u32[]{:S(2)}, u32[]{:S(2)}) %collective-permute-start.30) | collective-permute-done | bytes 262176 | tf_op jit(solution)/shard_map/ppermute | solution.py:22
  (71 shorter events, 13.2 us)
Async XLA Ops:
  0.6 15.5 %copy-start.1 = (bf16[1,128,4096]{2,1,0:T(8,128)(2,1)S(1)}, bf16[1,128,4096]{2,1,0:T(8,128)(2,1)}, u32[]{:S(2)}) copy-start(bf16[1,128,4096]{2,1,0:T(8,128)(2,1)} %refs_0_.3) | copy-start | bytes 3145732
  1.8 1.7 %collective-permute-start = (bf16[128,1024]{1,0:T(8,128)(2,1)S(1)}, bf16[128,1024]{1,0:T(8,128)(2,1)S(1)}, u32[]{:S(2)}, u32[]{:S(2)}) collective-permute-start(bf16[128,1024]{1,0:T(8,128)(2,1)S(1)} %bitcast.8), channel_id=1, source_target_pairs={{0,1},{1,0},{2,3},{3,2},{4,5},{5,4},{6,7},{7,6},{8,9},{9,8},{10,11... | collective-permute-start | bytes 786440 | tf_op jit(solution)/shard_map/ppermute | solution.py:22
  3.5 7.3 %collective-permute-start.2 = (bf16[1,128,4096]{2,1,0:T(8,128)(2,1)}, bf16[1,128,4096]{2,1,0:T(8,128)(2,1)S(1)}, u32[]{:S(2)}, u32[]{:S(2)}) collective-permute-start(bf16[1,128,4096]{2,1,0:T(8,128)(2,1)} %refs_0_.3), channel_id=1, source_target_pairs={{0,1},{1,0},{2,3},{3,2},{4,5},{5,4},{6,7},{7,6},{8,9},{9,8},{10,11... | collective-permute-start | bytes 3145736 | tf_op jit(solution)/shard_map/ppermute | solution.py:22
  4.0 6.9 %collective-permute-start.3 = (bf16[1,128,4096]{2,1,0:T(8,128)(2,1)}, bf16[1,128,4096]{2,1,0:T(8,128)(2,1)}, u32[]{:S(2)}, u32[]{:S(2)}) collective-permute-start(bf16[1,128,4096]{2,1,0:T(8,128)(2,1)} %refs_2_.1), channel_id=1, source_target_pairs={{0,1},{1,0},{2,3},{3,2},{4,5},{5,4},{6,7},{7,6},{8,9},{9,8},{10,11... | collective-permute-start | bytes 3145736 | tf_op jit(solution)/shard_map/ppermute | solution.py:22
  4.1 9.4 %collective-permute-start.9 = (bf16[128,512]{1,0:T(8,128)(2,1)S(1)}, bf16[128,512]{1,0:T(8,128)(2,1)S(1)}, u32[]{:S(2)}, u32[]{:S(2)}) collective-permute-start(bf16[128,512]{1,0:T(8,128)(2,1)S(1)} %get-tuple-element.75.refs_5_), channel_id=1, source_target_pairs={{0,6},{1,7},{2,4},{3,5},{4,2},{5,3},{6,0},{7,1},{8,14},{9,15},{10,... | collective-permute-start | bytes 393224 | tf_op jit(solution)/shard_map/ppermute | solution.py:22
  7.9 6.8 %collective-permute-start.8 = (bf16[128,512]{1,0:T(8,128)(2,1)S(1)}, bf16[128,512]{1,0:T(8,128)(2,1)}, u32[]{:S(2)}, u32[]{:S(2)}) collective-permute-start(bf16[128,512]{1,0:T(8,128)(2,1)S(1)} %get-tuple-element.75.refs_5_), channel_id=1, source_target_pairs={{0,4},{1,5},{2,6},{3,7},{4,0},{5,1},{6,2},{7,3},{8,12},{9,13},{10,... | collective-permute-start | bytes 393224 | tf_op jit(solution)/shard_map/ppermute | solution.py:22
  8.4 1.3 %collective-permute-start.1 = (s32[1,8]{1,0:T(1,128)}, s32[1,8]{1,0:T(1,128)S(1)}, u32[]{:S(2)}, u32[]{:S(2)}) collective-permute-start(s32[1,8]{1,0:T(1,128)} %bitcast.10), channel_id=1, source_target_pairs={{0,1},{1,0},{2,3},{3,2},{4,5},{5,4},{6,7},{7,6},{8,9},{9,8},{10,11... | collective-permute-start | bytes 104 | tf_op jit(solution)/shard_map/ppermute | solution.py:22
  9.7 6.4 %collective-permute-start.7 = (bf16[128,512]{1,0:T(8,128)(2,1)S(1)}, bf16[128,512]{1,0:T(8,128)(2,1)}, u32[]{:S(2)}, u32[]{:S(2)}) collective-permute-start(bf16[128,512]{1,0:T(8,128)(2,1)S(1)} %get-tuple-element.75.refs_5_), channel_id=1, source_target_pairs={{0,2},{1,3},{2,0},{3,1},{4,6},{5,7},{6,4},{7,5},{8,10},{9,11},{10,... | collective-permute-start | bytes 393224 | tf_op jit(solution)/shard_map/ppermute | solution.py:22
  10.9 16.1 %collective-permute-start.4 = (bf16[128,1024]{1,0:T(8,128)(2,1)S(1)}, bf16[128,1024]{1,0:T(8,128)(2,1)S(1)}, u32[]{:S(2)}, u32[]{:S(2)}) collective-permute-start(bf16[128,1024]{1,0:T(8,128)(2,1)S(1)} %get-tuple-element.84), channel_id=1, source_target_pairs={{0,2},{1,3},{2,0},{3,1},{4,6},{5,7},{6,4},{7,5},{8,10},{9,11},{10,... | collective-permute-start | bytes 786440 | tf_op jit(solution)/shard_map/ppermute | solution.py:22
  12.0 15.1 %collective-permute-start.5 = (bf16[128,1024]{1,0:T(8,128)(2,1)S(1)}, bf16[128,1024]{1,0:T(8,128)(2,1)S(1)}, u32[]{:S(2)}, u32[]{:S(2)}) collective-permute-start(bf16[128,1024]{1,0:T(8,128)(2,1)S(1)} %get-tuple-element.85), channel_id=1, source_target_pairs={{0,4},{1,5},{2,6},{3,7},{4,0},{5,1},{6,2},{7,3},{8,12},{9,13},{10,... | collective-permute-start | bytes 786440 | tf_op jit(solution)/shard_map/ppermute | solution.py:22
  13.5 14.0 %collective-permute-start.6 = (bf16[128,1024]{1,0:T(8,128)(2,1)S(1)}, bf16[128,1024]{1,0:T(8,128)(2,1)S(1)}, u32[]{:S(2)}, u32[]{:S(2)}) collective-permute-start(bf16[128,1024]{1,0:T(8,128)(2,1)S(1)} %get-tuple-element.86), channel_id=1, source_target_pairs={{0,6},{1,7},{2,4},{3,5},{4,2},{5,3},{6,0},{7,1},{8,14},{9,15},{10,... | collective-permute-start | bytes 786440 | tf_op jit(solution)/shard_map/ppermute | solution.py:22
  27.0 16.1 %collective-permute-start.13 = (bf16[128,2048]{1,0:T(8,128)(2,1)S(1)}, bf16[128,2048]{1,0:T(8,128)(2,1)S(1)}, u32[]{:S(2)}, u32[]{:S(2)}) collective-permute-start(bf16[128,2048]{1,0:T(8,128)(2,1)S(1)} %get-tuple-element.87), channel_id=1, source_target_pairs={{0,1},{1,0},{2,3},{3,2},{4,5},{5,4},{6,7},{7,6},{8,9},{9,8},{10,11... | collective-permute-start | bytes 1572872 | tf_op jit(solution)/shard_map/ppermute | solution.py:22
  27.7 15.3 %collective-permute-start.14 = (bf16[512,512]{1,0:T(8,128)(2,1)S(1)}, bf16[512,512]{1,0:T(8,128)(2,1)S(1)}, u32[]{:S(2)}, u32[]{:S(2)}) collective-permute-start(bf16[512,512]{1,0:T(8,128)(2,1)S(1)} %turn.2.own_low), channel_id=1, source_target_pairs={{0,1},{1,0},{2,3},{3,2},{4,5},{5,4},{6,7},{7,6},{8,9},{9,8},{10,11... | collective-permute-start | bytes 1572872 | tf_op jit(solution)/shard_map/ppermute | solution.py:22
  27.8 13.7 %collective-permute-start.10 = (bf16[128,1024]{1,0:T(8,128)(2,1)S(1)}, bf16[128,1024]{1,0:T(8,128)(2,1)S(1)}, u32[]{:S(2)}, u32[]{:S(2)}) collective-permute-start(bf16[128,1024]{1,0:T(8,128)(2,1)S(1)} %get-tuple-element.97), channel_id=1, source_target_pairs={{0,2},{1,3},{2,0},{3,1},{4,6},{5,7},{6,4},{7,5},{8,10},{9,11},{10,... | collective-permute-start | bytes 786440 | tf_op jit(solution)/shard_map/ppermute | solution.py:22
  28.9 13.0 %collective-permute-start.11 = (bf16[128,1024]{1,0:T(8,128)(2,1)S(1)}, bf16[128,1024]{1,0:T(8,128)(2,1)S(1)}, u32[]{:S(2)}, u32[]{:S(2)}) collective-permute-start(bf16[128,1024]{1,0:T(8,128)(2,1)S(1)} %get-tuple-element.98), channel_id=1, source_target_pairs={{0,4},{1,5},{2,6},{3,7},{4,0},{5,1},{6,2},{7,3},{8,12},{9,13},{10,... | collective-permute-start | bytes 786440 | tf_op jit(solution)/shard_map/ppermute | solution.py:22
  30.4 12.7 %collective-permute-start.12 = (bf16[128,1024]{1,0:T(8,128)(2,1)S(1)}, bf16[128,1024]{1,0:T(8,128)(2,1)S(1)}, u32[]{:S(2)}, u32[]{:S(2)}) collective-permute-start(bf16[128,1024]{1,0:T(8,128)(2,1)S(1)} %get-tuple-element.99), channel_id=1, source_target_pairs={{0,6},{1,7},{2,4},{3,5},{4,2},{5,3},{6,0},{7,1},{8,14},{9,15},{10,... | collective-permute-start | bytes 786440 | tf_op jit(solution)/shard_map/ppermute | solution.py:22
  43.9 11.6 %collective-permute-start.15 = (bf16[512,512]{1,0:T(8,128)(2,1)S(1)}, bf16[512,512]{1,0:T(8,128)(2,1)S(1)}, u32[]{:S(2)}, u32[]{:S(2)}) collective-permute-start(bf16[512,512]{1,0:T(8,128)(2,1)S(1)} %turn.3.own_high), channel_id=1, source_target_pairs={{0,1},{1,0},{2,3},{3,2},{4,5},{5,4},{6,7},{7,6},{8,9},{9,8},{10,11... | collective-permute-start | bytes 1572872 | tf_op jit(solution)/shard_map/ppermute | solution.py:22
  44.0 7.3 %collective-permute-start.18 = (bf16[128,512]{1,0:T(8,128)(2,1)S(1)}, bf16[128,512]{1,0:T(8,128)(2,1)S(1)}, u32[]{:S(2)}, u32[]{:S(2)}) collective-permute-start(bf16[128,512]{1,0:T(8,128)(2,1)S(1)} %add_convert_fusion.3.refs_0_), channel_id=1, source_target_pairs={{0,6},{1,7},{2,4},{3,5},{4,2},{5,3},{6,0},{7,1},{8,14},{9,15},{10,... | collective-permute-start | bytes 393224 | tf_op jit(solution)/shard_map/ppermute | solution.py:22
  45.8 7.9 %collective-permute-start.17 = (bf16[128,512]{1,0:T(8,128)(2,1)S(1)}, bf16[128,512]{1,0:T(8,128)(2,1)S(1)}, u32[]{:S(2)}, u32[]{:S(2)}) collective-permute-start(bf16[128,512]{1,0:T(8,128)(2,1)S(1)} %add_convert_fusion.3.refs_0_), channel_id=1, source_target_pairs={{0,4},{1,5},{2,6},{3,7},{4,0},{5,1},{6,2},{7,3},{8,12},{9,13},{10,... | collective-permute-start | bytes 393224 | tf_op jit(solution)/shard_map/ppermute | solution.py:22
  46.5 9.0 %collective-permute-start.16 = (bf16[128,512]{1,0:T(8,128)(2,1)S(1)}, bf16[128,512]{1,0:T(8,128)(2,1)S(1)}, u32[]{:S(2)}, u32[]{:S(2)}) collective-permute-start(bf16[128,512]{1,0:T(8,128)(2,1)S(1)} %add_convert_fusion.3.refs_0_), channel_id=1, source_target_pairs={{0,2},{1,3},{2,0},{3,1},{4,6},{5,7},{6,4},{7,5},{8,10},{9,11},{10,... | collective-permute-start | bytes 393224 | tf_op jit(solution)/shard_map/ppermute | solution.py:22
  47.5 10.4 %collective-permute-start.21 = (bf16[128,512]{1,0:T(8,128)(2,1)}, bf16[128,512]{1,0:T(8,128)(2,1)S(1)}, u32[]{:S(2)}, u32[]{:S(2)}) collective-permute-start(bf16[128,512]{1,0:T(8,128)(2,1)} %get-tuple-element.107), channel_id=1, source_target_pairs={{0,2},{1,3},{2,0},{3,1},{4,6},{5,7},{6,4},{7,5},{8,10},{9,11},{10,... | collective-permute-start | bytes 393224 | tf_op jit(solution)/shard_map/ppermute | solution.py:22
  51.3 6.7 %collective-permute-start.22 = (bf16[128,512]{1,0:T(8,128)(2,1)}, bf16[128,512]{1,0:T(8,128)(2,1)}, u32[]{:S(2)}, u32[]{:S(2)}) collective-permute-start(bf16[128,512]{1,0:T(8,128)(2,1)} %get-tuple-element.108), channel_id=1, source_target_pairs={{0,4},{1,5},{2,6},{3,7},{4,0},{5,1},{6,2},{7,3},{8,12},{9,13},{10,... | collective-permute-start | bytes 393224 | tf_op jit(solution)/shard_map/ppermute | solution.py:22
  53.7 6.4 %collective-permute-start.23 = (bf16[128,512]{1,0:T(8,128)(2,1)S(1)}, bf16[128,512]{1,0:T(8,128)(2,1)}, u32[]{:S(2)}, u32[]{:S(2)}) collective-permute-start(bf16[128,512]{1,0:T(8,128)(2,1)S(1)} %get-tuple-element.109), channel_id=1, source_target_pairs={{0,6},{1,7},{2,4},{3,5},{4,2},{5,3},{6,0},{7,1},{8,14},{9,15},{10,... | collective-permute-start | bytes 393224 | tf_op jit(solution)/shard_map/ppermute | solution.py:22
  56.3 14.0 %collective-permute-start.19 = (bf16[512,256]{1,0:T(8,128)(2,1)S(1)}, bf16[512,256]{1,0:T(8,128)(2,1)S(1)}, u32[]{:S(2)}, u32[]{:S(2)}) collective-permute-start(bf16[512,256]{1,0:T(8,128)(2,1)S(1)} %get-tuple-element.104), channel_id=1, source_target_pairs={{0,8},{8,0},{16,24},{24,16},{1,9},{9,1},{17,25},{25,17},{2,10},{10... | collective-permute-start | bytes 786440 | tf_op jit(solution)/shard_map/ppermute | solution.py:22
  61.1 7.2 %collective-permute-start.26 = (bf16[128,512]{1,0:T(8,128)(2,1)S(1)}, bf16[128,512]{1,0:T(8,128)(2,1)S(1)}, u32[]{:S(2)}, u32[]{:S(2)}) collective-permute-start(bf16[128,512]{1,0:T(8,128)(2,1)S(1)} %add_convert_fusion.1.refs_0_), channel_id=1, source_target_pairs={{0,6},{1,7},{2,4},{3,5},{4,2},{5,3},{6,0},{7,1},{8,14},{9,15},{10,... | collective-permute-start | bytes 393224 | tf_op jit(solution)/shard_map/ppermute | solution.py:22
  62.9 6.5 %collective-permute-start.25 = (bf16[128,512]{1,0:T(8,128)(2,1)S(1)}, bf16[128,512]{1,0:T(8,128)(2,1)S(1)}, u32[]{:S(2)}, u32[]{:S(2)}) collective-permute-start(bf16[128,512]{1,0:T(8,128)(2,1)S(1)} %add_convert_fusion.1.refs_0_), channel_id=1, source_target_pairs={{0,4},{1,5},{2,6},{3,7},{4,0},{5,1},{6,2},{7,3},{8,12},{9,13},{10,... | collective-permute-start | bytes 393224 | tf_op jit(solution)/shard_map/ppermute | solution.py:22
  63.7 5.8 %collective-permute-start.24 = (bf16[128,512]{1,0:T(8,128)(2,1)S(1)}, bf16[128,512]{1,0:T(8,128)(2,1)S(1)}, u32[]{:S(2)}, u32[]{:S(2)}) collective-permute-start(bf16[128,512]{1,0:T(8,128)(2,1)S(1)} %add_convert_fusion.1.refs_0_), channel_id=1, source_target_pairs={{0,2},{1,3},{2,0},{3,1},{4,6},{5,7},{6,4},{7,5},{8,10},{9,11},{10,... | collective-permute-start | bytes 393224 | tf_op jit(solution)/shard_map/ppermute | solution.py:22
  70.3 11.4 %collective-permute-start.27 = (bf16[512,256]{1,0:T(8,128)(2,1)S(1)}, bf16[512,256]{1,0:T(8,128)(2,1)S(1)}, u32[]{:S(2)}, u32[]{:S(2)}) collective-permute-start(bf16[512,256]{1,0:T(8,128)(2,1)S(1)} %get-tuple-element.116), channel_id=1, source_target_pairs={{0,8},{8,0},{16,24},{24,16},{1,9},{9,1},{17,25},{25,17},{2,10},{10... | collective-permute-start | bytes 786440 | tf_op jit(solution)/shard_map/ppermute | solution.py:22
  71.9 10.0 %collective-permute-start.29 = (bf16[128,2048]{1,0:T(8,128)(2,1)S(1)}, bf16[128,2048]{1,0:T(8,128)(2,1)S(1)}, u32[]{:S(2)}, u32[]{:S(2)}) collective-permute-start(bf16[128,2048]{1,0:T(8,128)(2,1)S(1)} %copy-done.9), channel_id=1, source_target_pairs={{0,1},{1,0},{2,3},{3,2},{4,5},{5,4},{6,7},{7,6},{8,9},{9,8},{10,11... | collective-permute-start | bytes 1572872 | tf_op jit(solution)/shard_map/ppermute | solution.py:22
  71.9 13.7 %collective-permute-start.20 = (bf16[256,256]{1,0:T(8,128)(2,1)S(1)}, bf16[256,256]{1,0:T(8,128)(2,1)S(1)}, u32[]{:S(2)}, u32[]{:S(2)}) collective-permute-start(bf16[256,256]{1,0:T(8,128)(2,1)S(1)} %add_convert_fusion.2), channel_id=1, source_target_pairs={{0,16},{8,24},{16,0},{24,8},{1,17},{9,25},{17,1},{25,9},{2,18},{10... | collective-permute-start | bytes 393224 | tf_op jit(solution)/shard_map/ppermute | solution.py:22
  81.7 6.5 %collective-permute-start.28 = (bf16[256,256]{1,0:T(8,128)(2,1)S(1)}, bf16[256,256]{1,0:T(8,128)(2,1)S(1)}, u32[]{:S(2)}, u32[]{:S(2)}) collective-permute-start(bf16[256,256]{1,0:T(8,128)(2,1)S(1)} %add_convert_fusion), channel_id=1, source_target_pairs={{0,16},{8,24},{16,0},{24,8},{1,17},{9,25},{17,1},{25,9},{2,18},{10... | collective-permute-start | bytes 393224 | tf_op jit(solution)/shard_map/ppermute | solution.py:22
  88.2 1.6 %collective-permute-start.30 = (f32[128,512]{1,0:T(8,128)S(1)}, f32[128,512]{1,0:T(8,128)S(1)}, u32[]{:S(2)}, u32[]{:S(2)}) collective-permute-start(f32[128,512]{1,0:T(8,128)S(1)} %get-tuple-element.141), channel_id=1, source_target_pairs={{0,1},{1,0},{2,3},{3,2},{4,5},{5,4},{6,7},{7,6},{8,9},{9,8},{10,11... | collective-permute-start | bytes 786440 | tf_op jit(solution)/shard_map/ppermute | solution.py:22
  (11 other events, 26.6 us)

commit v4 on v3

--- a/solution.py
+++ b/solution.py
@@ -507,9 +507,10 @@
     if pairwise:
         near_a = swap(chunks_a[2], "dp", 1)
         cross_a = (chunks_a[1] + near_a[:size].astype(high)).astype(low)
-        near_b = swap(hold(chunks_b[2], cross_a), "dp", 1)
+        far_a = swap(cross_a, "dp", 2)
+        near_b = swap(hold(chunks_b[2], far_a), "dp", 1)
         cross_b = (chunks_b[1] + near_b[:size].astype(high)).astype(low)
-        arrived = [[near_a, swap(cross_a, "dp", 2)], [near_b, swap(cross_b, "dp", 2)]]
+        arrived = [[near_a, far_a], [near_b, swap(cross_b, "dp", 2)]]
         starts = [0, size, 0]
     else:
         arrived = [[swap(x[k], "dp", k) for k in range(1, data_size)] for x in (chunks_a, chunks_b)]

time: 91 us -> 88.7 us (0.975)
  waiting for transfers between devices: 28 us -> 24.3 us
  starting transfers between devices: 31 us -> 32.6 us
    ppermute x31, waiting for transfers between devices: 28 us -> 24.3 us  [swap(): return lax.ppermute(value, axis, pairs)]
    ppermute x31, starting transfers between devices: 31 us -> 32.6 us  [swap(): return lax.ppermute(value, axis, pairs)]
  transfers between devices with their start and end apart: 31 -> 31, of which waited for: 15 -> 16; matrix products, arithmetic and copies ran while one was open for 1% -> 1% of each run, Pallas kernels for 27% -> 28%
where the time goes in v4:
time: 88.7 us; the launch traced here: 88.5 us
  starting transfers between devices  32.6 us (37%)
  Pallas kernels  25.7 us (29%)
  waiting for transfers between devices  24.3 us (27%)
  local copies, waits for them, and re-layouts  3.84 us (4%)
  other arithmetic  1.25 us (1%)
    ppermute x31, starting transfers between devices, swap(): return lax.ppermute(value, axis, pairs)  32.6 us
    ppermute x31, waiting for transfers between devices, swap(): return lax.ppermute(value, axis, pairs)  24.3 us
    pallas_call x2, Pallas kernels, attention(): pl.pallas_call(functools.partial(attention_kernel, pieces, blocks_here, s...  19.8 us
    unnamed x25, local copies, waits for them, and re-layouts  3.84 us
    pallas_call x8, Pallas kernels, small_call(): pl.pallas_call(kernel, grid=(1,) if streamed else (), in_specs=[pl.BlockS...  2.99 us
    pallas_call x1, Pallas kernels, join(): pl.pallas_call(join_kernel, in_specs=[pl.BlockSpec(memory_space=pltpu.SME...  2.88 us
  transfers between devices with their start and end apart: 31, of which 16 were waited for; matrix products, arithmetic and copies ran while one was open for 1% of the time, Pallas kernels for 28%

profile of v4, /device:TPU:0, one launch (start us, length us, event | category | flops | bytes accessed | tf_op | source)
XLA Modules:
  0.0 88.5 jit_solution(14892220606887980776)
XLA Ops:
  0.7 1.1 %copy.9 = bf16[16,8,2,512]{3,1,2,0:T(8,128)(2,1)S(1)} copy(bf16[16,8,2,512]{3,2,1,0:T(2,128)(2,1)} %bitcast.13) | data formatting | bytes 524288
  2.3 1.2 %collective-permute-done.peer = bf16[128,1024]{1,0:T(8,128)(2,1)S(1)} collective-permute-done((bf16[128,1024]{1,0:T(8,128)(2,1)S(1)}, bf16[128,1024]{1,0:T(8,128)(2,1)S(1)}, u32[]{:S(2)}, u32[]{:S(2)}) %collective-permute-start) | collective-permute-done | bytes 262176 | tf_op jit(solution)/shard_map/ppermute | solution.py:22
  4.1 3.8 %collective-permute-start.9 = (bf16[128,512]{1,0:T(8,128)(2,1)S(1)}, bf16[128,512]{1,0:T(8,128)(2,1)S(1)}, u32[]{:S(2)}, u32[]{:S(2)}) collective-permute-start(bf16[128,512]{1,0:T(8,128)(2,1)S(1)} %get-tuple-element.75.refs_5_), channel_id=1, source_target_pairs={{0,6},{1,7},{2,4},{3,5},{4,2},{5,3},{6,0},{7,1},{8,14},{9,15},{10,... | collective-permute-start | bytes 393224 | tf_op jit(solution)/shard_map/ppermute | solution.py:22
  8.4 1.3 %collective-permute-done.1.peer_mask = s32[1,8]{1,0:T(1,128)S(1)} collective-permute-done((s32[1,8]{1,0:T(1,128)}, s32[1,8]{1,0:T(1,128)S(1)}, u32[]{:S(2)}, u32[]{:S(2)}) %collective-permute-start.1) | collective-permute-done | bytes 64 | tf_op jit(solution)/shard_map/ppermute | solution.py:22
  9.7 1.0 %collective-permute-start.7 = (bf16[128,512]{1,0:T(8,128)(2,1)S(1)}, bf16[128,512]{1,0:T(8,128)(2,1)}, u32[]{:S(2)}, u32[]{:S(2)}) collective-permute-start(bf16[128,512]{1,0:T(8,128)(2,1)S(1)} %get-tuple-element.75.refs_5_), channel_id=1, source_target_pairs={{0,2},{1,3},{2,0},{3,1},{4,6},{5,7},{6,4},{7,5},{8,10},{9,11},{10,... | collective-permute-start | bytes 393224 | tf_op jit(solution)/shard_map/ppermute | solution.py:22
  10.9 1.1 %collective-permute-start.4 = (bf16[128,1024]{1,0:T(8,128)(2,1)S(1)}, bf16[128,1024]{1,0:T(8,128)(2,1)S(1)}, u32[]{:S(2)}, u32[]{:S(2)}) collective-permute-start(bf16[128,1024]{1,0:T(8,128)(2,1)S(1)} %get-tuple-element.84), channel_id=1, source_target_pairs={{0,2},{1,3},{2,0},{3,1},{4,6},{5,7},{6,4},{7,5},{8,10},{9,11},{10,... | collective-permute-start | bytes 786440 | tf_op jit(solution)/shard_map/ppermute | solution.py:22
  12.0 1.5 %collective-permute-start.5 = (bf16[128,1024]{1,0:T(8,128)(2,1)S(1)}, bf16[128,1024]{1,0:T(8,128)(2,1)S(1)}, u32[]{:S(2)}, u32[]{:S(2)}) collective-permute-start(bf16[128,1024]{1,0:T(8,128)(2,1)S(1)} %get-tuple-element.85), channel_id=1, source_target_pairs={{0,4},{1,5},{2,6},{3,7},{4,0},{5,1},{6,2},{7,3},{8,12},{9,13},{10,... | collective-permute-start | bytes 786440 | tf_op jit(solution)/shard_map/ppermute | solution.py:22
  14.7 1.4 %collective-permute-done.7.refs_6_ = bf16[128,512]{1,0:T(8,128)(2,1)} collective-permute-done((bf16[128,512]{1,0:T(8,128)(2,1)S(1)}, bf16[128,512]{1,0:T(8,128)(2,1)}, u32[]{:S(2)}, u32[]{:S(2)}) %collective-permute-start.7) | collective-permute-done | bytes 131104 | tf_op jit(solution)/shard_map/ppermute | solution.py:22
  16.1 1.2 %copy-done.2 = bf16[1,128,4096]{2,1,0:T(8,128)(2,1)S(1)} copy-done((bf16[1,128,4096]{2,1,0:T(8,128)(2,1)S(1)}, bf16[1,128,4096]{2,1,0:T(8,128)(2,1)}, u32[]{:S(2)}) %copy-start.2) | copy-done | bytes 1048600
  17.4 9.6 %attention.2 = (bf16[128,1024]{1,0:T(8,128)(2,1)S(1)}, bf16[128,1024]{1,0:T(8,128)(2,1)S(1)}, bf16[128,2048]{1,0:T(8,128)(2,1)S(1)}, bf16[128,1024]{1,0:T(8,128)...) custom-call(s32[2]{0:T(128)S(1)} %pad_add_fusion.where_ref, ...), custom_call_target="tpu_custom_call" | custom-call | flops 6442450944 | bytes 2097152 | tf_op jit(solution)/shard_map/attention/pallas_call | solution.py:228
  27.8 1.0 %collective-permute-start.10 = (bf16[128,1024]{1,0:T(8,128)(2,1)S(1)}, bf16[128,1024]{1,0:T(8,128)(2,1)S(1)}, u32[]{:S(2)}, u32[]{:S(2)}) collective-permute-start(bf16[128,1024]{1,0:T(8,128)(2,1)S(1)} %get-tuple-element.97), channel_id=1, source_target_pairs={{0,2},{1,3},{2,0},{3,1},{4,6},{5,7},{6,4},{7,5},{8,10},{9,11},{10,... | collective-permute-start | bytes 786440 | tf_op jit(solution)/shard_map/ppermute | solution.py:22
  28.9 1.5 %collective-permute-start.11 = (bf16[128,1024]{1,0:T(8,128)(2,1)S(1)}, bf16[128,1024]{1,0:T(8,128)(2,1)S(1)}, u32[]{:S(2)}, u32[]{:S(2)}) collective-permute-start(bf16[128,1024]{1,0:T(8,128)(2,1)S(1)} %get-tuple-element.98), channel_id=1, source_target_pairs={{0,4},{1,5},{2,6},{3,7},{4,0},{5,1},{6,2},{7,3},{8,12},{9,13},{10,... | collective-permute-start | bytes 786440 | tf_op jit(solution)/shard_map/ppermute | solution.py:22
  31.3 10.2 %attention.3 = (bf16[128,1024]{1,0:T(8,128)(2,1)S(1)}, bf16[128,1024]{1,0:T(8,128)(2,1)S(1)}, bf16[128,2048]{1,0:T(8,128)(2,1)S(1)}, bf16[128,512]{1,0:T(8,128)(...) custom-call(s32[2]{0:T(128)S(1)} %pad_add_fusion.where_ref, ...), custom_call_target="tpu_custom_call" | custom-call | flops 268435456 | bytes 2097152 | tf_op jit(solution)/shard_map/attention/pallas_call | solution.py:228
  41.9 1.2 %collective-permute-done.12.refs_3_ = bf16[128,1024]{1,0:T(8,128)(2,1)S(1)} collective-permute-done((bf16[128,1024]{1,0:T(8,128)(2,1)S(1)}, bf16[128,1024]{1,0:T(8,128)(2,1)S(1)}, u32[]{:S(2)}, u32[]{:S(2)}) %collective-permute-start.12) | collective-permute-done | bytes 262176 | tf_op jit(solution)/shard_map/ppermute | solution.py:22
  44.0 1.8 %collective-permute-start.18 = (bf16[128,512]{1,0:T(8,128)(2,1)S(1)}, bf16[128,512]{1,0:T(8,128)(2,1)S(1)}, u32[]{:S(2)}, u32[]{:S(2)}) collective-permute-start(bf16[128,512]{1,0:T(8,128)(2,1)S(1)} %add_convert_fusion.3.refs_0_), channel_id=1, source_target_pairs={{0,6},{1,7},{2,4},{3,5},{4,2},{5,3},{6,0},{7,1},{8,14},{9,15},{10,... | collective-permute-start | bytes 393224 | tf_op jit(solution)/shard_map/ppermute | solution.py:22
  46.5 1.0 %collective-permute-start.16 = (bf16[128,512]{1,0:T(8,128)(2,1)S(1)}, bf16[128,512]{1,0:T(8,128)(2,1)S(1)}, u32[]{:S(2)}, u32[]{:S(2)}) collective-permute-start(bf16[128,512]{1,0:T(8,128)(2,1)S(1)} %add_convert_fusion.3.refs_0_), channel_id=1, source_target_pairs={{0,2},{1,3},{2,0},{3,1},{4,6},{5,7},{6,4},{7,5},{8,10},{9,11},{10,... | collective-permute-start | bytes 393224 | tf_op jit(solution)/shard_map/ppermute | solution.py:22
  47.5 1.0 %collective-permute-start.21 = (bf16[128,512]{1,0:T(8,128)(2,1)}, bf16[128,512]{1,0:T(8,128)(2,1)S(1)}, u32[]{:S(2)}, u32[]{:S(2)}) collective-permute-start(bf16[128,512]{1,0:T(8,128)(2,1)} %get-tuple-element.107), channel_id=1, source_target_pairs={{0,2},{1,3},{2,0},{3,1},{4,6},{5,7},{6,4},{7,5},{8,10},{9,11},{10,... | collective-permute-start | bytes 393224 | tf_op jit(solution)/shard_map/ppermute | solution.py:22
  48.5 2.7 %collective-permute-done.18.refs_3_ = bf16[128,512]{1,0:T(8,128)(2,1)S(1)} collective-permute-done((bf16[128,512]{1,0:T(8,128)(2,1)S(1)}, bf16[128,512]{1,0:T(8,128)(2,1)S(1)}, u32[]{:S(2)}, u32[]{:S(2)}) %collective-permute-start.18) | collective-permute-done | bytes 131104 | tf_op jit(solution)/shard_map/ppermute | solution.py:22
  51.3 1.3 %collective-permute-start.22 = (bf16[128,512]{1,0:T(8,128)(2,1)}, bf16[128,512]{1,0:T(8,128)(2,1)}, u32[]{:S(2)}, u32[]{:S(2)}) collective-permute-start(bf16[128,512]{1,0:T(8,128)(2,1)} %get-tuple-element.108), channel_id=1, source_target_pairs={{0,4},{1,5},{2,6},{3,7},{4,0},{5,1},{6,2},{7,3},{8,12},{9,13},{10,... | collective-permute-start | bytes 393224 | tf_op jit(solution)/shard_map/ppermute | solution.py:22
  52.6 1.1 %collective-permute-done.17.refs_2_ = bf16[128,512]{1,0:T(8,128)(2,1)S(1)} collective-permute-done((bf16[128,512]{1,0:T(8,128)(2,1)S(1)}, bf16[128,512]{1,0:T(8,128)(2,1)S(1)}, u32[]{:S(2)}, u32[]{:S(2)}) %collective-permute-start.17) | collective-permute-done | bytes 131104 | tf_op jit(solution)/shard_map/ppermute | solution.py:22
  53.7 1.8 %collective-permute-start.23 = (bf16[128,512]{1,0:T(8,128)(2,1)S(1)}, bf16[128,512]{1,0:T(8,128)(2,1)}, u32[]{:S(2)}, u32[]{:S(2)}) collective-permute-start(bf16[128,512]{1,0:T(8,128)(2,1)S(1)} %get-tuple-element.109), channel_id=1, source_target_pairs={{0,6},{1,7},{2,4},{3,5},{4,2},{5,3},{6,0},{7,1},{8,14},{9,15},{10,... | collective-permute-start | bytes 393224 | tf_op jit(solution)/shard_map/ppermute | solution.py:22
  56.3 1.6 %collective-permute-start.19 = (bf16[512,256]{1,0:T(8,128)(2,1)S(1)}, bf16[512,256]{1,0:T(8,128)(2,1)S(1)}, u32[]{:S(2)}, u32[]{:S(2)}) collective-permute-start(bf16[512,256]{1,0:T(8,128)(2,1)S(1)} %get-tuple-element.104), channel_id=1, source_target_pairs={{0,8},{8,0},{16,24},{24,16},{1,9},{9,1},{17,25},{25,17},{2,10},{10... | collective-permute-start | bytes 786440 | tf_op jit(solution)/shard_map/ppermute | solution.py:22
  57.9 2.2 %collective-permute-done.23 = bf16[128,512]{1,0:T(8,128)(2,1)} collective-permute-done((bf16[128,512]{1,0:T(8,128)(2,1)S(1)}, bf16[128,512]{1,0:T(8,128)(2,1)}, u32[]{:S(2)}, u32[]{:S(2)}) %collective-permute-start.23) | collective-permute-done | bytes 131104 | tf_op jit(solution)/shard_map/ppermute | solution.py:22
  60.1 1.0 %add_convert_fusion.1.refs_0_ = bf16[128,512]{1,0:T(8,128)(2,1)S(1)} fusion(bf16[128,512]{1,0:T(8,128)(2,1)} %collective-permute-done.23, bf16[128,512]{1,0:T(8,128)(2,1)} %collective-permute-done.22, bf16[128,512]{1,0:T(8,128)(2,1)S(1)} %collective-permute-done.21, bf16[128,512]{1,0:T(8,128)(2,1)S(1)} %get-tuple-element.106), kind=kLoop, calls=%fused_computation.1 | loop fusion | flops 524288 | bytes 655360 | tf_op jit(solution)/shard_map/convert_element_type | solution.py:476
  61.1 1.8 %collective-permute-start.26 = (bf16[128,512]{1,0:T(8,128)(2,1)S(1)}, bf16[128,512]{1,0:T(8,128)(2,1)S(1)}, u32[]{:S(2)}, u32[]{:S(2)}) collective-permute-start(bf16[128,512]{1,0:T(8,128)(2,1)S(1)} %add_convert_fusion.1.refs_0_), channel_id=1, source_target_pairs={{0,6},{1,7},{2,4},{3,5},{4,2},{5,3},{6,0},{7,1},{8,14},{9,15},{10,... | collective-permute-start | bytes 393224 | tf_op jit(solution)/shard_map/ppermute | solution.py:22
  64.7 2.6 %collective-permute-start.20 = (bf16[256,256]{1,0:T(8,128)(2,1)S(1)}, bf16[256,256]{1,0:T(8,128)(2,1)S(1)}, u32[]{:S(2)}, u32[]{:S(2)}) collective-permute-start(bf16[256,256]{1,0:T(8,128)(2,1)S(1)} %add_convert_fusion.2), channel_id=1, source_target_pairs={{0,16},{8,24},{16,0},{24,8},{1,17},{9,25},{17,1},{25,9},{2,18},{10... | collective-permute-start | bytes 393224 | tf_op jit(solution)/shard_map/ppermute | solution.py:22
  68.3 1.1 %collective-permute-done.25.refs_2_ = bf16[128,512]{1,0:T(8,128)(2,1)S(1)} collective-permute-done((bf16[128,512]{1,0:T(8,128)(2,1)S(1)}, bf16[128,512]{1,0:T(8,128)(2,1)S(1)}, u32[]{:S(2)}, u32[]{:S(2)}) %collective-permute-start.25) | collective-permute-done | bytes 131104 | tf_op jit(solution)/shard_map/ppermute | solution.py:22
  70.2 2.0 %collective-permute-done.20.refs_2_ = bf16[256,256]{1,0:T(8,128)(2,1)S(1)} collective-permute-done((bf16[256,256]{1,0:T(8,128)(2,1)S(1)}, bf16[256,256]{1,0:T(8,128)(2,1)S(1)}, u32[]{:S(2)}, u32[]{:S(2)}) %collective-permute-start.20) | collective-permute-done | bytes 131104 | tf_op jit(solution)/shard_map/ppermute | solution.py:22
  72.9 5.7 %collective-permute-done.27.refs_4_ = bf16[512,256]{1,0:T(8,128)(2,1)S(1)} collective-permute-done((bf16[512,256]{1,0:T(8,128)(2,1)S(1)}, bf16[512,256]{1,0:T(8,128)(2,1)S(1)}, u32[]{:S(2)}, u32[]{:S(2)}) %collective-permute-start.27) | collective-permute-done | bytes 262176 | tf_op jit(solution)/shard_map/ppermute | solution.py:22
  78.6 2.6 %collective-permute-start.28 = (bf16[256,256]{1,0:T(8,128)(2,1)S(1)}, bf16[256,256]{1,0:T(8,128)(2,1)S(1)}, u32[]{:S(2)}, u32[]{:S(2)}) collective-permute-start(bf16[256,256]{1,0:T(8,128)(2,1)S(1)} %add_convert_fusion), channel_id=1, source_target_pairs={{0,16},{8,24},{16,0},{24,8},{1,17},{9,25},{17,1},{25,9},{2,18},{10... | collective-permute-start | bytes 393224 | tf_op jit(solution)/shard_map/ppermute | solution.py:22
  82.0 2.9 %join.1 = (bf16[1,128,4096]{2,1,0:T(8,128)(2,1)}, bf16[1,128,4096]{2,1,0:T(8,128)(2,1)}) custom-call(s32[1]{0:T(128)} %bitcast.1.scalar_ref, bf16[128,1024]{1,0:T(8,128)(2,1)} %copy-done.3, bf16[128,1024]{1,0:T(8,128)(2,1)} %copy-done.5, bf16[128,1024]{1,0:T(8,128)(2,1)} %copy-done.4, bf16[128,1024]{1,0:T(8,128)(2,1)} %copy-done.6, ...), custom_call_target="tpu_custom_call" | custom-call | bytes 4000000 | tf_op jit(solution)/shard_map/join/pallas_call | solution.py:389
  86.1 1.5 %collective-permute-done.30.got = f32[128,512]{1,0:T(8,128)S(1)} collective-permute-done((f32[128,512]{1,0:T(8,128)S(1)}, f32[128,512]{1,0:T(8,128)S(1)}, u32[]{:S(2)}, u32[]{:S(2)}) %collective-permute-start.30) | collective-permute-done | bytes 262176 | tf_op jit(solution)/shard_map/ppermute | solution.py:22
  (71 shorter events, 14.6 us)
Async XLA Ops:
  0.6 15.5 %copy-start.1 = (bf16[1,128,4096]{2,1,0:T(8,128)(2,1)S(1)}, bf16[1,128,4096]{2,1,0:T(8,128)(2,1)}, u32[]{:S(2)}) copy-start(bf16[1,128,4096]{2,1,0:T(8,128)(2,1)} %refs_0_.3) | copy-start | bytes 3145732
  1.8 1.7 %collective-permute-start = (bf16[128,1024]{1,0:T(8,128)(2,1)S(1)}, bf16[128,1024]{1,0:T(8,128)(2,1)S(1)}, u32[]{:S(2)}, u32[]{:S(2)}) collective-permute-start(bf16[128,1024]{1,0:T(8,128)(2,1)S(1)} %bitcast.8), channel_id=1, source_target_pairs={{0,1},{1,0},{2,3},{3,2},{4,5},{5,4},{6,7},{7,6},{8,9},{9,8},{10,11... | collective-permute-start | bytes 786440 | tf_op jit(solution)/shard_map/ppermute | solution.py:22
  3.5 7.3 %collective-permute-start.2 = (bf16[1,128,4096]{2,1,0:T(8,128)(2,1)}, bf16[1,128,4096]{2,1,0:T(8,128)(2,1)S(1)}, u32[]{:S(2)}, u32[]{:S(2)}) collective-permute-start(bf16[1,128,4096]{2,1,0:T(8,128)(2,1)} %refs_0_.3), channel_id=1, source_target_pairs={{0,1},{1,0},{2,3},{3,2},{4,5},{5,4},{6,7},{7,6},{8,9},{9,8},{10,11... | collective-permute-start | bytes 3145736 | tf_op jit(solution)/shard_map/ppermute | solution.py:22
  4.0 6.9 %collective-permute-start.3 = (bf16[1,128,4096]{2,1,0:T(8,128)(2,1)}, bf16[1,128,4096]{2,1,0:T(8,128)(2,1)}, u32[]{:S(2)}, u32[]{:S(2)}) collective-permute-start(bf16[1,128,4096]{2,1,0:T(8,128)(2,1)} %refs_2_.1), channel_id=1, source_target_pairs={{0,1},{1,0},{2,3},{3,2},{4,5},{5,4},{6,7},{7,6},{8,9},{9,8},{10,11... | collective-permute-start | bytes 3145736 | tf_op jit(solution)/shard_map/ppermute | solution.py:22
  4.1 9.4 %collective-permute-start.9 = (bf16[128,512]{1,0:T(8,128)(2,1)S(1)}, bf16[128,512]{1,0:T(8,128)(2,1)S(1)}, u32[]{:S(2)}, u32[]{:S(2)}) collective-permute-start(bf16[128,512]{1,0:T(8,128)(2,1)S(1)} %get-tuple-element.75.refs_5_), channel_id=1, source_target_pairs={{0,6},{1,7},{2,4},{3,5},{4,2},{5,3},{6,0},{7,1},{8,14},{9,15},{10,... | collective-permute-start | bytes 393224 | tf_op jit(solution)/shard_map/ppermute | solution.py:22
  7.9 6.8 %collective-permute-start.8 = (bf16[128,512]{1,0:T(8,128)(2,1)S(1)}, bf16[128,512]{1,0:T(8,128)(2,1)}, u32[]{:S(2)}, u32[]{:S(2)}) collective-permute-start(bf16[128,512]{1,0:T(8,128)(2,1)S(1)} %get-tuple-element.75.refs_5_), channel_id=1, source_target_pairs={{0,4},{1,5},{2,6},{3,7},{4,0},{5,1},{6,2},{7,3},{8,12},{9,13},{10,... | collective-permute-start | bytes 393224 | tf_op jit(solution)/shard_map/ppermute | solution.py:22
  8.4 1.3 %collective-permute-start.1 = (s32[1,8]{1,0:T(1,128)}, s32[1,8]{1,0:T(1,128)S(1)}, u32[]{:S(2)}, u32[]{:S(2)}) collective-permute-start(s32[1,8]{1,0:T(1,128)} %bitcast.10), channel_id=1, source_target_pairs={{0,1},{1,0},{2,3},{3,2},{4,5},{5,4},{6,7},{7,6},{8,9},{9,8},{10,11... | collective-permute-start | bytes 104 | tf_op jit(solution)/shard_map/ppermute | solution.py:22
  9.7 6.4 %collective-permute-start.7 = (bf16[128,512]{1,0:T(8,128)(2,1)S(1)}, bf16[128,512]{1,0:T(8,128)(2,1)}, u32[]{:S(2)}, u32[]{:S(2)}) collective-permute-start(bf16[128,512]{1,0:T(8,128)(2,1)S(1)} %get-tuple-element.75.refs_5_), channel_id=1, source_target_pairs={{0,2},{1,3},{2,0},{3,1},{4,6},{5,7},{6,4},{7,5},{8,10},{9,11},{10,... | collective-permute-start | bytes 393224 | tf_op jit(solution)/shard_map/ppermute | solution.py:22
  10.9 16.1 %collective-permute-start.4 = (bf16[128,1024]{1,0:T(8,128)(2,1)S(1)}, bf16[128,1024]{1,0:T(8,128)(2,1)S(1)}, u32[]{:S(2)}, u32[]{:S(2)}) collective-permute-start(bf16[128,1024]{1,0:T(8,128)(2,1)S(1)} %get-tuple-element.84), channel_id=1, source_target_pairs={{0,2},{1,3},{2,0},{3,1},{4,6},{5,7},{6,4},{7,5},{8,10},{9,11},{10,... | collective-permute-start | bytes 786440 | tf_op jit(solution)/shard_map/ppermute | solution.py:22
  12.0 15.1 %collective-permute-start.5 = (bf16[128,1024]{1,0:T(8,128)(2,1)S(1)}, bf16[128,1024]{1,0:T(8,128)(2,1)S(1)}, u32[]{:S(2)}, u32[]{:S(2)}) collective-permute-start(bf16[128,1024]{1,0:T(8,128)(2,1)S(1)} %get-tuple-element.85), channel_id=1, source_target_pairs={{0,4},{1,5},{2,6},{3,7},{4,0},{5,1},{6,2},{7,3},{8,12},{9,13},{10,... | collective-permute-start | bytes 786440 | tf_op jit(solution)/shard_map/ppermute | solution.py:22
  13.5 14.0 %collective-permute-start.6 = (bf16[128,1024]{1,0:T(8,128)(2,1)S(1)}, bf16[128,1024]{1,0:T(8,128)(2,1)S(1)}, u32[]{:S(2)}, u32[]{:S(2)}) collective-permute-start(bf16[128,1024]{1,0:T(8,128)(2,1)S(1)} %get-tuple-element.86), channel_id=1, source_target_pairs={{0,6},{1,7},{2,4},{3,5},{4,2},{5,3},{6,0},{7,1},{8,14},{9,15},{10,... | collective-permute-start | bytes 786440 | tf_op jit(solution)/shard_map/ppermute | solution.py:22
  27.0 16.1 %collective-permute-start.13 = (bf16[128,2048]{1,0:T(8,128)(2,1)S(1)}, bf16[128,2048]{1,0:T(8,128)(2,1)S(1)}, u32[]{:S(2)}, u32[]{:S(2)}) collective-permute-start(bf16[128,2048]{1,0:T(8,128)(2,1)S(1)} %get-tuple-element.87), channel_id=1, source_target_pairs={{0,1},{1,0},{2,3},{3,2},{4,5},{5,4},{6,7},{7,6},{8,9},{9,8},{10,11... | collective-permute-start | bytes 1572872 | tf_op jit(solution)/shard_map/ppermute | solution.py:22
  27.7 15.3 %collective-permute-start.14 = (bf16[512,512]{1,0:T(8,128)(2,1)S(1)}, bf16[512,512]{1,0:T(8,128)(2,1)S(1)}, u32[]{:S(2)}, u32[]{:S(2)}) collective-permute-start(bf16[512,512]{1,0:T(8,128)(2,1)S(1)} %turn.2.own_low), channel_id=1, source_target_pairs={{0,1},{1,0},{2,3},{3,2},{4,5},{5,4},{6,7},{7,6},{8,9},{9,8},{10,11... | collective-permute-start | bytes 1572872 | tf_op jit(solution)/shard_map/ppermute | solution.py:22
  27.8 13.7 %collective-permute-start.10 = (bf16[128,1024]{1,0:T(8,128)(2,1)S(1)}, bf16[128,1024]{1,0:T(8,128)(2,1)S(1)}, u32[]{:S(2)}, u32[]{:S(2)}) collective-permute-start(bf16[128,1024]{1,0:T(8,128)(2,1)S(1)} %get-tuple-element.97), channel_id=1, source_target_pairs={{0,2},{1,3},{2,0},{3,1},{4,6},{5,7},{6,4},{7,5},{8,10},{9,11},{10,... | collective-permute-start | bytes 786440 | tf_op jit(solution)/shard_map/ppermute | solution.py:22
  28.9 13.0 %collective-permute-start.11 = (bf16[128,1024]{1,0:T(8,128)(2,1)S(1)}, bf16[128,1024]{1,0:T(8,128)(2,1)S(1)}, u32[]{:S(2)}, u32[]{:S(2)}) collective-permute-start(bf16[128,1024]{1,0:T(8,128)(2,1)S(1)} %get-tuple-element.98), channel_id=1, source_target_pairs={{0,4},{1,5},{2,6},{3,7},{4,0},{5,1},{6,2},{7,3},{8,12},{9,13},{10,... | collective-permute-start | bytes 786440 | tf_op jit(solution)/shard_map/ppermute | solution.py:22
  30.4 12.7 %collective-permute-start.12 = (bf16[128,1024]{1,0:T(8,128)(2,1)S(1)}, bf16[128,1024]{1,0:T(8,128)(2,1)S(1)}, u32[]{:S(2)}, u32[]{:S(2)}) collective-permute-start(bf16[128,1024]{1,0:T(8,128)(2,1)S(1)} %get-tuple-element.99), channel_id=1, source_target_pairs={{0,6},{1,7},{2,4},{3,5},{4,2},{5,3},{6,0},{7,1},{8,14},{9,15},{10,... | collective-permute-start | bytes 786440 | tf_op jit(solution)/shard_map/ppermute | solution.py:22
  43.9 11.6 %collective-permute-start.15 = (bf16[512,512]{1,0:T(8,128)(2,1)S(1)}, bf16[512,512]{1,0:T(8,128)(2,1)S(1)}, u32[]{:S(2)}, u32[]{:S(2)}) collective-permute-start(bf16[512,512]{1,0:T(8,128)(2,1)S(1)} %turn.3.own_high), channel_id=1, source_target_pairs={{0,1},{1,0},{2,3},{3,2},{4,5},{5,4},{6,7},{7,6},{8,9},{9,8},{10,11... | collective-permute-start | bytes 1572872 | tf_op jit(solution)/shard_map/ppermute | solution.py:22
  44.0 7.3 %collective-permute-start.18 = (bf16[128,512]{1,0:T(8,128)(2,1)S(1)}, bf16[128,512]{1,0:T(8,128)(2,1)S(1)}, u32[]{:S(2)}, u32[]{:S(2)}) collective-permute-start(bf16[128,512]{1,0:T(8,128)(2,1)S(1)} %add_convert_fusion.3.refs_0_), channel_id=1, source_target_pairs={{0,6},{1,7},{2,4},{3,5},{4,2},{5,3},{6,0},{7,1},{8,14},{9,15},{10,... | collective-permute-start | bytes 393224 | tf_op jit(solution)/shard_map/ppermute | solution.py:22
  45.8 7.9 %collective-permute-start.17 = (bf16[128,512]{1,0:T(8,128)(2,1)S(1)}, bf16[128,512]{1,0:T(8,128)(2,1)S(1)}, u32[]{:S(2)}, u32[]{:S(2)}) collective-permute-start(bf16[128,512]{1,0:T(8,128)(2,1)S(1)} %add_convert_fusion.3.refs_0_), channel_id=1, source_target_pairs={{0,4},{1,5},{2,6},{3,7},{4,0},{5,1},{6,2},{7,3},{8,12},{9,13},{10,... | collective-permute-start | bytes 393224 | tf_op jit(solution)/shard_map/ppermute | solution.py:22
  46.5 9.0 %collective-permute-start.16 = (bf16[128,512]{1,0:T(8,128)(2,1)S(1)}, bf16[128,512]{1,0:T(8,128)(2,1)S(1)}, u32[]{:S(2)}, u32[]{:S(2)}) collective-permute-start(bf16[128,512]{1,0:T(8,128)(2,1)S(1)} %add_convert_fusion.3.refs_0_), channel_id=1, source_target_pairs={{0,2},{1,3},{2,0},{3,1},{4,6},{5,7},{6,4},{7,5},{8,10},{9,11},{10,... | collective-permute-start | bytes 393224 | tf_op jit(solution)/shard_map/ppermute | solution.py:22
  47.5 10.4 %collective-permute-start.21 = (bf16[128,512]{1,0:T(8,128)(2,1)}, bf16[128,512]{1,0:T(8,128)(2,1)S(1)}, u32[]{:S(2)}, u32[]{:S(2)}) collective-permute-start(bf16[128,512]{1,0:T(8,128)(2,1)} %get-tuple-element.107), channel_id=1, source_target_pairs={{0,2},{1,3},{2,0},{3,1},{4,6},{5,7},{6,4},{7,5},{8,10},{9,11},{10,... | collective-permute-start | bytes 393224 | tf_op jit(solution)/shard_map/ppermute | solution.py:22
  51.3 6.7 %collective-permute-start.22 = (bf16[128,512]{1,0:T(8,128)(2,1)}, bf16[128,512]{1,0:T(8,128)(2,1)}, u32[]{:S(2)}, u32[]{:S(2)}) collective-permute-start(bf16[128,512]{1,0:T(8,128)(2,1)} %get-tuple-element.108), channel_id=1, source_target_pairs={{0,4},{1,5},{2,6},{3,7},{4,0},{5,1},{6,2},{7,3},{8,12},{9,13},{10,... | collective-permute-start | bytes 393224 | tf_op jit(solution)/shard_map/ppermute | solution.py:22
  53.7 6.4 %collective-permute-start.23 = (bf16[128,512]{1,0:T(8,128)(2,1)S(1)}, bf16[128,512]{1,0:T(8,128)(2,1)}, u32[]{:S(2)}, u32[]{:S(2)}) collective-permute-start(bf16[128,512]{1,0:T(8,128)(2,1)S(1)} %get-tuple-element.109), channel_id=1, source_target_pairs={{0,6},{1,7},{2,4},{3,5},{4,2},{5,3},{6,0},{7,1},{8,14},{9,15},{10,... | collective-permute-start | bytes 393224 | tf_op jit(solution)/shard_map/ppermute | solution.py:22
  56.3 8.4 %collective-permute-start.19 = (bf16[512,256]{1,0:T(8,128)(2,1)S(1)}, bf16[512,256]{1,0:T(8,128)(2,1)S(1)}, u32[]{:S(2)}, u32[]{:S(2)}) collective-permute-start(bf16[512,256]{1,0:T(8,128)(2,1)S(1)} %get-tuple-element.104), channel_id=1, source_target_pairs={{0,8},{8,0},{16,24},{24,16},{1,9},{9,1},{17,25},{25,17},{2,10},{10... | collective-permute-start | bytes 786440 | tf_op jit(solution)/shard_map/ppermute | solution.py:22
  61.1 7.2 %collective-permute-start.26 = (bf16[128,512]{1,0:T(8,128)(2,1)S(1)}, bf16[128,512]{1,0:T(8,128)(2,1)S(1)}, u32[]{:S(2)}, u32[]{:S(2)}) collective-permute-start(bf16[128,512]{1,0:T(8,128)(2,1)S(1)} %add_convert_fusion.1.refs_0_), channel_id=1, source_target_pairs={{0,6},{1,7},{2,4},{3,5},{4,2},{5,3},{6,0},{7,1},{8,14},{9,15},{10,... | collective-permute-start | bytes 393224 | tf_op jit(solution)/shard_map/ppermute | solution.py:22
  62.9 6.5 %collective-permute-start.25 = (bf16[128,512]{1,0:T(8,128)(2,1)S(1)}, bf16[128,512]{1,0:T(8,128)(2,1)S(1)}, u32[]{:S(2)}, u32[]{:S(2)}) collective-permute-start(bf16[128,512]{1,0:T(8,128)(2,1)S(1)} %add_convert_fusion.1.refs_0_), channel_id=1, source_target_pairs={{0,4},{1,5},{2,6},{3,7},{4,0},{5,1},{6,2},{7,3},{8,12},{9,13},{10,... | collective-permute-start | bytes 393224 | tf_op jit(solution)/shard_map/ppermute | solution.py:22
  63.7 5.8 %collective-permute-start.24 = (bf16[128,512]{1,0:T(8,128)(2,1)S(1)}, bf16[128,512]{1,0:T(8,128)(2,1)S(1)}, u32[]{:S(2)}, u32[]{:S(2)}) collective-permute-start(bf16[128,512]{1,0:T(8,128)(2,1)S(1)} %add_convert_fusion.1.refs_0_), channel_id=1, source_target_pairs={{0,2},{1,3},{2,0},{3,1},{4,6},{5,7},{6,4},{7,5},{8,10},{9,11},{10,... | collective-permute-start | bytes 393224 | tf_op jit(solution)/shard_map/ppermute | solution.py:22
  64.7 7.5 %collective-permute-start.20 = (bf16[256,256]{1,0:T(8,128)(2,1)S(1)}, bf16[256,256]{1,0:T(8,128)(2,1)S(1)}, u32[]{:S(2)}, u32[]{:S(2)}) collective-permute-start(bf16[256,256]{1,0:T(8,128)(2,1)S(1)} %add_convert_fusion.2), channel_id=1, source_target_pairs={{0,16},{8,24},{16,0},{24,8},{1,17},{9,25},{17,1},{25,9},{2,18},{10... | collective-permute-start | bytes 393224 | tf_op jit(solution)/shard_map/ppermute | solution.py:22
  72.2 6.4 %collective-permute-start.27 = (bf16[512,256]{1,0:T(8,128)(2,1)S(1)}, bf16[512,256]{1,0:T(8,128)(2,1)S(1)}, u32[]{:S(2)}, u32[]{:S(2)}) collective-permute-start(bf16[512,256]{1,0:T(8,128)(2,1)S(1)} %get-tuple-element.116), channel_id=1, source_target_pairs={{0,8},{8,0},{16,24},{24,16},{1,9},{9,1},{17,25},{25,17},{2,10},{10... | collective-permute-start | bytes 786440 | tf_op jit(solution)/shard_map/ppermute | solution.py:22
  72.9 8.4 %collective-permute-start.29 = (bf16[128,2048]{1,0:T(8,128)(2,1)S(1)}, bf16[128,2048]{1,0:T(8,128)(2,1)S(1)}, u32[]{:S(2)}, u32[]{:S(2)}) collective-permute-start(bf16[128,2048]{1,0:T(8,128)(2,1)S(1)} %copy-done.9), channel_id=1, source_target_pairs={{0,1},{1,0},{2,3},{3,2},{4,5},{5,4},{6,7},{7,6},{8,9},{9,8},{10,11... | collective-permute-start | bytes 1572872 | tf_op jit(solution)/shard_map/ppermute | solution.py:22
  78.6 7.3 %collective-permute-start.28 = (bf16[256,256]{1,0:T(8,128)(2,1)S(1)}, bf16[256,256]{1,0:T(8,128)(2,1)S(1)}, u32[]{:S(2)}, u32[]{:S(2)}) collective-permute-start(bf16[256,256]{1,0:T(8,128)(2,1)S(1)} %add_convert_fusion), channel_id=1, source_target_pairs={{0,16},{8,24},{16,0},{24,8},{1,17},{9,25},{17,1},{25,9},{2,18},{10... | collective-permute-start | bytes 393224 | tf_op jit(solution)/shard_map/ppermute | solution.py:22
  86.0 1.6 %collective-permute-start.30 = (f32[128,512]{1,0:T(8,128)S(1)}, f32[128,512]{1,0:T(8,128)S(1)}, u32[]{:S(2)}, u32[]{:S(2)}) collective-permute-start(f32[128,512]{1,0:T(8,128)S(1)} %get-tuple-element.141), channel_id=1, source_target_pairs={{0,1},{1,0},{2,3},{3,2},{4,5},{5,4},{6,7},{7,6},{8,9},{9,8},{10,11... | collective-permute-start | bytes 786440 | tf_op jit(solution)/shard_map/ppermute | solution.py:22
  (11 other events, 28.3 us)

commit v5 on v4

--- a/solution.py
+++ b/solution.py
@@ -354,7 +354,7 @@
     for first, out in ((core * size, keep), ((1 - core) * size, send)):
         for j in range(2):
             total = None
-            for ref, start in zip(parts[j * count : (j + 1) * count], starts):
+            for ref, start in zip(parts[j * count : (j + 1) * count], starts[j]):
                 part = ref[pl.ds(pl.multiple_of(first + start, size), size), :].astype(jnp.float32)
                 total = part if total is None else total + part
             out[:, j * 2 * HEAD_DIM : (j + 1) * 2 * HEAD_DIM] = total
@@ -485,7 +485,7 @@
     plan = [[0], [2], [3, 1]] if pairwise else [[k] for k in range(data_size)]
     kinds = [high, high, low] if pairwise else [high] + [low] * (data_size - 1)
 
-    def product(grads):
+    def product(grads, plan, kinds):
         return small_call(
             functools.partial(product_kernel, plan, scale),
             "product",
@@ -501,24 +501,28 @@
     folded = 4 * HEAD_DIM
     all_a = gathered(owned(packed_a[0][:, :folded], [x[:, :folded] for x in back_a]))
     all_b = gathered(owned(grads_b[0], back_b))
-    chunks_a = product(all_a)
+    chunks_a = product(all_a, plan, kinds)
     all_b = hold(all_b, chunks_a)
-    chunks_b = product(all_b)
+    if pairwise:
+        plan, kinds = [[0], [2], [3], [1]], [high, high, low, low]
+    chunks_b = product(all_b, plan, kinds)
     if pairwise:
         near_a = swap(chunks_a[2], "dp", 1)
         cross_a = (chunks_a[1] + near_a[:size].astype(high)).astype(low)
         far_a = swap(cross_a, "dp", 2)
         near_b = swap(hold(chunks_b[2], far_a), "dp", 1)
-        cross_b = (chunks_b[1] + near_b[:size].astype(high)).astype(low)
-        arrived = [[near_a, far_a], [near_b, swap(cross_b, "dp", 2)]]
-        starts = [0, size, 0]
+        cross_b = (chunks_b[1] + near_b.astype(high)).astype(low)
+        far_b = swap(cross_b, "dp", 2)
+        beside = swap(hold(chunks_b[3], cross_b), "dp", 1)
+        arrived = [[near_a, far_a], [beside, far_b]]
+        starts = [[0, size, 0], [0, 0, 0]]
     else:
         arrived = [[swap(x[k], "dp", k) for k in range(1, data_size)] for x in (chunks_a, chunks_b)]
         cross_b = chunks_b[0]
-        starts = [0] * data_size
-    got_b = swap(hold(outs_b[2], chunks_b), "ctx", 1)
+        starts = [[0] * data_size] * 2
+    got_b = swap(hold(outs_b[2], chunks_a), "ctx", 1)
     parts = [outs_a[0], outs_b[0], outs_a[1], outs_b[1], got_a, got_b]
-    attn_out, query_grad = join(core_scalar, hold(parts, cross_b), queries.shape)
+    attn_out, query_grad = join(core_scalar, hold(parts, arrived[0], chunks_b), queries.shape)
     arrived, attn_out, query_grad = lax.optimization_barrier((arrived, attn_out, query_grad))
     kept, sent = small_call(
         functools.partial(settle_kernel, starts),

time: 88.7 us -> 88.4 us (level)
  starting transfers between devices: 32.6 us -> 33.6 us
  other arithmetic: 1.25 us -> 0.28 us
    ppermute x31 -> x32, starting transfers between devices: 32.6 us -> 33.6 us  [swap(): return lax.ppermute(value, axis, pairs)]
    convert_element_type x2, other arithmetic: 1.12 us -> 0.16 us  [owned(): return total.astype(low)]
    ppermute x31 -> x32, waiting for transfers between devices: 24.3 us -> 23.8 us  [swap(): return lax.ppermute(value, axis, pairs)]
  transfers between devices with their start and end apart: 31 -> 32, of which waited for: 16 -> 17; matrix products, arithmetic and copies ran while one was open for 1% -> 0% of each run, Pallas kernels for 28% -> 28%
where the time goes in v5:
time: 88.4 us; the launch traced here: 88.1 us
  starting transfers between devices  33.6 us (38%)
  Pallas kernels  25.7 us (29%)
  waiting for transfers between devices  23.8 us (27%)
  local copies, waits for them, and re-layouts  3.83 us (4%)
    ppermute x32, starting transfers between devices, swap(): return lax.ppermute(value, axis, pairs)  33.6 us
    ppermute x32, waiting for transfers between devices, swap(): return lax.ppermute(value, axis, pairs)  23.8 us
    pallas_call x2, Pallas kernels, attention(): pl.pallas_call(functools.partial(attention_kernel, pieces, blocks_here, s...  19.8 us
    unnamed x25, local copies, waits for them, and re-layouts  3.83 us
    pallas_call x8, Pallas kernels, small_call(): pl.pallas_call(kernel, grid=(1,) if streamed else (), in_specs=[pl.BlockS...  2.99 us
    pallas_call x1, Pallas kernels, join(): pl.pallas_call(join_kernel, in_specs=[pl.BlockSpec(memory_space=pltpu.SME...  2.88 us
  transfers between devices with their start and end apart: 32, of which 17 were waited for; matrix products, arithmetic and copies ran while one was open for 0% of the time, Pallas kernels for 28%

profile of v5, /device:TPU:0, one launch (start us, length us, event | category | flops | bytes accessed | tf_op | source)
XLA Modules:
  0.0 88.1 jit_solution(1573658265079989263)
XLA Ops:
  0.7 1.1 %copy.9 = bf16[16,8,2,512]{3,1,2,0:T(8,128)(2,1)S(1)} copy(bf16[16,8,2,512]{3,2,1,0:T(2,128)(2,1)} %bitcast.13) | data formatting | bytes 524288
  2.3 1.2 %collective-permute-done.peer = bf16[128,1024]{1,0:T(8,128)(2,1)S(1)} collective-permute-done((bf16[128,1024]{1,0:T(8,128)(2,1)S(1)}, bf16[128,1024]{1,0:T(8,128)(2,1)S(1)}, u32[]{:S(2)}, u32[]{:S(2)}) %collective-permute-start) | collective-permute-done | bytes 262176 | tf_op jit(solution)/shard_map/ppermute | solution.py:22
  4.1 3.8 %collective-permute-start.9 = (bf16[128,512]{1,0:T(8,128)(2,1)S(1)}, bf16[128,512]{1,0:T(8,128)(2,1)S(1)}, u32[]{:S(2)}, u32[]{:S(2)}) collective-permute-start(bf16[128,512]{1,0:T(8,128)(2,1)S(1)} %get-tuple-element.77.refs_5_), channel_id=1, source_target_pairs={{0,6},{1,7},{2,4},{3,5},{4,2},{5,3},{6,0},{7,1},{8,14},{9,15},{10,... | collective-permute-start | bytes 393224 | tf_op jit(solution)/shard_map/ppermute | solution.py:22
  8.4 1.3 %collective-permute-done.1.peer_mask = s32[1,8]{1,0:T(1,128)S(1)} collective-permute-done((s32[1,8]{1,0:T(1,128)}, s32[1,8]{1,0:T(1,128)S(1)}, u32[]{:S(2)}, u32[]{:S(2)}) %collective-permute-start.1) | collective-permute-done | bytes 64 | tf_op jit(solution)/shard_map/ppermute | solution.py:22
  9.7 1.0 %collective-permute-start.7 = (bf16[128,512]{1,0:T(8,128)(2,1)S(1)}, bf16[128,512]{1,0:T(8,128)(2,1)}, u32[]{:S(2)}, u32[]{:S(2)}) collective-permute-start(bf16[128,512]{1,0:T(8,128)(2,1)S(1)} %get-tuple-element.77.refs_5_), channel_id=1, source_target_pairs={{0,2},{1,3},{2,0},{3,1},{4,6},{5,7},{6,4},{7,5},{8,10},{9,11},{10,... | collective-permute-start | bytes 393224 | tf_op jit(solution)/shard_map/ppermute | solution.py:22
  10.9 1.1 %collective-permute-start.4 = (bf16[128,1024]{1,0:T(8,128)(2,1)S(1)}, bf16[128,1024]{1,0:T(8,128)(2,1)S(1)}, u32[]{:S(2)}, u32[]{:S(2)}) collective-permute-start(bf16[128,1024]{1,0:T(8,128)(2,1)S(1)} %get-tuple-element.86), channel_id=1, source_target_pairs={{0,2},{1,3},{2,0},{3,1},{4,6},{5,7},{6,4},{7,5},{8,10},{9,11},{10,... | collective-permute-start | bytes 786440 | tf_op jit(solution)/shard_map/ppermute | solution.py:22
  12.0 1.5 %collective-permute-start.5 = (bf16[128,1024]{1,0:T(8,128)(2,1)S(1)}, bf16[128,1024]{1,0:T(8,128)(2,1)S(1)}, u32[]{:S(2)}, u32[]{:S(2)}) collective-permute-start(bf16[128,1024]{1,0:T(8,128)(2,1)S(1)} %get-tuple-element.87), channel_id=1, source_target_pairs={{0,4},{1,5},{2,6},{3,7},{4,0},{5,1},{6,2},{7,3},{8,12},{9,13},{10,... | collective-permute-start | bytes 786440 | tf_op jit(solution)/shard_map/ppermute | solution.py:22
  14.7 1.4 %collective-permute-done.7.refs_6_ = bf16[128,512]{1,0:T(8,128)(2,1)} collective-permute-done((bf16[128,512]{1,0:T(8,128)(2,1)S(1)}, bf16[128,512]{1,0:T(8,128)(2,1)}, u32[]{:S(2)}, u32[]{:S(2)}) %collective-permute-start.7) | collective-permute-done | bytes 131104 | tf_op jit(solution)/shard_map/ppermute | solution.py:22
  16.1 1.2 %copy-done.2 = bf16[1,128,4096]{2,1,0:T(8,128)(2,1)S(1)} copy-done((bf16[1,128,4096]{2,1,0:T(8,128)(2,1)S(1)}, bf16[1,128,4096]{2,1,0:T(8,128)(2,1)}, u32[]{:S(2)}) %copy-start.2) | copy-done | bytes 1048600
  17.4 9.6 %attention.2 = (bf16[128,1024]{1,0:T(8,128)(2,1)S(1)}, bf16[128,1024]{1,0:T(8,128)(2,1)S(1)}, bf16[128,2048]{1,0:T(8,128)(2,1)S(1)}, bf16[128,1024]{1,0:T(8,128)...) custom-call(s32[2]{0:T(128)S(1)} %pad_add_fusion.where_ref, ...), custom_call_target="tpu_custom_call" | custom-call | flops 6442450944 | bytes 2097152 | tf_op jit(solution)/shard_map/attention/pallas_call | solution.py:228
  27.8 1.0 %collective-permute-start.10 = (bf16[128,1024]{1,0:T(8,128)(2,1)S(1)}, bf16[128,1024]{1,0:T(8,128)(2,1)S(1)}, u32[]{:S(2)}, u32[]{:S(2)}) collective-permute-start(bf16[128,1024]{1,0:T(8,128)(2,1)S(1)} %get-tuple-element.99), channel_id=1, source_target_pairs={{0,2},{1,3},{2,0},{3,1},{4,6},{5,7},{6,4},{7,5},{8,10},{9,11},{10,... | collective-permute-start | bytes 786440 | tf_op jit(solution)/shard_map/ppermute | solution.py:22
  28.9 1.5 %collective-permute-start.11 = (bf16[128,1024]{1,0:T(8,128)(2,1)S(1)}, bf16[128,1024]{1,0:T(8,128)(2,1)S(1)}, u32[]{:S(2)}, u32[]{:S(2)}) collective-permute-start(bf16[128,1024]{1,0:T(8,128)(2,1)S(1)} %get-tuple-element.100), channel_id=1, source_target_pairs={{0,4},{1,5},{2,6},{3,7},{4,0},{5,1},{6,2},{7,3},{8,12},{9,13},{10,... | collective-permute-start | bytes 786440 | tf_op jit(solution)/shard_map/ppermute | solution.py:22
  31.3 10.2 %attention.3 = (bf16[128,1024]{1,0:T(8,128)(2,1)S(1)}, bf16[128,1024]{1,0:T(8,128)(2,1)S(1)}, bf16[128,2048]{1,0:T(8,128)(2,1)S(1)}, bf16[128,512]{1,0:T(8,128)(...) custom-call(s32[2]{0:T(128)S(1)} %pad_add_fusion.where_ref, ...), custom_call_target="tpu_custom_call" | custom-call | flops 268435456 | bytes 2097152 | tf_op jit(solution)/shard_map/attention/pallas_call | solution.py:228
  41.9 1.2 %collective-permute-done.12.refs_3_ = bf16[128,1024]{1,0:T(8,128)(2,1)S(1)} collective-permute-done((bf16[128,1024]{1,0:T(8,128)(2,1)S(1)}, bf16[128,1024]{1,0:T(8,128)(2,1)S(1)}, u32[]{:S(2)}, u32[]{:S(2)}) %collective-permute-start.12) | collective-permute-done | bytes 262176 | tf_op jit(solution)/shard_map/ppermute | solution.py:22
  44.0 1.8 %collective-permute-start.18 = (bf16[128,512]{1,0:T(8,128)(2,1)S(1)}, bf16[128,512]{1,0:T(8,128)(2,1)S(1)}, u32[]{:S(2)}, u32[]{:S(2)}) collective-permute-start(bf16[128,512]{1,0:T(8,128)(2,1)S(1)} %add_convert_fusion.3.refs_0_), channel_id=1, source_target_pairs={{0,6},{1,7},{2,4},{3,5},{4,2},{5,3},{6,0},{7,1},{8,14},{9,15},{10,... | collective-permute-start | bytes 393224 | tf_op jit(solution)/shard_map/ppermute | solution.py:22
  46.5 1.0 %collective-permute-start.16 = (bf16[128,512]{1,0:T(8,128)(2,1)S(1)}, bf16[128,512]{1,0:T(8,128)(2,1)S(1)}, u32[]{:S(2)}, u32[]{:S(2)}) collective-permute-start(bf16[128,512]{1,0:T(8,128)(2,1)S(1)} %add_convert_fusion.3.refs_0_), channel_id=1, source_target_pairs={{0,2},{1,3},{2,0},{3,1},{4,6},{5,7},{6,4},{7,5},{8,10},{9,11},{10,... | collective-permute-start | bytes 393224 | tf_op jit(solution)/shard_map/ppermute | solution.py:22
  47.5 1.0 %collective-permute-start.21 = (bf16[128,512]{1,0:T(8,128)(2,1)}, bf16[128,512]{1,0:T(8,128)(2,1)S(1)}, u32[]{:S(2)}, u32[]{:S(2)}) collective-permute-start(bf16[128,512]{1,0:T(8,128)(2,1)} %get-tuple-element.109), channel_id=1, source_target_pairs={{0,2},{1,3},{2,0},{3,1},{4,6},{5,7},{6,4},{7,5},{8,10},{9,11},{10,... | collective-permute-start | bytes 393224 | tf_op jit(solution)/shard_map/ppermute | solution.py:22
  48.5 2.7 %collective-permute-done.18.refs_3_ = bf16[128,512]{1,0:T(8,128)(2,1)S(1)} collective-permute-done((bf16[128,512]{1,0:T(8,128)(2,1)S(1)}, bf16[128,512]{1,0:T(8,128)(2,1)S(1)}, u32[]{:S(2)}, u32[]{:S(2)}) %collective-permute-start.18) | collective-permute-done | bytes 131104 | tf_op jit(solution)/shard_map/ppermute | solution.py:22
  51.3 1.3 %collective-permute-start.22 = (bf16[128,512]{1,0:T(8,128)(2,1)}, bf16[128,512]{1,0:T(8,128)(2,1)S(1)}, u32[]{:S(2)}, u32[]{:S(2)}) collective-permute-start(bf16[128,512]{1,0:T(8,128)(2,1)} %get-tuple-element.110), channel_id=1, source_target_pairs={{0,4},{1,5},{2,6},{3,7},{4,0},{5,1},{6,2},{7,3},{8,12},{9,13},{10,... | collective-permute-start | bytes 393224 | tf_op jit(solution)/shard_map/ppermute | solution.py:22
  52.6 1.1 %collective-permute-done.17.refs_2_ = bf16[128,512]{1,0:T(8,128)(2,1)S(1)} collective-permute-done((bf16[128,512]{1,0:T(8,128)(2,1)S(1)}, bf16[128,512]{1,0:T(8,128)(2,1)S(1)}, u32[]{:S(2)}, u32[]{:S(2)}) %collective-permute-start.17) | collective-permute-done | bytes 131104 | tf_op jit(solution)/shard_map/ppermute | solution.py:22
  53.7 1.8 %collective-permute-start.23 = (bf16[128,512]{1,0:T(8,128)(2,1)S(1)}, bf16[128,512]{1,0:T(8,128)(2,1)S(1)}, u32[]{:S(2)}, u32[]{:S(2)}) collective-permute-start(bf16[128,512]{1,0:T(8,128)(2,1)S(1)} %get-tuple-element.111), channel_id=1, source_target_pairs={{0,6},{1,7},{2,4},{3,5},{4,2},{5,3},{6,0},{7,1},{8,14},{9,15},{10,... | collective-permute-start | bytes 393224 | tf_op jit(solution)/shard_map/ppermute | solution.py:22
  56.3 1.6 %collective-permute-start.19 = (bf16[512,256]{1,0:T(8,128)(2,1)S(1)}, bf16[512,256]{1,0:T(8,128)(2,1)S(1)}, u32[]{:S(2)}, u32[]{:S(2)}) collective-permute-start(bf16[512,256]{1,0:T(8,128)(2,1)S(1)} %get-tuple-element.106), channel_id=1, source_target_pairs={{0,8},{8,0},{16,24},{24,16},{1,9},{9,1},{17,25},{25,17},{2,10},{10... | collective-permute-start | bytes 786440 | tf_op jit(solution)/shard_map/ppermute | solution.py:22
  57.9 2.1 %collective-permute-done.23 = bf16[128,512]{1,0:T(8,128)(2,1)S(1)} collective-permute-done((bf16[128,512]{1,0:T(8,128)(2,1)S(1)}, bf16[128,512]{1,0:T(8,128)(2,1)S(1)}, u32[]{:S(2)}, u32[]{:S(2)}) %collective-permute-start.23) | collective-permute-done | bytes 131104 | tf_op jit(solution)/shard_map/ppermute | solution.py:22
  60.1 1.8 %collective-permute-start.26 = (bf16[128,512]{1,0:T(8,128)(2,1)S(1)}, bf16[128,512]{1,0:T(8,128)(2,1)S(1)}, u32[]{:S(2)}, u32[]{:S(2)}) collective-permute-start(bf16[128,512]{1,0:T(8,128)(2,1)S(1)} %add_convert_fusion.1.refs_0_), channel_id=1, source_target_pairs={{0,6},{1,7},{2,4},{3,5},{4,2},{5,3},{6,0},{7,1},{8,14},{9,15},{10,... | collective-permute-start | bytes 393224 | tf_op jit(solution)/shard_map/ppermute | solution.py:22
  62.6 1.0 %collective-permute-start.24 = (bf16[128,512]{1,0:T(8,128)(2,1)S(1)}, bf16[128,512]{1,0:T(8,128)(2,1)S(1)}, u32[]{:S(2)}, u32[]{:S(2)}) collective-permute-start(bf16[128,512]{1,0:T(8,128)(2,1)S(1)} %add_convert_fusion.1.refs_0_), channel_id=1, source_target_pairs={{0,2},{1,3},{2,0},{3,1},{4,6},{5,7},{6,4},{7,5},{8,10},{9,11},{10,... | collective-permute-start | bytes 393224 | tf_op jit(solution)/shard_map/ppermute | solution.py:22
  64.2 2.6 %collective-permute-start.20 = (bf16[256,256]{1,0:T(8,128)(2,1)S(1)}, bf16[256,256]{1,0:T(8,128)(2,1)S(1)}, u32[]{:S(2)}, u32[]{:S(2)}) collective-permute-start(bf16[256,256]{1,0:T(8,128)(2,1)S(1)} %add_convert_fusion.2), channel_id=1, source_target_pairs={{0,16},{8,24},{16,0},{24,8},{1,17},{9,25},{17,1},{25,9},{2,18},{10... | collective-permute-start | bytes 393224 | tf_op jit(solution)/shard_map/ppermute | solution.py:22
  67.2 1.1 %collective-permute-done.25.refs_2_ = bf16[128,512]{1,0:T(8,128)(2,1)S(1)} collective-permute-done((bf16[128,512]{1,0:T(8,128)(2,1)S(1)}, bf16[128,512]{1,0:T(8,128)(2,1)S(1)}, u32[]{:S(2)}, u32[]{:S(2)}) %collective-permute-start.25) | collective-permute-done | bytes 131104 | tf_op jit(solution)/shard_map/ppermute | solution.py:22
  69.1 3.0 %collective-permute-done.20.refs_2_ = bf16[256,256]{1,0:T(8,128)(2,1)S(1)} collective-permute-done((bf16[256,256]{1,0:T(8,128)(2,1)S(1)}, bf16[256,256]{1,0:T(8,128)(2,1)S(1)}, u32[]{:S(2)}, u32[]{:S(2)}) %collective-permute-start.20) | collective-permute-done | bytes 131104 | tf_op jit(solution)/shard_map/ppermute | solution.py:22
  72.8 4.7 %collective-permute-done.27 = bf16[256,256]{1,0:T(8,128)(2,1)S(1)} collective-permute-done((bf16[256,256]{1,0:T(8,128)(2,1)S(1)}, bf16[256,256]{1,0:T(8,128)(2,1)S(1)}, u32[]{:S(2)}, u32[]{:S(2)}) %collective-permute-start.27) | collective-permute-done | bytes 131104 | tf_op jit(solution)/shard_map/ppermute | solution.py:22
  77.9 3.4 %collective-permute-start.29 = (bf16[256,256]{1,0:T(8,128)(2,1)S(1)}, bf16[256,256]{1,0:T(8,128)(2,1)S(1)}, u32[]{:S(2)}, u32[]{:S(2)}) collective-permute-start(bf16[256,256]{1,0:T(8,128)(2,1)S(1)} %add_convert_fusion), channel_id=1, source_target_pairs={{0,16},{8,24},{16,0},{24,8},{1,17},{9,25},{17,1},{25,9},{2,18},{10... | collective-permute-start | bytes 393224 | tf_op jit(solution)/shard_map/ppermute | solution.py:22
  82.1 2.9 %join.1 = (bf16[1,128,4096]{2,1,0:T(8,128)(2,1)}, bf16[1,128,4096]{2,1,0:T(8,128)(2,1)}) custom-call(s32[1]{0:T(128)} %bitcast.1.scalar_ref, bf16[128,1024]{1,0:T(8,128)(2,1)} %copy-done.3, bf16[128,1024]{1,0:T(8,128)(2,1)} %copy-done.5, bf16[128,1024]{1,0:T(8,128)(2,1)} %copy-done.4, bf16[128,1024]{1,0:T(8,128)(2,1)} %copy-done.6, ...), custom_call_target="tpu_custom_call" | custom-call | bytes 4000000 | tf_op jit(solution)/shard_map/join/pallas_call | solution.py:389
  85.7 1.5 %collective-permute-done.31.got = f32[128,512]{1,0:T(8,128)S(1)} collective-permute-done((f32[128,512]{1,0:T(8,128)S(1)}, f32[128,512]{1,0:T(8,128)S(1)}, u32[]{:S(2)}, u32[]{:S(2)}) %collective-permute-start.31) | collective-permute-done | bytes 262176 | tf_op jit(solution)/shard_map/ppermute | solution.py:22
  (73 shorter events, 13.6 us)
Async XLA Ops:
  1.8 1.7 %collective-permute-start = (bf16[128,1024]{1,0:T(8,128)(2,1)S(1)}, bf16[128,1024]{1,0:T(8,128)(2,1)S(1)}, u32[]{:S(2)}, u32[]{:S(2)}) collective-permute-start(bf16[128,1024]{1,0:T(8,128)(2,1)S(1)} %bitcast.8), channel_id=1, source_target_pairs={{0,1},{1,0},{2,3},{3,2},{4,5},{5,4},{6,7},{7,6},{8,9},{9,8},{10,11... | collective-permute-start | bytes 786440 | tf_op jit(solution)/shard_map/ppermute | solution.py:22
  3.5 7.3 %collective-permute-start.2 = (bf16[1,128,4096]{2,1,0:T(8,128)(2,1)}, bf16[1,128,4096]{2,1,0:T(8,128)(2,1)S(1)}, u32[]{:S(2)}, u32[]{:S(2)}) collective-permute-start(bf16[1,128,4096]{2,1,0:T(8,128)(2,1)} %refs_0_.3), channel_id=1, source_target_pairs={{0,1},{1,0},{2,3},{3,2},{4,5},{5,4},{6,7},{7,6},{8,9},{9,8},{10,11... | collective-permute-start | bytes 3145736 | tf_op jit(solution)/shard_map/ppermute | solution.py:22
  4.0 6.9 %collective-permute-start.3 = (bf16[1,128,4096]{2,1,0:T(8,128)(2,1)}, bf16[1,128,4096]{2,1,0:T(8,128)(2,1)}, u32[]{:S(2)}, u32[]{:S(2)}) collective-permute-start(bf16[1,128,4096]{2,1,0:T(8,128)(2,1)} %refs_2_.1), channel_id=1, source_target_pairs={{0,1},{1,0},{2,3},{3,2},{4,5},{5,4},{6,7},{7,6},{8,9},{9,8},{10,11... | collective-permute-start | bytes 3145736 | tf_op jit(solution)/shard_map/ppermute | solution.py:22
  4.1 9.4 %collective-permute-start.9 = (bf16[128,512]{1,0:T(8,128)(2,1)S(1)}, bf16[128,512]{1,0:T(8,128)(2,1)S(1)}, u32[]{:S(2)}, u32[]{:S(2)}) collective-permute-start(bf16[128,512]{1,0:T(8,128)(2,1)S(1)} %get-tuple-element.77.refs_5_), channel_id=1, source_target_pairs={{0,6},{1,7},{2,4},{3,5},{4,2},{5,3},{6,0},{7,1},{8,14},{9,15},{10,... | collective-permute-start | bytes 393224 | tf_op jit(solution)/shard_map/ppermute | solution.py:22
  7.9 6.8 %collective-permute-start.8 = (bf16[128,512]{1,0:T(8,128)(2,1)S(1)}, bf16[128,512]{1,0:T(8,128)(2,1)}, u32[]{:S(2)}, u32[]{:S(2)}) collective-permute-start(bf16[128,512]{1,0:T(8,128)(2,1)S(1)} %get-tuple-element.77.refs_5_), channel_id=1, source_target_pairs={{0,4},{1,5},{2,6},{3,7},{4,0},{5,1},{6,2},{7,3},{8,12},{9,13},{10,... | collective-permute-start | bytes 393224 | tf_op jit(solution)/shard_map/ppermute | solution.py:22
  8.4 1.3 %collective-permute-start.1 = (s32[1,8]{1,0:T(1,128)}, s32[1,8]{1,0:T(1,128)S(1)}, u32[]{:S(2)}, u32[]{:S(2)}) collective-permute-start(s32[1,8]{1,0:T(1,128)} %bitcast.10), channel_id=1, source_target_pairs={{0,1},{1,0},{2,3},{3,2},{4,5},{5,4},{6,7},{7,6},{8,9},{9,8},{10,11... | collective-permute-start | bytes 104 | tf_op jit(solution)/shard_map/ppermute | solution.py:22
  9.7 6.4 %collective-permute-start.7 = (bf16[128,512]{1,0:T(8,128)(2,1)S(1)}, bf16[128,512]{1,0:T(8,128)(2,1)}, u32[]{:S(2)}, u32[]{:S(2)}) collective-permute-start(bf16[128,512]{1,0:T(8,128)(2,1)S(1)} %get-tuple-element.77.refs_5_), channel_id=1, source_target_pairs={{0,2},{1,3},{2,0},{3,1},{4,6},{5,7},{6,4},{7,5},{8,10},{9,11},{10,... | collective-permute-start | bytes 393224 | tf_op jit(solution)/shard_map/ppermute | solution.py:22
  10.9 16.1 %collective-permute-start.4 = (bf16[128,1024]{1,0:T(8,128)(2,1)S(1)}, bf16[128,1024]{1,0:T(8,128)(2,1)S(1)}, u32[]{:S(2)}, u32[]{:S(2)}) collective-permute-start(bf16[128,1024]{1,0:T(8,128)(2,1)S(1)} %get-tuple-element.86), channel_id=1, source_target_pairs={{0,2},{1,3},{2,0},{3,1},{4,6},{5,7},{6,4},{7,5},{8,10},{9,11},{10,... | collective-permute-start | bytes 786440 | tf_op jit(solution)/shard_map/ppermute | solution.py:22
  12.0 15.1 %collective-permute-start.5 = (bf16[128,1024]{1,0:T(8,128)(2,1)S(1)}, bf16[128,1024]{1,0:T(8,128)(2,1)S(1)}, u32[]{:S(2)}, u32[]{:S(2)}) collective-permute-start(bf16[128,1024]{1,0:T(8,128)(2,1)S(1)} %get-tuple-element.87), channel_id=1, source_target_pairs={{0,4},{1,5},{2,6},{3,7},{4,0},{5,1},{6,2},{7,3},{8,12},{9,13},{10,... | collective-permute-start | bytes 786440 | tf_op jit(solution)/shard_map/ppermute | solution.py:22
  13.5 14.0 %collective-permute-start.6 = (bf16[128,1024]{1,0:T(8,128)(2,1)S(1)}, bf16[128,1024]{1,0:T(8,128)(2,1)S(1)}, u32[]{:S(2)}, u32[]{:S(2)}) collective-permute-start(bf16[128,1024]{1,0:T(8,128)(2,1)S(1)} %get-tuple-element.88), channel_id=1, source_target_pairs={{0,6},{1,7},{2,4},{3,5},{4,2},{5,3},{6,0},{7,1},{8,14},{9,15},{10,... | collective-permute-start | bytes 786440 | tf_op jit(solution)/shard_map/ppermute | solution.py:22
  27.0 16.1 %collective-permute-start.13 = (bf16[128,2048]{1,0:T(8,128)(2,1)S(1)}, bf16[128,2048]{1,0:T(8,128)(2,1)S(1)}, u32[]{:S(2)}, u32[]{:S(2)}) collective-permute-start(bf16[128,2048]{1,0:T(8,128)(2,1)S(1)} %get-tuple-element.89), channel_id=1, source_target_pairs={{0,1},{1,0},{2,3},{3,2},{4,5},{5,4},{6,7},{7,6},{8,9},{9,8},{10,11... | collective-permute-start | bytes 1572872 | tf_op jit(solution)/shard_map/ppermute | solution.py:22
  27.7 15.3 %collective-permute-start.14 = (bf16[512,512]{1,0:T(8,128)(2,1)S(1)}, bf16[512,512]{1,0:T(8,128)(2,1)S(1)}, u32[]{:S(2)}, u32[]{:S(2)}) collective-permute-start(bf16[512,512]{1,0:T(8,128)(2,1)S(1)} %turn.2.own_low), channel_id=1, source_target_pairs={{0,1},{1,0},{2,3},{3,2},{4,5},{5,4},{6,7},{7,6},{8,9},{9,8},{10,11... | collective-permute-start | bytes 1572872 | tf_op jit(solution)/shard_map/ppermute | solution.py:22
  27.8 13.7 %collective-permute-start.10 = (bf16[128,1024]{1,0:T(8,128)(2,1)S(1)}, bf16[128,1024]{1,0:T(8,128)(2,1)S(1)}, u32[]{:S(2)}, u32[]{:S(2)}) collective-permute-start(bf16[128,1024]{1,0:T(8,128)(2,1)S(1)} %get-tuple-element.99), channel_id=1, source_target_pairs={{0,2},{1,3},{2,0},{3,1},{4,6},{5,7},{6,4},{7,5},{8,10},{9,11},{10,... | collective-permute-start | bytes 786440 | tf_op jit(solution)/shard_map/ppermute | solution.py:22
  28.9 13.0 %collective-permute-start.11 = (bf16[128,1024]{1,0:T(8,128)(2,1)S(1)}, bf16[128,1024]{1,0:T(8,128)(2,1)S(1)}, u32[]{:S(2)}, u32[]{:S(2)}) collective-permute-start(bf16[128,1024]{1,0:T(8,128)(2,1)S(1)} %get-tuple-element.100), channel_id=1, source_target_pairs={{0,4},{1,5},{2,6},{3,7},{4,0},{5,1},{6,2},{7,3},{8,12},{9,13},{10,... | collective-permute-start | bytes 786440 | tf_op jit(solution)/shard_map/ppermute | solution.py:22
  30.4 12.7 %collective-permute-start.12 = (bf16[128,1024]{1,0:T(8,128)(2,1)S(1)}, bf16[128,1024]{1,0:T(8,128)(2,1)S(1)}, u32[]{:S(2)}, u32[]{:S(2)}) collective-permute-start(bf16[128,1024]{1,0:T(8,128)(2,1)S(1)} %get-tuple-element.101), channel_id=1, source_target_pairs={{0,6},{1,7},{2,4},{3,5},{4,2},{5,3},{6,0},{7,1},{8,14},{9,15},{10,... | collective-permute-start | bytes 786440 | tf_op jit(solution)/shard_map/ppermute | solution.py:22
  43.9 11.6 %collective-permute-start.15 = (bf16[512,512]{1,0:T(8,128)(2,1)S(1)}, bf16[512,512]{1,0:T(8,128)(2,1)S(1)}, u32[]{:S(2)}, u32[]{:S(2)}) collective-permute-start(bf16[512,512]{1,0:T(8,128)(2,1)S(1)} %turn.3.own_high), channel_id=1, source_target_pairs={{0,1},{1,0},{2,3},{3,2},{4,5},{5,4},{6,7},{7,6},{8,9},{9,8},{10,11... | collective-permute-start | bytes 1572872 | tf_op jit(solution)/shard_map/ppermute | solution.py:22
  44.0 7.3 %collective-permute-start.18 = (bf16[128,512]{1,0:T(8,128)(2,1)S(1)}, bf16[128,512]{1,0:T(8,128)(2,1)S(1)}, u32[]{:S(2)}, u32[]{:S(2)}) collective-permute-start(bf16[128,512]{1,0:T(8,128)(2,1)S(1)} %add_convert_fusion.3.refs_0_), channel_id=1, source_target_pairs={{0,6},{1,7},{2,4},{3,5},{4,2},{5,3},{6,0},{7,1},{8,14},{9,15},{10,... | collective-permute-start | bytes 393224 | tf_op jit(solution)/shard_map/ppermute | solution.py:22
  45.8 7.9 %collective-permute-start.17 = (bf16[128,512]{1,0:T(8,128)(2,1)S(1)}, bf16[128,512]{1,0:T(8,128)(2,1)S(1)}, u32[]{:S(2)}, u32[]{:S(2)}) collective-permute-start(bf16[128,512]{1,0:T(8,128)(2,1)S(1)} %add_convert_fusion.3.refs_0_), channel_id=1, source_target_pairs={{0,4},{1,5},{2,6},{3,7},{4,0},{5,1},{6,2},{7,3},{8,12},{9,13},{10,... | collective-permute-start | bytes 393224 | tf_op jit(solution)/shard_map/ppermute | solution.py:22
  46.5 9.0 %collective-permute-start.16 = (bf16[128,512]{1,0:T(8,128)(2,1)S(1)}, bf16[128,512]{1,0:T(8,128)(2,1)S(1)}, u32[]{:S(2)}, u32[]{:S(2)}) collective-permute-start(bf16[128,512]{1,0:T(8,128)(2,1)S(1)} %add_convert_fusion.3.refs_0_), channel_id=1, source_target_pairs={{0,2},{1,3},{2,0},{3,1},{4,6},{5,7},{6,4},{7,5},{8,10},{9,11},{10,... | collective-permute-start | bytes 393224 | tf_op jit(solution)/shard_map/ppermute | solution.py:22
  47.5 10.4 %collective-permute-start.21 = (bf16[128,512]{1,0:T(8,128)(2,1)}, bf16[128,512]{1,0:T(8,128)(2,1)S(1)}, u32[]{:S(2)}, u32[]{:S(2)}) collective-permute-start(bf16[128,512]{1,0:T(8,128)(2,1)} %get-tuple-element.109), channel_id=1, source_target_pairs={{0,2},{1,3},{2,0},{3,1},{4,6},{5,7},{6,4},{7,5},{8,10},{9,11},{10,... | collective-permute-start | bytes 393224 | tf_op jit(solution)/shard_map/ppermute | solution.py:22
  51.3 6.7 %collective-permute-start.22 = (bf16[128,512]{1,0:T(8,128)(2,1)}, bf16[128,512]{1,0:T(8,128)(2,1)S(1)}, u32[]{:S(2)}, u32[]{:S(2)}) collective-permute-start(bf16[128,512]{1,0:T(8,128)(2,1)} %get-tuple-element.110), channel_id=1, source_target_pairs={{0,4},{1,5},{2,6},{3,7},{4,0},{5,1},{6,2},{7,3},{8,12},{9,13},{10,... | collective-permute-start | bytes 393224 | tf_op jit(solution)/shard_map/ppermute | solution.py:22
  53.7 6.3 %collective-permute-start.23 = (bf16[128,512]{1,0:T(8,128)(2,1)S(1)}, bf16[128,512]{1,0:T(8,128)(2,1)S(1)}, u32[]{:S(2)}, u32[]{:S(2)}) collective-permute-start(bf16[128,512]{1,0:T(8,128)(2,1)S(1)} %get-tuple-element.111), channel_id=1, source_target_pairs={{0,6},{1,7},{2,4},{3,5},{4,2},{5,3},{6,0},{7,1},{8,14},{9,15},{10,... | collective-permute-start | bytes 393224 | tf_op jit(solution)/shard_map/ppermute | solution.py:22
  56.3 7.9 %collective-permute-start.19 = (bf16[512,256]{1,0:T(8,128)(2,1)S(1)}, bf16[512,256]{1,0:T(8,128)(2,1)S(1)}, u32[]{:S(2)}, u32[]{:S(2)}) collective-permute-start(bf16[512,256]{1,0:T(8,128)(2,1)S(1)} %get-tuple-element.106), channel_id=1, source_target_pairs={{0,8},{8,0},{16,24},{24,16},{1,9},{9,1},{17,25},{25,17},{2,10},{10... | collective-permute-start | bytes 786440 | tf_op jit(solution)/shard_map/ppermute | solution.py:22
  60.1 7.2 %collective-permute-start.26 = (bf16[128,512]{1,0:T(8,128)(2,1)S(1)}, bf16[128,512]{1,0:T(8,128)(2,1)S(1)}, u32[]{:S(2)}, u32[]{:S(2)}) collective-permute-start(bf16[128,512]{1,0:T(8,128)(2,1)S(1)} %add_convert_fusion.1.refs_0_), channel_id=1, source_target_pairs={{0,6},{1,7},{2,4},{3,5},{4,2},{5,3},{6,0},{7,1},{8,14},{9,15},{10,... | collective-permute-start | bytes 393224 | tf_op jit(solution)/shard_map/ppermute | solution.py:22
  61.8 6.5 %collective-permute-start.25 = (bf16[128,512]{1,0:T(8,128)(2,1)S(1)}, bf16[128,512]{1,0:T(8,128)(2,1)S(1)}, u32[]{:S(2)}, u32[]{:S(2)}) collective-permute-start(bf16[128,512]{1,0:T(8,128)(2,1)S(1)} %add_convert_fusion.1.refs_0_), channel_id=1, source_target_pairs={{0,4},{1,5},{2,6},{3,7},{4,0},{5,1},{6,2},{7,3},{8,12},{9,13},{10,... | collective-permute-start | bytes 393224 | tf_op jit(solution)/shard_map/ppermute | solution.py:22
  62.6 5.8 %collective-permute-start.24 = (bf16[128,512]{1,0:T(8,128)(2,1)S(1)}, bf16[128,512]{1,0:T(8,128)(2,1)S(1)}, u32[]{:S(2)}, u32[]{:S(2)}) collective-permute-start(bf16[128,512]{1,0:T(8,128)(2,1)S(1)} %add_convert_fusion.1.refs_0_), channel_id=1, source_target_pairs={{0,2},{1,3},{2,0},{3,1},{4,6},{5,7},{6,4},{7,5},{8,10},{9,11},{10,... | collective-permute-start | bytes 393224 | tf_op jit(solution)/shard_map/ppermute | solution.py:22
  64.2 7.9 %collective-permute-start.20 = (bf16[256,256]{1,0:T(8,128)(2,1)S(1)}, bf16[256,256]{1,0:T(8,128)(2,1)S(1)}, u32[]{:S(2)}, u32[]{:S(2)}) collective-permute-start(bf16[256,256]{1,0:T(8,128)(2,1)S(1)} %add_convert_fusion.2), channel_id=1, source_target_pairs={{0,16},{8,24},{16,0},{24,8},{1,17},{9,25},{17,1},{25,9},{2,18},{10... | collective-permute-start | bytes 393224 | tf_op jit(solution)/shard_map/ppermute | solution.py:22
  66.9 14.4 %collective-permute-start.30 = (bf16[128,2048]{1,0:T(8,128)(2,1)S(1)}, bf16[128,2048]{1,0:T(8,128)(2,1)S(1)}, u32[]{:S(2)}, u32[]{:S(2)}) collective-permute-start(bf16[128,2048]{1,0:T(8,128)(2,1)S(1)} %copy-done.9), channel_id=1, source_target_pairs={{0,1},{1,0},{2,3},{3,2},{4,5},{5,4},{6,7},{7,6},{8,9},{9,8},{10,11... | collective-permute-start | bytes 1572872 | tf_op jit(solution)/shard_map/ppermute | solution.py:22
  72.1 5.4 %collective-permute-start.27 = (bf16[256,256]{1,0:T(8,128)(2,1)S(1)}, bf16[256,256]{1,0:T(8,128)(2,1)S(1)}, u32[]{:S(2)}, u32[]{:S(2)}) collective-permute-start(bf16[256,256]{1,0:T(8,128)(2,1)S(1)} %get-tuple-element.120), channel_id=1, source_target_pairs={{0,8},{8,0},{16,24},{24,16},{1,9},{9,1},{17,25},{25,17},{2,10},{10... | collective-permute-start | bytes 393224 | tf_op jit(solution)/shard_map/ppermute | solution.py:22
  77.5 7.4 %collective-permute-start.28 = (bf16[256,256]{1,0:T(8,128)(2,1)S(1)}, bf16[256,256]{1,0:T(8,128)(2,1)S(1)}, u32[]{:S(2)}, u32[]{:S(2)}) collective-permute-start(bf16[256,256]{1,0:T(8,128)(2,1)S(1)} %get-tuple-element.121), channel_id=1, source_target_pairs={{0,8},{8,0},{16,24},{24,16},{1,9},{9,1},{17,25},{25,17},{2,10},{10... | collective-permute-start | bytes 393224 | tf_op jit(solution)/shard_map/ppermute | solution.py:22
  77.9 7.7 %collective-permute-start.29 = (bf16[256,256]{1,0:T(8,128)(2,1)S(1)}, bf16[256,256]{1,0:T(8,128)(2,1)S(1)}, u32[]{:S(2)}, u32[]{:S(2)}) collective-permute-start(bf16[256,256]{1,0:T(8,128)(2,1)S(1)} %add_convert_fusion), channel_id=1, source_target_pairs={{0,16},{8,24},{16,0},{24,8},{1,17},{9,25},{17,1},{25,9},{2,18},{10... | collective-permute-start | bytes 393224 | tf_op jit(solution)/shard_map/ppermute | solution.py:22
  85.7 1.6 %collective-permute-start.31 = (f32[128,512]{1,0:T(8,128)S(1)}, f32[128,512]{1,0:T(8,128)S(1)}, u32[]{:S(2)}, u32[]{:S(2)}) collective-permute-start(f32[128,512]{1,0:T(8,128)S(1)} %get-tuple-element.145), channel_id=1, source_target_pairs={{0,1},{1,0},{2,3},{3,2},{4,5},{5,4},{6,7},{7,6},{8,9},{9,8},{10,11... | collective-permute-start | bytes 786440 | tf_op jit(solution)/shard_map/ppermute | solution.py:22
  (12 other events, 51.0 us)

commit v6 on v5

--- a/solution.py
+++ b/solution.py
@@ -447,7 +447,6 @@
             for k, x in enumerate(packed_a)
         ]
     back_a = [swap(x, "ctx", k) for x, k in zip(packed_a[1:], hops)]
-    got_a = swap(outs_a[2], "ctx", 1)
     pieces_b = hold(pieces_b, outs_a[2])
 
     def turn(parts, streamed):
@@ -464,7 +463,7 @@
     own_low = turn(list(packed_b[:1]) + list(pieces_b[1:]), True)
     peer_low = swap(own_low, "ctx", 1)
     outs_b, grads_b = attention(*heads, pieces_b, 1)
-    grads_b, back_a, got_a, peer_low = lax.optimization_barrier((grads_b, back_a, got_a, peer_low))
+    grads_b, back_a, peer_low = lax.optimization_barrier((grads_b, back_a, peer_low))
     back_b = [swap(x, "ctx", k) for x, k in zip(grads_b[1:], hops)]
     own_high = turn(list(packed_a[:1]) + list(back_a), False)
     peer_high = swap(own_high, "ctx", 1)
@@ -520,6 +519,7 @@
         arrived = [[swap(x[k], "dp", k) for k in range(1, data_size)] for x in (chunks_a, chunks_b)]
         cross_b = chunks_b[0]
         starts = [[0] * data_size] * 2
+    got_a = swap(hold(outs_a[2], chunks_b), "ctx", 1)
     got_b = swap(hold(outs_b[2], chunks_a), "ctx", 1)
     parts = [outs_a[0], outs_b[0], outs_a[1], outs_b[1], got_a, got_b]
     attn_out, query_grad = join(core_scalar, hold(parts, arrived[0], chunks_b), queries.shape)

time: 88.4 us -> 88 us (level)
    unnamed x25 -> x29, local copies, waits for them, and re-layouts: 3.83 us -> 3.59 us
where the time goes in v6:
time: 88 us; the launch traced here: 87.8 us
  starting transfers between devices  34.1 us (39%)
  Pallas kernels  25.7 us (29%)
  waiting for transfers between devices  23.2 us (26%)
  local copies, waits for them, and re-layouts  3.59 us (4%)
  between operations  0.92 us (1%)
    ppermute x32, starting transfers between devices, swap(): return lax.ppermute(value, axis, pairs)  34.1 us
    ppermute x32, waiting for transfers between devices, swap(): return lax.ppermute(value, axis, pairs)  23.2 us
    pallas_call x2, Pallas kernels, attention(): pl.pallas_call(functools.partial(attention_kernel, pieces, blocks_here, s...  19.8 us
    unnamed x29, local copies, waits for them, and re-layouts  3.59 us
    pallas_call x8, Pallas kernels, small_call(): pl.pallas_call(kernel, grid=(1,) if streamed else (), in_specs=[pl.BlockS...  2.99 us
    pallas_call x1, Pallas kernels, join(): pl.pallas_call(join_kernel, in_specs=[pl.BlockSpec(memory_space=pltpu.SME...  2.88 us
  transfers between devices with their start and end apart: 32, of which 17 were waited for; matrix products, arithmetic and copies ran while one was open for 0% of the time, Pallas kernels for 28%

profile of v6, /device:TPU:0, one launch (start us, length us, event | category | flops | bytes accessed | tf_op | source)
XLA Modules:
  0.0 87.8 jit_solution(9956732604885122803)
XLA Ops:
  0.7 1.1 %copy.9 = bf16[16,8,2,512]{3,1,2,0:T(8,128)(2,1)S(1)} copy(bf16[16,8,2,512]{3,2,1,0:T(2,128)(2,1)} %bitcast.13) | data formatting | bytes 524288
  2.3 1.2 %collective-permute-done.peer = bf16[128,1024]{1,0:T(8,128)(2,1)S(1)} collective-permute-done((bf16[128,1024]{1,0:T(8,128)(2,1)S(1)}, bf16[128,1024]{1,0:T(8,128)(2,1)S(1)}, u32[]{:S(2)}, u32[]{:S(2)}) %collective-permute-start) | collective-permute-done | bytes 262176 | tf_op jit(solution)/shard_map/ppermute | solution.py:22
  4.1 3.8 %collective-permute-start.9 = (bf16[128,512]{1,0:T(8,128)(2,1)S(1)}, bf16[128,512]{1,0:T(8,128)(2,1)S(1)}, u32[]{:S(2)}, u32[]{:S(2)}) collective-permute-start(bf16[128,512]{1,0:T(8,128)(2,1)S(1)} %get-tuple-element.77.refs_5_), channel_id=1, source_target_pairs={{0,6},{1,7},{2,4},{3,5},{4,2},{5,3},{6,0},{7,1},{8,14},{9,15},{10,... | collective-permute-start | bytes 393224 | tf_op jit(solution)/shard_map/ppermute | solution.py:22
  8.4 1.3 %collective-permute-done.1.peer_mask = s32[1,8]{1,0:T(1,128)S(1)} collective-permute-done((s32[1,8]{1,0:T(1,128)}, s32[1,8]{1,0:T(1,128)S(1)}, u32[]{:S(2)}, u32[]{:S(2)}) %collective-permute-start.1) | collective-permute-done | bytes 64 | tf_op jit(solution)/shard_map/ppermute | solution.py:22
  9.7 1.0 %collective-permute-start.7 = (bf16[128,512]{1,0:T(8,128)(2,1)S(1)}, bf16[128,512]{1,0:T(8,128)(2,1)}, u32[]{:S(2)}, u32[]{:S(2)}) collective-permute-start(bf16[128,512]{1,0:T(8,128)(2,1)S(1)} %get-tuple-element.77.refs_5_), channel_id=1, source_target_pairs={{0,2},{1,3},{2,0},{3,1},{4,6},{5,7},{6,4},{7,5},{8,10},{9,11},{10,... | collective-permute-start | bytes 393224 | tf_op jit(solution)/shard_map/ppermute | solution.py:22
  10.9 1.1 %collective-permute-start.4 = (bf16[128,1024]{1,0:T(8,128)(2,1)S(1)}, bf16[128,1024]{1,0:T(8,128)(2,1)S(1)}, u32[]{:S(2)}, u32[]{:S(2)}) collective-permute-start(bf16[128,1024]{1,0:T(8,128)(2,1)S(1)} %get-tuple-element.86), channel_id=1, source_target_pairs={{0,2},{1,3},{2,0},{3,1},{4,6},{5,7},{6,4},{7,5},{8,10},{9,11},{10,... | collective-permute-start | bytes 786440 | tf_op jit(solution)/shard_map/ppermute | solution.py:22
  12.0 1.5 %collective-permute-start.5 = (bf16[128,1024]{1,0:T(8,128)(2,1)S(1)}, bf16[128,1024]{1,0:T(8,128)(2,1)S(1)}, u32[]{:S(2)}, u32[]{:S(2)}) collective-permute-start(bf16[128,1024]{1,0:T(8,128)(2,1)S(1)} %get-tuple-element.87), channel_id=1, source_target_pairs={{0,4},{1,5},{2,6},{3,7},{4,0},{5,1},{6,2},{7,3},{8,12},{9,13},{10,... | collective-permute-start | bytes 786440 | tf_op jit(solution)/shard_map/ppermute | solution.py:22
  14.7 1.4 %collective-permute-done.7.refs_6_ = bf16[128,512]{1,0:T(8,128)(2,1)} collective-permute-done((bf16[128,512]{1,0:T(8,128)(2,1)S(1)}, bf16[128,512]{1,0:T(8,128)(2,1)}, u32[]{:S(2)}, u32[]{:S(2)}) %collective-permute-start.7) | collective-permute-done | bytes 131104 | tf_op jit(solution)/shard_map/ppermute | solution.py:22
  16.1 1.2 %copy-done.2 = bf16[1,128,4096]{2,1,0:T(8,128)(2,1)S(1)} copy-done((bf16[1,128,4096]{2,1,0:T(8,128)(2,1)S(1)}, bf16[1,128,4096]{2,1,0:T(8,128)(2,1)}, u32[]{:S(2)}) %copy-start.2) | copy-done | bytes 1048600
  17.4 9.6 %attention.2 = (bf16[128,1024]{1,0:T(8,128)(2,1)S(1)}, bf16[128,1024]{1,0:T(8,128)(2,1)S(1)}, bf16[128,2048]{1,0:T(8,128)(2,1)S(1)}, bf16[128,1024]{1,0:T(8,128)...) custom-call(s32[2]{0:T(128)S(1)} %pad_add_fusion.where_ref, ...), custom_call_target="tpu_custom_call" | custom-call | flops 6442450944 | bytes 2097152 | tf_op jit(solution)/shard_map/attention/pallas_call | solution.py:228
  27.9 1.0 %collective-permute-start.10 = (bf16[128,1024]{1,0:T(8,128)(2,1)S(1)}, bf16[128,1024]{1,0:T(8,128)(2,1)S(1)}, u32[]{:S(2)}, u32[]{:S(2)}) collective-permute-start(bf16[128,1024]{1,0:T(8,128)(2,1)S(1)} %get-tuple-element.99), channel_id=1, source_target_pairs={{0,2},{1,3},{2,0},{3,1},{4,6},{5,7},{6,4},{7,5},{8,10},{9,11},{10,... | collective-permute-start | bytes 786440 | tf_op jit(solution)/shard_map/ppermute | solution.py:22
  29.0 1.5 %collective-permute-start.11 = (bf16[128,1024]{1,0:T(8,128)(2,1)S(1)}, bf16[128,1024]{1,0:T(8,128)(2,1)S(1)}, u32[]{:S(2)}, u32[]{:S(2)}) collective-permute-start(bf16[128,1024]{1,0:T(8,128)(2,1)S(1)} %get-tuple-element.100), channel_id=1, source_target_pairs={{0,4},{1,5},{2,6},{3,7},{4,0},{5,1},{6,2},{7,3},{8,12},{9,13},{10,... | collective-permute-start | bytes 786440 | tf_op jit(solution)/shard_map/ppermute | solution.py:22
  31.4 10.2 %attention.3 = (bf16[128,1024]{1,0:T(8,128)(2,1)S(1)}, bf16[128,1024]{1,0:T(8,128)(2,1)S(1)}, bf16[128,2048]{1,0:T(8,128)(2,1)S(1)}, bf16[128,512]{1,0:T(8,128)(...) custom-call(s32[2]{0:T(128)S(1)} %pad_add_fusion.where_ref, ...), custom_call_target="tpu_custom_call" | custom-call | flops 268435456 | bytes 2097152 | tf_op jit(solution)/shard_map/attention/pallas_call | solution.py:228
  42.1 1.2 %collective-permute-done.12.refs_3_ = bf16[128,1024]{1,0:T(8,128)(2,1)S(1)} collective-permute-done((bf16[128,1024]{1,0:T(8,128)(2,1)S(1)}, bf16[128,1024]{1,0:T(8,128)(2,1)S(1)}, u32[]{:S(2)}, u32[]{:S(2)}) %collective-permute-start.12) | collective-permute-done | bytes 262176 | tf_op jit(solution)/shard_map/ppermute | solution.py:22
  43.6 1.8 %collective-permute-start.17 = (bf16[128,512]{1,0:T(8,128)(2,1)S(1)}, bf16[128,512]{1,0:T(8,128)(2,1)S(1)}, u32[]{:S(2)}, u32[]{:S(2)}) collective-permute-start(bf16[128,512]{1,0:T(8,128)(2,1)S(1)} %add_convert_fusion.3.refs_0_), channel_id=1, source_target_pairs={{0,6},{1,7},{2,4},{3,5},{4,2},{5,3},{6,0},{7,1},{8,14},{9,15},{10,... | collective-permute-start | bytes 393224 | tf_op jit(solution)/shard_map/ppermute | solution.py:22
  46.2 1.0 %collective-permute-start.15 = (bf16[128,512]{1,0:T(8,128)(2,1)S(1)}, bf16[128,512]{1,0:T(8,128)(2,1)S(1)}, u32[]{:S(2)}, u32[]{:S(2)}) collective-permute-start(bf16[128,512]{1,0:T(8,128)(2,1)S(1)} %add_convert_fusion.3.refs_0_), channel_id=1, source_target_pairs={{0,2},{1,3},{2,0},{3,1},{4,6},{5,7},{6,4},{7,5},{8,10},{9,11},{10,... | collective-permute-start | bytes 393224 | tf_op jit(solution)/shard_map/ppermute | solution.py:22
  47.2 1.0 %collective-permute-start.20 = (bf16[128,512]{1,0:T(8,128)(2,1)}, bf16[128,512]{1,0:T(8,128)(2,1)S(1)}, u32[]{:S(2)}, u32[]{:S(2)}) collective-permute-start(bf16[128,512]{1,0:T(8,128)(2,1)} %get-tuple-element.109), channel_id=1, source_target_pairs={{0,2},{1,3},{2,0},{3,1},{4,6},{5,7},{6,4},{7,5},{8,10},{9,11},{10,... | collective-permute-start | bytes 393224 | tf_op jit(solution)/shard_map/ppermute | solution.py:22
  48.2 2.7 %collective-permute-done.17.refs_3_ = bf16[128,512]{1,0:T(8,128)(2,1)S(1)} collective-permute-done((bf16[128,512]{1,0:T(8,128)(2,1)S(1)}, bf16[128,512]{1,0:T(8,128)(2,1)S(1)}, u32[]{:S(2)}, u32[]{:S(2)}) %collective-permute-start.17) | collective-permute-done | bytes 131104 | tf_op jit(solution)/shard_map/ppermute | solution.py:22
  50.9 1.3 %collective-permute-start.21 = (bf16[128,512]{1,0:T(8,128)(2,1)}, bf16[128,512]{1,0:T(8,128)(2,1)S(1)}, u32[]{:S(2)}, u32[]{:S(2)}) collective-permute-start(bf16[128,512]{1,0:T(8,128)(2,1)} %get-tuple-element.110), channel_id=1, source_target_pairs={{0,4},{1,5},{2,6},{3,7},{4,0},{5,1},{6,2},{7,3},{8,12},{9,13},{10,... | collective-permute-start | bytes 393224 | tf_op jit(solution)/shard_map/ppermute | solution.py:22
  52.3 1.1 %collective-permute-done.16.refs_2_ = bf16[128,512]{1,0:T(8,128)(2,1)S(1)} collective-permute-done((bf16[128,512]{1,0:T(8,128)(2,1)S(1)}, bf16[128,512]{1,0:T(8,128)(2,1)S(1)}, u32[]{:S(2)}, u32[]{:S(2)}) %collective-permute-start.16) | collective-permute-done | bytes 131104 | tf_op jit(solution)/shard_map/ppermute | solution.py:22
  53.4 1.8 %collective-permute-start.22 = (bf16[128,512]{1,0:T(8,128)(2,1)S(1)}, bf16[128,512]{1,0:T(8,128)(2,1)S(1)}, u32[]{:S(2)}, u32[]{:S(2)}) collective-permute-start(bf16[128,512]{1,0:T(8,128)(2,1)S(1)} %get-tuple-element.111), channel_id=1, source_target_pairs={{0,6},{1,7},{2,4},{3,5},{4,2},{5,3},{6,0},{7,1},{8,14},{9,15},{10,... | collective-permute-start | bytes 393224 | tf_op jit(solution)/shard_map/ppermute | solution.py:22
  55.9 1.6 %collective-permute-start.18 = (bf16[512,256]{1,0:T(8,128)(2,1)S(1)}, bf16[512,256]{1,0:T(8,128)(2,1)S(1)}, u32[]{:S(2)}, u32[]{:S(2)}) collective-permute-start(bf16[512,256]{1,0:T(8,128)(2,1)S(1)} %get-tuple-element.106), channel_id=1, source_target_pairs={{0,8},{8,0},{16,24},{24,16},{1,9},{9,1},{17,25},{25,17},{2,10},{10... | collective-permute-start | bytes 786440 | tf_op jit(solution)/shard_map/ppermute | solution.py:22
  57.6 2.1 %collective-permute-done.22 = bf16[128,512]{1,0:T(8,128)(2,1)S(1)} collective-permute-done((bf16[128,512]{1,0:T(8,128)(2,1)S(1)}, bf16[128,512]{1,0:T(8,128)(2,1)S(1)}, u32[]{:S(2)}, u32[]{:S(2)}) %collective-permute-start.22) | collective-permute-done | bytes 131104 | tf_op jit(solution)/shard_map/ppermute | solution.py:22
  59.7 1.8 %collective-permute-start.25 = (bf16[128,512]{1,0:T(8,128)(2,1)S(1)}, bf16[128,512]{1,0:T(8,128)(2,1)S(1)}, u32[]{:S(2)}, u32[]{:S(2)}) collective-permute-start(bf16[128,512]{1,0:T(8,128)(2,1)S(1)} %add_convert_fusion.1.refs_0_), channel_id=1, source_target_pairs={{0,6},{1,7},{2,4},{3,5},{4,2},{5,3},{6,0},{7,1},{8,14},{9,15},{10,... | collective-permute-start | bytes 393224 | tf_op jit(solution)/shard_map/ppermute | solution.py:22
  62.3 1.0 %collective-permute-start.23 = (bf16[128,512]{1,0:T(8,128)(2,1)S(1)}, bf16[128,512]{1,0:T(8,128)(2,1)S(1)}, u32[]{:S(2)}, u32[]{:S(2)}) collective-permute-start(bf16[128,512]{1,0:T(8,128)(2,1)S(1)} %add_convert_fusion.1.refs_0_), channel_id=1, source_target_pairs={{0,2},{1,3},{2,0},{3,1},{4,6},{5,7},{6,4},{7,5},{8,10},{9,11},{10,... | collective-permute-start | bytes 393224 | tf_op jit(solution)/shard_map/ppermute | solution.py:22
  63.9 2.7 %collective-permute-start.19 = (bf16[256,256]{1,0:T(8,128)(2,1)S(1)}, bf16[256,256]{1,0:T(8,128)(2,1)S(1)}, u32[]{:S(2)}, u32[]{:S(2)}) collective-permute-start(bf16[256,256]{1,0:T(8,128)(2,1)S(1)} %add_convert_fusion.2), channel_id=1, source_target_pairs={{0,16},{8,24},{16,0},{24,8},{1,17},{9,25},{17,1},{25,9},{2,18},{10... | collective-permute-start | bytes 393224 | tf_op jit(solution)/shard_map/ppermute | solution.py:22
  66.9 1.1 %collective-permute-done.24.refs_2_ = bf16[128,512]{1,0:T(8,128)(2,1)S(1)} collective-permute-done((bf16[128,512]{1,0:T(8,128)(2,1)S(1)}, bf16[128,512]{1,0:T(8,128)(2,1)S(1)}, u32[]{:S(2)}, u32[]{:S(2)}) %collective-permute-start.24) | collective-permute-done | bytes 131104 | tf_op jit(solution)/shard_map/ppermute | solution.py:22
  69.4 2.4 %collective-permute-done.19.refs_2_ = bf16[256,256]{1,0:T(8,128)(2,1)S(1)} collective-permute-done((bf16[256,256]{1,0:T(8,128)(2,1)S(1)}, bf16[256,256]{1,0:T(8,128)(2,1)S(1)}, u32[]{:S(2)}, u32[]{:S(2)}) %collective-permute-start.19) | collective-permute-done | bytes 131104 | tf_op jit(solution)/shard_map/ppermute | solution.py:22
  72.4 4.7 %collective-permute-done.26 = bf16[256,256]{1,0:T(8,128)(2,1)S(1)} collective-permute-done((bf16[256,256]{1,0:T(8,128)(2,1)S(1)}, bf16[256,256]{1,0:T(8,128)(2,1)S(1)}, u32[]{:S(2)}, u32[]{:S(2)}) %collective-permute-start.26) | collective-permute-done | bytes 131104 | tf_op jit(solution)/shard_map/ppermute | solution.py:22
  77.5 3.4 %collective-permute-start.28 = (bf16[256,256]{1,0:T(8,128)(2,1)S(1)}, bf16[256,256]{1,0:T(8,128)(2,1)S(1)}, u32[]{:S(2)}, u32[]{:S(2)}) collective-permute-start(bf16[256,256]{1,0:T(8,128)(2,1)S(1)} %add_convert_fusion), channel_id=1, source_target_pairs={{0,16},{8,24},{16,0},{24,8},{1,17},{9,25},{17,1},{25,9},{2,18},{10... | collective-permute-start | bytes 393224 | tf_op jit(solution)/shard_map/ppermute | solution.py:22
  81.9 2.9 %join.1 = (bf16[1,128,4096]{2,1,0:T(8,128)(2,1)}, bf16[1,128,4096]{2,1,0:T(8,128)(2,1)}) custom-call(s32[1]{0:T(128)} %bitcast.1.scalar_ref, bf16[128,1024]{1,0:T(8,128)(2,1)} %copy-done.3, bf16[128,1024]{1,0:T(8,128)(2,1)} %copy-done.5, bf16[128,1024]{1,0:T(8,128)(2,1)} %copy-done.4, bf16[128,1024]{1,0:T(8,128)(2,1)} %copy-done.6, ...), custom_call_target="tpu_custom_call" | custom-call | bytes 4000000 | tf_op jit(solution)/shard_map/join/pallas_call | solution.py:389
  85.4 1.5 %collective-permute-done.31.got = f32[128,512]{1,0:T(8,128)S(1)} collective-permute-done((f32[128,512]{1,0:T(8,128)S(1)}, f32[128,512]{1,0:T(8,128)S(1)}, u32[]{:S(2)}, u32[]{:S(2)}) %collective-permute-start.31) | collective-permute-done | bytes 262176 | tf_op jit(solution)/shard_map/ppermute | solution.py:22
  (77 shorter events, 13.8 us)
Async XLA Ops:
  1.8 1.7 %collective-permute-start = (bf16[128,1024]{1,0:T(8,128)(2,1)S(1)}, bf16[128,1024]{1,0:T(8,128)(2,1)S(1)}, u32[]{:S(2)}, u32[]{:S(2)}) collective-permute-start(bf16[128,1024]{1,0:T(8,128)(2,1)S(1)} %bitcast.8), channel_id=1, source_target_pairs={{0,1},{1,0},{2,3},{3,2},{4,5},{5,4},{6,7},{7,6},{8,9},{9,8},{10,11... | collective-permute-start | bytes 786440 | tf_op jit(solution)/shard_map/ppermute | solution.py:22
  3.5 7.3 %collective-permute-start.2 = (bf16[1,128,4096]{2,1,0:T(8,128)(2,1)}, bf16[1,128,4096]{2,1,0:T(8,128)(2,1)S(1)}, u32[]{:S(2)}, u32[]{:S(2)}) collective-permute-start(bf16[1,128,4096]{2,1,0:T(8,128)(2,1)} %refs_0_.3), channel_id=1, source_target_pairs={{0,1},{1,0},{2,3},{3,2},{4,5},{5,4},{6,7},{7,6},{8,9},{9,8},{10,11... | collective-permute-start | bytes 3145736 | tf_op jit(solution)/shard_map/ppermute | solution.py:22
  4.0 6.9 %collective-permute-start.3 = (bf16[1,128,4096]{2,1,0:T(8,128)(2,1)}, bf16[1,128,4096]{2,1,0:T(8,128)(2,1)}, u32[]{:S(2)}, u32[]{:S(2)}) collective-permute-start(bf16[1,128,4096]{2,1,0:T(8,128)(2,1)} %refs_2_.1), channel_id=1, source_target_pairs={{0,1},{1,0},{2,3},{3,2},{4,5},{5,4},{6,7},{7,6},{8,9},{9,8},{10,11... | collective-permute-start | bytes 3145736 | tf_op jit(solution)/shard_map/ppermute | solution.py:22
  4.1 9.4 %collective-permute-start.9 = (bf16[128,512]{1,0:T(8,128)(2,1)S(1)}, bf16[128,512]{1,0:T(8,128)(2,1)S(1)}, u32[]{:S(2)}, u32[]{:S(2)}) collective-permute-start(bf16[128,512]{1,0:T(8,128)(2,1)S(1)} %get-tuple-element.77.refs_5_), channel_id=1, source_target_pairs={{0,6},{1,7},{2,4},{3,5},{4,2},{5,3},{6,0},{7,1},{8,14},{9,15},{10,... | collective-permute-start | bytes 393224 | tf_op jit(solution)/shard_map/ppermute | solution.py:22
  7.9 6.8 %collective-permute-start.8 = (bf16[128,512]{1,0:T(8,128)(2,1)S(1)}, bf16[128,512]{1,0:T(8,128)(2,1)}, u32[]{:S(2)}, u32[]{:S(2)}) collective-permute-start(bf16[128,512]{1,0:T(8,128)(2,1)S(1)} %get-tuple-element.77.refs_5_), channel_id=1, source_target_pairs={{0,4},{1,5},{2,6},{3,7},{4,0},{5,1},{6,2},{7,3},{8,12},{9,13},{10,... | collective-permute-start | bytes 393224 | tf_op jit(solution)/shard_map/ppermute | solution.py:22
  8.4 1.3 %collective-permute-start.1 = (s32[1,8]{1,0:T(1,128)}, s32[1,8]{1,0:T(1,128)S(1)}, u32[]{:S(2)}, u32[]{:S(2)}) collective-permute-start(s32[1,8]{1,0:T(1,128)} %bitcast.10), channel_id=1, source_target_pairs={{0,1},{1,0},{2,3},{3,2},{4,5},{5,4},{6,7},{7,6},{8,9},{9,8},{10,11... | collective-permute-start | bytes 104 | tf_op jit(solution)/shard_map/ppermute | solution.py:22
  9.7 6.4 %collective-permute-start.7 = (bf16[128,512]{1,0:T(8,128)(2,1)S(1)}, bf16[128,512]{1,0:T(8,128)(2,1)}, u32[]{:S(2)}, u32[]{:S(2)}) collective-permute-start(bf16[128,512]{1,0:T(8,128)(2,1)S(1)} %get-tuple-element.77.refs_5_), channel_id=1, source_target_pairs={{0,2},{1,3},{2,0},{3,1},{4,6},{5,7},{6,4},{7,5},{8,10},{9,11},{10,... | collective-permute-start | bytes 393224 | tf_op jit(solution)/shard_map/ppermute | solution.py:22
  10.9 16.1 %collective-permute-start.4 = (bf16[128,1024]{1,0:T(8,128)(2,1)S(1)}, bf16[128,1024]{1,0:T(8,128)(2,1)S(1)}, u32[]{:S(2)}, u32[]{:S(2)}) collective-permute-start(bf16[128,1024]{1,0:T(8,128)(2,1)S(1)} %get-tuple-element.86), channel_id=1, source_target_pairs={{0,2},{1,3},{2,0},{3,1},{4,6},{5,7},{6,4},{7,5},{8,10},{9,11},{10,... | collective-permute-start | bytes 786440 | tf_op jit(solution)/shard_map/ppermute | solution.py:22
  12.0 15.0 %collective-permute-start.5 = (bf16[128,1024]{1,0:T(8,128)(2,1)S(1)}, bf16[128,1024]{1,0:T(8,128)(2,1)S(1)}, u32[]{:S(2)}, u32[]{:S(2)}) collective-permute-start(bf16[128,1024]{1,0:T(8,128)(2,1)S(1)} %get-tuple-element.87), channel_id=1, source_target_pairs={{0,4},{1,5},{2,6},{3,7},{4,0},{5,1},{6,2},{7,3},{8,12},{9,13},{10,... | collective-permute-start | bytes 786440 | tf_op jit(solution)/shard_map/ppermute | solution.py:22
  13.5 14.0 %collective-permute-start.6 = (bf16[128,1024]{1,0:T(8,128)(2,1)S(1)}, bf16[128,1024]{1,0:T(8,128)(2,1)S(1)}, u32[]{:S(2)}, u32[]{:S(2)}) collective-permute-start(bf16[128,1024]{1,0:T(8,128)(2,1)S(1)} %get-tuple-element.88), channel_id=1, source_target_pairs={{0,6},{1,7},{2,4},{3,5},{4,2},{5,3},{6,0},{7,1},{8,14},{9,15},{10,... | collective-permute-start | bytes 786440 | tf_op jit(solution)/shard_map/ppermute | solution.py:22
  27.9 15.3 %collective-permute-start.13 = (bf16[512,512]{1,0:T(8,128)(2,1)S(1)}, bf16[512,512]{1,0:T(8,128)(2,1)S(1)}, u32[]{:S(2)}, u32[]{:S(2)}) collective-permute-start(bf16[512,512]{1,0:T(8,128)(2,1)S(1)} %turn.2.own_low), channel_id=1, source_target_pairs={{0,1},{1,0},{2,3},{3,2},{4,5},{5,4},{6,7},{7,6},{8,9},{9,8},{10,11... | collective-permute-start | bytes 1572872 | tf_op jit(solution)/shard_map/ppermute | solution.py:22
  27.9 13.7 %collective-permute-start.10 = (bf16[128,1024]{1,0:T(8,128)(2,1)S(1)}, bf16[128,1024]{1,0:T(8,128)(2,1)S(1)}, u32[]{:S(2)}, u32[]{:S(2)}) collective-permute-start(bf16[128,1024]{1,0:T(8,128)(2,1)S(1)} %get-tuple-element.99), channel_id=1, source_target_pairs={{0,2},{1,3},{2,0},{3,1},{4,6},{5,7},{6,4},{7,5},{8,10},{9,11},{10,... | collective-permute-start | bytes 786440 | tf_op jit(solution)/shard_map/ppermute | solution.py:22
  29.0 13.1 %collective-permute-start.11 = (bf16[128,1024]{1,0:T(8,128)(2,1)S(1)}, bf16[128,1024]{1,0:T(8,128)(2,1)S(1)}, u32[]{:S(2)}, u32[]{:S(2)}) collective-permute-start(bf16[128,1024]{1,0:T(8,128)(2,1)S(1)} %get-tuple-element.100), channel_id=1, source_target_pairs={{0,4},{1,5},{2,6},{3,7},{4,0},{5,1},{6,2},{7,3},{8,12},{9,13},{10,... | collective-permute-start | bytes 786440 | tf_op jit(solution)/shard_map/ppermute | solution.py:22
  30.5 12.7 %collective-permute-start.12 = (bf16[128,1024]{1,0:T(8,128)(2,1)S(1)}, bf16[128,1024]{1,0:T(8,128)(2,1)S(1)}, u32[]{:S(2)}, u32[]{:S(2)}) collective-permute-start(bf16[128,1024]{1,0:T(8,128)(2,1)S(1)} %get-tuple-element.101), channel_id=1, source_target_pairs={{0,6},{1,7},{2,4},{3,5},{4,2},{5,3},{6,0},{7,1},{8,14},{9,15},{10,... | collective-permute-start | bytes 786440 | tf_op jit(solution)/shard_map/ppermute | solution.py:22
  43.5 11.7 %collective-permute-start.14 = (bf16[512,512]{1,0:T(8,128)(2,1)S(1)}, bf16[512,512]{1,0:T(8,128)(2,1)S(1)}, u32[]{:S(2)}, u32[]{:S(2)}) collective-permute-start(bf16[512,512]{1,0:T(8,128)(2,1)S(1)} %turn.3.own_high), channel_id=1, source_target_pairs={{0,1},{1,0},{2,3},{3,2},{4,5},{5,4},{6,7},{7,6},{8,9},{9,8},{10,11... | collective-permute-start | bytes 1572872 | tf_op jit(solution)/shard_map/ppermute | solution.py:22
  43.6 7.3 %collective-permute-start.17 = (bf16[128,512]{1,0:T(8,128)(2,1)S(1)}, bf16[128,512]{1,0:T(8,128)(2,1)S(1)}, u32[]{:S(2)}, u32[]{:S(2)}) collective-permute-start(bf16[128,512]{1,0:T(8,128)(2,1)S(1)} %add_convert_fusion.3.refs_0_), channel_id=1, source_target_pairs={{0,6},{1,7},{2,4},{3,5},{4,2},{5,3},{6,0},{7,1},{8,14},{9,15},{10,... | collective-permute-start | bytes 393224 | tf_op jit(solution)/shard_map/ppermute | solution.py:22
  45.5 7.9 %collective-permute-start.16 = (bf16[128,512]{1,0:T(8,128)(2,1)S(1)}, bf16[128,512]{1,0:T(8,128)(2,1)S(1)}, u32[]{:S(2)}, u32[]{:S(2)}) collective-permute-start(bf16[128,512]{1,0:T(8,128)(2,1)S(1)} %add_convert_fusion.3.refs_0_), channel_id=1, source_target_pairs={{0,4},{1,5},{2,6},{3,7},{4,0},{5,1},{6,2},{7,3},{8,12},{9,13},{10,... | collective-permute-start | bytes 393224 | tf_op jit(solution)/shard_map/ppermute | solution.py:22
  46.2 9.0 %collective-permute-start.15 = (bf16[128,512]{1,0:T(8,128)(2,1)S(1)}, bf16[128,512]{1,0:T(8,128)(2,1)S(1)}, u32[]{:S(2)}, u32[]{:S(2)}) collective-permute-start(bf16[128,512]{1,0:T(8,128)(2,1)S(1)} %add_convert_fusion.3.refs_0_), channel_id=1, source_target_pairs={{0,2},{1,3},{2,0},{3,1},{4,6},{5,7},{6,4},{7,5},{8,10},{9,11},{10,... | collective-permute-start | bytes 393224 | tf_op jit(solution)/shard_map/ppermute | solution.py:22
  47.2 10.4 %collective-permute-start.20 = (bf16[128,512]{1,0:T(8,128)(2,1)}, bf16[128,512]{1,0:T(8,128)(2,1)S(1)}, u32[]{:S(2)}, u32[]{:S(2)}) collective-permute-start(bf16[128,512]{1,0:T(8,128)(2,1)} %get-tuple-element.109), channel_id=1, source_target_pairs={{0,2},{1,3},{2,0},{3,1},{4,6},{5,7},{6,4},{7,5},{8,10},{9,11},{10,... | collective-permute-start | bytes 393224 | tf_op jit(solution)/shard_map/ppermute | solution.py:22
  50.9 6.6 %collective-permute-start.21 = (bf16[128,512]{1,0:T(8,128)(2,1)}, bf16[128,512]{1,0:T(8,128)(2,1)S(1)}, u32[]{:S(2)}, u32[]{:S(2)}) collective-permute-start(bf16[128,512]{1,0:T(8,128)(2,1)} %get-tuple-element.110), channel_id=1, source_target_pairs={{0,4},{1,5},{2,6},{3,7},{4,0},{5,1},{6,2},{7,3},{8,12},{9,13},{10,... | collective-permute-start | bytes 393224 | tf_op jit(solution)/shard_map/ppermute | solution.py:22
  53.4 6.3 %collective-permute-start.22 = (bf16[128,512]{1,0:T(8,128)(2,1)S(1)}, bf16[128,512]{1,0:T(8,128)(2,1)S(1)}, u32[]{:S(2)}, u32[]{:S(2)}) collective-permute-start(bf16[128,512]{1,0:T(8,128)(2,1)S(1)} %get-tuple-element.111), channel_id=1, source_target_pairs={{0,6},{1,7},{2,4},{3,5},{4,2},{5,3},{6,0},{7,1},{8,14},{9,15},{10,... | collective-permute-start | bytes 393224 | tf_op jit(solution)/shard_map/ppermute | solution.py:22
  55.9 7.9 %collective-permute-start.18 = (bf16[512,256]{1,0:T(8,128)(2,1)S(1)}, bf16[512,256]{1,0:T(8,128)(2,1)S(1)}, u32[]{:S(2)}, u32[]{:S(2)}) collective-permute-start(bf16[512,256]{1,0:T(8,128)(2,1)S(1)} %get-tuple-element.106), channel_id=1, source_target_pairs={{0,8},{8,0},{16,24},{24,16},{1,9},{9,1},{17,25},{25,17},{2,10},{10... | collective-permute-start | bytes 786440 | tf_op jit(solution)/shard_map/ppermute | solution.py:22
  59.7 7.2 %collective-permute-start.25 = (bf16[128,512]{1,0:T(8,128)(2,1)S(1)}, bf16[128,512]{1,0:T(8,128)(2,1)S(1)}, u32[]{:S(2)}, u32[]{:S(2)}) collective-permute-start(bf16[128,512]{1,0:T(8,128)(2,1)S(1)} %add_convert_fusion.1.refs_0_), channel_id=1, source_target_pairs={{0,6},{1,7},{2,4},{3,5},{4,2},{5,3},{6,0},{7,1},{8,14},{9,15},{10,... | collective-permute-start | bytes 393224 | tf_op jit(solution)/shard_map/ppermute | solution.py:22
  61.5 6.5 %collective-permute-start.24 = (bf16[128,512]{1,0:T(8,128)(2,1)S(1)}, bf16[128,512]{1,0:T(8,128)(2,1)S(1)}, u32[]{:S(2)}, u32[]{:S(2)}) collective-permute-start(bf16[128,512]{1,0:T(8,128)(2,1)S(1)} %add_convert_fusion.1.refs_0_), channel_id=1, source_target_pairs={{0,4},{1,5},{2,6},{3,7},{4,0},{5,1},{6,2},{7,3},{8,12},{9,13},{10,... | collective-permute-start | bytes 393224 | tf_op jit(solution)/shard_map/ppermute | solution.py:22
  62.3 5.8 %collective-permute-start.23 = (bf16[128,512]{1,0:T(8,128)(2,1)S(1)}, bf16[128,512]{1,0:T(8,128)(2,1)S(1)}, u32[]{:S(2)}, u32[]{:S(2)}) collective-permute-start(bf16[128,512]{1,0:T(8,128)(2,1)S(1)} %add_convert_fusion.1.refs_0_), channel_id=1, source_target_pairs={{0,2},{1,3},{2,0},{3,1},{4,6},{5,7},{6,4},{7,5},{8,10},{9,11},{10,... | collective-permute-start | bytes 393224 | tf_op jit(solution)/shard_map/ppermute | solution.py:22
  63.9 7.9 %collective-permute-start.19 = (bf16[256,256]{1,0:T(8,128)(2,1)S(1)}, bf16[256,256]{1,0:T(8,128)(2,1)S(1)}, u32[]{:S(2)}, u32[]{:S(2)}) collective-permute-start(bf16[256,256]{1,0:T(8,128)(2,1)S(1)} %add_convert_fusion.2), channel_id=1, source_target_pairs={{0,16},{8,24},{16,0},{24,8},{1,17},{9,25},{17,1},{25,9},{2,18},{10... | collective-permute-start | bytes 393224 | tf_op jit(solution)/shard_map/ppermute | solution.py:22
  68.8 12.1 %collective-permute-start.29 = (bf16[128,2048]{1,0:T(8,128)(2,1)S(1)}, bf16[128,2048]{1,0:T(8,128)(2,1)S(1)}, u32[]{:S(2)}, u32[]{:S(2)}) collective-permute-start(bf16[128,2048]{1,0:T(8,128)(2,1)S(1)} %copy-done.9), channel_id=1, source_target_pairs={{0,1},{1,0},{2,3},{3,2},{4,5},{5,4},{6,7},{7,6},{8,9},{9,8},{10,11... | collective-permute-start | bytes 1572872 | tf_op jit(solution)/shard_map/ppermute | solution.py:22
  68.9 12.0 %collective-permute-start.30 = (bf16[128,2048]{1,0:T(8,128)(2,1)S(1)}, bf16[128,2048]{1,0:T(8,128)(2,1)S(1)}, u32[]{:S(2)}, u32[]{:S(2)}) collective-permute-start(bf16[128,2048]{1,0:T(8,128)(2,1)S(1)} %copy-done.11), channel_id=1, source_target_pairs={{0,1},{1,0},{2,3},{3,2},{4,5},{5,4},{6,7},{7,6},{8,9},{9,8},{10,11... | collective-permute-start | bytes 1572872 | tf_op jit(solution)/shard_map/ppermute | solution.py:22
  71.8 5.4 %collective-permute-start.26 = (bf16[256,256]{1,0:T(8,128)(2,1)S(1)}, bf16[256,256]{1,0:T(8,128)(2,1)S(1)}, u32[]{:S(2)}, u32[]{:S(2)}) collective-permute-start(bf16[256,256]{1,0:T(8,128)(2,1)S(1)} %get-tuple-element.120), channel_id=1, source_target_pairs={{0,8},{8,0},{16,24},{24,16},{1,9},{9,1},{17,25},{25,17},{2,10},{10... | collective-permute-start | bytes 393224 | tf_op jit(solution)/shard_map/ppermute | solution.py:22
  77.2 7.6 %collective-permute-start.27 = (bf16[256,256]{1,0:T(8,128)(2,1)S(1)}, bf16[256,256]{1,0:T(8,128)(2,1)S(1)}, u32[]{:S(2)}, u32[]{:S(2)}) collective-permute-start(bf16[256,256]{1,0:T(8,128)(2,1)S(1)} %get-tuple-element.121), channel_id=1, source_target_pairs={{0,8},{8,0},{16,24},{24,16},{1,9},{9,1},{17,25},{25,17},{2,10},{10... | collective-permute-start | bytes 393224 | tf_op jit(solution)/shard_map/ppermute | solution.py:22
  77.5 7.7 %collective-permute-start.28 = (bf16[256,256]{1,0:T(8,128)(2,1)S(1)}, bf16[256,256]{1,0:T(8,128)(2,1)S(1)}, u32[]{:S(2)}, u32[]{:S(2)}) collective-permute-start(bf16[256,256]{1,0:T(8,128)(2,1)S(1)} %add_convert_fusion), channel_id=1, source_target_pairs={{0,16},{8,24},{16,0},{24,8},{1,17},{9,25},{17,1},{25,9},{2,18},{10... | collective-permute-start | bytes 393224 | tf_op jit(solution)/shard_map/ppermute | solution.py:22
  85.3 1.6 %collective-permute-start.31 = (f32[128,512]{1,0:T(8,128)S(1)}, f32[128,512]{1,0:T(8,128)S(1)}, u32[]{:S(2)}, u32[]{:S(2)}) collective-permute-start(f32[128,512]{1,0:T(8,128)S(1)} %get-tuple-element.145), channel_id=1, source_target_pairs={{0,1},{1,0},{2,3},{3,2},{4,5},{5,4},{6,7},{7,6},{8,9},{9,8},{10,11... | collective-permute-start | bytes 786440 | tf_op jit(solution)/shard_map/ppermute | solution.py:22
  (14 other events, 46.3 us)
